TPU v7x, 32 devices: a whole 2x2x4 slice. The times are simulated.
32 devices in a mesh: groups: 2 (over y), section: 4 (over z), replica: 4 (over x, core).
Axes of the slice: x: 2, y: 2, z: 4, core: 2. Of those that a mesh axis runs over, the one named last changes fastest.
Arguments:
- section_inputs: bfloat16 [8, 4, 2, 16, 16, 256], P(('groups', 'replica'), 'section'), parts along dimension 0, may hold values from -6 to 6
- cotangent: bfloat16 [8, 2, 16, 16, 256], P(('groups', 'replica')), parts along dimension 0, may hold values from -6 to 6
- crop_rows: int32 [8, 2], P(('groups', 'replica')), parts along dimension 0, may hold values from 0 to 705
- drift: bfloat16 [8, 4, 9, 256, 256], P(('groups', 'replica'), 'section'), parts along dimension 0, may hold values from -6 to 6
- params: float32 [8, 9, 256, 256], P(('groups', 'section')), parts along dimension 0, may hold values from -6 to 6
- momentum: float32 [8, 9, 256, 256], P(('groups', 'section'), None, 'replica'), parts along dimension 0, may hold values from -4 to 4
Outputs:
- new_params: float32 [8, 9, 256, 256], P(('groups', 'section')), parts along dimension 0
- new_momentum: float32 [8, 9, 256, 256], P(('groups', 'section'), None, 'replica'), parts along dimension 0
There are 2 independent parts, one for each index of `groups`. A program takes and returns all parts, laid end to end along the dimension named above; each array names one. Nothing has to cross between parts.
All inputs are finite; a program needn't handle non-finite values.
Results may differ from a plain program's by a relative error of at most 0.0075.
Values may be sent and summed in bfloat16 or wider, within the bound.
No kernel may reach another device: no remote copies, remote signals or barrier semaphores. Data moves between devices by JAX's collectives and lax.ppermute only.
A program may use at most 64 MiB of HBM per device.

v0:
```python
import math

import jax
import jax.numpy as jnp
from jax import lax
from jax.sharding import PartitionSpec as P

LATS = 721


def from_behind(x, axis, by):
    devices = lax.axis_size(axis)
    pairs = [(i, i + by) for i in range(devices) if 0 <= i + by < devices]
    return lax.ppermute(x, axis, pairs)


def lat_weight(first_row, count):
    rows = jnp.arange(count, dtype=jnp.float32) + first_row.astype(jnp.float32)
    middle = (LATS - 1) / 2.0
    every = jnp.arange(LATS, dtype=jnp.float32)
    norm_value = jnp.mean(jnp.cos(math.pi * (every - middle) / (LATS - 1)))
    return jnp.cos(math.pi * (rows - middle) / (LATS - 1)) / norm_value


def backward(inputs, out_grad, weights):
    rows, cols, width = inputs.shape
    scale = (9.0 * width) ** (-0.5)
    padded = jnp.pad(inputs, ((1, 1), (1, 1), (0, 0)))
    taps = jnp.stack([padded[a : a + rows, b : b + cols] for a in range(3) for b in range(3)])
    pre = jnp.einsum("krcd,kde->rce", taps, weights, preferred_element_type=jnp.float32) * scale
    tangent = jnp.tanh(pre)
    local = (out_grad.astype(jnp.float32) * (1.0 - tangent * tangent)).astype(jnp.bfloat16)
    grad = jnp.einsum("krcd,rce->kde", taps, local, preferred_element_type=jnp.float32) * scale
    back = jnp.einsum("rce,kde->krcd", local, weights, preferred_element_type=jnp.float32)
    accum = jnp.zeros((rows + 2, cols + 2, width), jnp.float32)
    for a in range(3):
        for b in range(3):
            accum = accum.at[a : a + rows, b : b + cols].add(back[3 * a + b])
    in_grad = (out_grad.astype(jnp.float32) + scale * accum[1 : rows + 1, 1 : cols + 1]).astype(
        jnp.bfloat16
    )
    return (grad, in_grad)


def per_device(section_inputs, cotangent, crop_rows, drift, params, momentum):
    section = lax.axis_index("section")
    sections = lax.axis_size("section")
    inputs_here = section_inputs[0, 0]
    cot_here = cotangent[0]
    crops_here = crop_rows[0]
    micro = inputs_here.shape[0]
    rows, cols, width = inputs_here.shape[1:]
    weights_bf = params[0].astype(jnp.bfloat16)

    def tick(step, carry):
        incoming, grad_total = carry
        micro_index = step - (sections - 1 - section)
        valid = jnp.logical_and(micro_index >= 0, micro_index < micro)
        chosen = jnp.clip(micro_index, 0, micro - 1)
        inputs_now = lax.dynamic_index_in_dim(inputs_here, chosen, 0, keepdims=False)
        cot_now = lax.dynamic_index_in_dim(cot_here, chosen, 0, keepdims=False)
        first_row = lax.dynamic_index_in_dim(crops_here, chosen, 0, keepdims=False)
        top_grad = (
            cot_now.astype(jnp.float32) * lat_weight(first_row, rows)[:, None, None]
        ).astype(jnp.bfloat16)
        out_grad = jnp.where(section == sections - 1, top_grad, incoming)
        contrib, in_grad = backward(inputs_now, out_grad, weights_bf)
        grad_total = grad_total + jnp.where(valid, contrib, jnp.zeros_like(contrib))
        passed = from_behind(in_grad, "section", -1)
        return (passed, grad_total)

    start = (
        jnp.zeros((rows, cols, width), jnp.bfloat16),
        jnp.zeros((9, width, width), jnp.float32),
    )
    unused, grad_total = lax.fori_loop(0, sections + micro - 1, tick, start)
    delta_bf = (drift[0, 0].astype(jnp.float32) + 0.5 * grad_total).astype(jnp.bfloat16)
    delta_bf = lax.optimization_barrier(delta_bf)
    delta = delta_bf.astype(jnp.float32)
    replicas = lax.axis_size("replica")
    here = lax.axis_index("replica")
    share_rows = width // replicas
    mean_delta = lax.psum(delta.astype(jnp.bfloat16), "replica").astype(jnp.float32) / replicas
    mom_whole = lax.all_gather(momentum[0], "replica", axis=1, tiled=True)
    mom_next = 0.9 * mom_whole + mean_delta
    new_params = params[0] - 0.7 * (mean_delta + 0.9 * mom_next)
    new_momentum = lax.dynamic_slice_in_dim(mom_next, here * share_rows, share_rows, 1)
    return (new_params[None], new_momentum[None])


def solution(mesh):
    placed = (
        P(("groups", "replica"), "section", None, None, None, None),
        P(("groups", "replica"), None, None, None, None),
        P(("groups", "replica"), None),
        P(("groups", "replica"), "section", None, None, None),
        P(("groups", "section"), None, None, None),
        P(("groups", "section"), None, "replica", None),
    )
    return jax.shard_map(
        per_device,
        mesh=mesh,
        in_specs=placed,
        out_specs=(
            P(("groups", "section"), None, None, None),
            P(("groups", "section"), None, "replica", None),
        ),
        check_vma=False,
    )
```

profile of v0, /device:TPU:27, one launch (start us, length us, event | category | flops | bytes accessed | tf_op | source)
XLA Modules:
  0.0 205.7 jit_solution(15496415123760340458)
XLA Ops:
  7.3 1.8 bitcast_convert_fusion
  9.1 114.8 %while.28 = (s32[]{:T(128)}, bf16[16,16,256]{2,1,0:T(8,128)(2,1)S(1)}, f32[9,256,256]{2,1,0:T(8,128)}, pred[]{:T(512)}, s32[]{:T(128)}, /*index=5*/bf16[2,16,16,...) while((s32[]{:T(128)}, ...), condition=%wide.region_3.4_spmd.clone, body=%wide.region_0.3_spmd.clone.sunk | while | flops 910100672 | bytes 44110644 | solution.py:76
  12.6 1.4 fusion.102
  15.9 1.3 fusion.104
  17.2 1.6 scatter-add.71
  19.5 1.9 add_select_fusion.2
  21.4 1.6 scatter-add.72
  24.7 1.0 fusion.112
  25.8 2.1 %collective-permute-start = (bf16[16,16,256]{2,1,0:T(8,128)(2,1)S(1)}, bf16[16,16,256]{2,1,0:T(8,128)(2,1)S(1)}, u32[]{:S(2)}, u32[]{:S(2)}) collective-permute-start(bf16[16,16,256]{2,1,0:T(8,128)(2,1)S(1)} %fusion.112), channel_id=1, source_target_pairs={{4,0},{8,4},{12,8},{5,1},{9,5},{13,9},{6,2},{10,6},{14,10},{7,3},{... | collective-permute-start | bytes 393224 | tf_op jit(solution)/shard_map/while/body/eval_jaxpr/ppermute | solution.py:14
  28.0 3.4 %fusion.113 = f32[9,256,256]{2,1,0:T(8,128)} fusion(f32[9,256,256]{2,1,0:T(8,128)} %get-tuple-element.608, bf16[9,16,16,256]{3,2,0,1:T(8,128)(2,1)} %copy-done.7, pred[]{:T(512)S(6)} %compare.180, pred[]{:T(512)S(6)} %and.113, bf16[16,16,256]{2,1,0:T(8,128)(2,1)} %copy-done.6), kind=kOutput, calls=%fused_computation.2.clone.1 | convolution fusion | flops 304349184 | bytes 6029314 | tf_op jit(solution)/shard_map/while/body/eval_jaxpr/krcd,rce->kde/dot_general | solution.py:33
  31.4 0.9 cosine_reduce_fusion.2
  34.8 1.4 fusion.102
  38.1 1.3 fusion.104
  39.4 1.6 scatter-add.71
  41.8 1.9 add_select_fusion.2
  43.7 1.6 scatter-add.72
  47.0 1.0 fusion.112
  48.0 2.8 %collective-permute-start = (bf16[16,16,256]{2,1,0:T(8,128)(2,1)S(1)}, bf16[16,16,256]{2,1,0:T(8,128)(2,1)S(1)}, u32[]{:S(2)}, u32[]{:S(2)}) collective-permute-start(bf16[16,16,256]{2,1,0:T(8,128)(2,1)S(1)} %fusion.112), channel_id=1, source_target_pairs={{4,0},{8,4},{12,8},{5,1},{9,5},{13,9},{6,2},{10,6},{14,10},{7,3},{... | collective-permute-start | bytes 393224 | tf_op jit(solution)/shard_map/while/body/eval_jaxpr/ppermute | solution.py:14
  50.9 4.2 %fusion.113 = f32[9,256,256]{2,1,0:T(8,128)} fusion(f32[9,256,256]{2,1,0:T(8,128)} %get-tuple-element.608, bf16[9,16,16,256]{3,2,0,1:T(8,128)(2,1)} %copy-done.7, pred[]{:T(512)S(6)} %compare.180, pred[]{:T(512)S(6)} %and.113, bf16[16,16,256]{2,1,0:T(8,128)(2,1)} %copy-done.6), kind=kOutput, calls=%fused_computation.2.clone.1 | convolution fusion | flops 304349184 | bytes 6029314 | tf_op jit(solution)/shard_map/while/body/eval_jaxpr/krcd,rce->kde/dot_general | solution.py:33
  58.5 1.4 fusion.102
  61.8 1.3 fusion.104
  63.1 1.6 scatter-add.71
  65.5 1.9 add_select_fusion.2
  67.4 1.6 scatter-add.72
  70.7 1.0 fusion.112
  71.7 2.1 %collective-permute-start = (bf16[16,16,256]{2,1,0:T(8,128)(2,1)S(1)}, bf16[16,16,256]{2,1,0:T(8,128)(2,1)S(1)}, u32[]{:S(2)}, u32[]{:S(2)}) collective-permute-start(bf16[16,16,256]{2,1,0:T(8,128)(2,1)S(1)} %fusion.112), channel_id=1, source_target_pairs={{4,0},{8,4},{12,8},{5,1},{9,5},{13,9},{6,2},{10,6},{14,10},{7,3},{... | collective-permute-start | bytes 393224 | tf_op jit(solution)/shard_map/while/body/eval_jaxpr/ppermute | solution.py:14
  73.9 4.2 %fusion.113 = f32[9,256,256]{2,1,0:T(8,128)} fusion(f32[9,256,256]{2,1,0:T(8,128)} %get-tuple-element.608, bf16[9,16,16,256]{3,2,0,1:T(8,128)(2,1)} %copy-done.7, pred[]{:T(512)S(6)} %compare.180, pred[]{:T(512)S(6)} %and.113, bf16[16,16,256]{2,1,0:T(8,128)(2,1)} %copy-done.6), kind=kOutput, calls=%fused_computation.2.clone.1 | convolution fusion | flops 304349184 | bytes 6029314 | tf_op jit(solution)/shard_map/while/body/eval_jaxpr/krcd,rce->kde/dot_general | solution.py:33
  78.2 0.9 cosine_reduce_fusion.2
  81.5 1.4 fusion.102
  84.8 1.3 fusion.104
  86.1 1.6 scatter-add.71
  88.5 1.9 add_select_fusion.2
  90.4 1.6 scatter-add.72
  93.7 1.0 fusion.112
  94.8 2.1 %collective-permute-start = (bf16[16,16,256]{2,1,0:T(8,128)(2,1)S(1)}, bf16[16,16,256]{2,1,0:T(8,128)(2,1)S(1)}, u32[]{:S(2)}, u32[]{:S(2)}) collective-permute-start(bf16[16,16,256]{2,1,0:T(8,128)(2,1)S(1)} %fusion.112), channel_id=1, source_target_pairs={{4,0},{8,4},{12,8},{5,1},{9,5},{13,9},{6,2},{10,6},{14,10},{7,3},{... | collective-permute-start | bytes 393224 | tf_op jit(solution)/shard_map/while/body/eval_jaxpr/ppermute | solution.py:14
  96.9 4.2 %fusion.113 = f32[9,256,256]{2,1,0:T(8,128)} fusion(f32[9,256,256]{2,1,0:T(8,128)} %get-tuple-element.608, bf16[9,16,16,256]{3,2,0,1:T(8,128)(2,1)} %copy-done.7, pred[]{:T(512)S(6)} %compare.180, pred[]{:T(512)S(6)} %and.113, bf16[16,16,256]{2,1,0:T(8,128)(2,1)} %copy-done.6), kind=kOutput, calls=%fused_computation.2.clone.1 | convolution fusion | flops 304349184 | bytes 6029314 | tf_op jit(solution)/shard_map/while/body/eval_jaxpr/krcd,rce->kde/dot_general | solution.py:33
  104.5 1.4 fusion.102
  107.8 1.3 fusion.104
  109.2 1.6 scatter-add.71
  111.5 1.9 add_select_fusion.2
  113.4 1.6 scatter-add.72
  116.7 1.0 fusion.112
  117.8 2.0 collective-permute-start
  119.8 4.2 %fusion.113 = f32[9,256,256]{2,1,0:T(8,128)} fusion(f32[9,256,256]{2,1,0:T(8,128)} %get-tuple-element.608, bf16[9,16,16,256]{3,2,0,1:T(8,128)(2,1)} %copy-done.7, pred[]{:T(512)S(6)} %compare.180, pred[]{:T(512)S(6)} %and.113, bf16[16,16,256]{2,1,0:T(8,128)(2,1)} %copy-done.6), kind=kOutput, calls=%fused_computation.2.clone.1 | convolution fusion | flops 304349184 | bytes 6029314 | tf_op jit(solution)/shard_map/while/body/eval_jaxpr/krcd,rce->kde/dot_general | solution.py:33
  124.0 3.5 %fusion.56 = bf16[9,256,256]{2,1,0:T(8,128)(2,1)} fusion(f32[9,256,256]{2,1,0:T(8,128)} %get-tuple-element.472, bf16[1,1,9,256,256]{4,3,2,1,0:T(8,128)(2,1)} %param.29), kind=kLoop, calls=%fused_computation.72 | loop fusion | flops 2359296 | bytes 4718592 | tf_op jit(solution)/shard_map/convert_element_type | solution.py:77
  128.2 39.8 %all-reduce.4.cloned.1.call-done = bf16[9,256,256]{2,1,0:T(8,128)(2,1)} async-done(((bf16[9,256,256]{2,1,0:T(8,128)(2,1)}), bf16[9,256,256]{2,1,0:T(8,128)(2,1)}) %all-reduce.4.cloned.1.call-update) | async-done | bytes 1179664 | tf_op jit(solution)/shard_map/psum | solution.py:83
  168.1 26.0 %all-gather.3.cloned.1.call-done = f32[1,9,256,256]{3,2,1,0:T(8,128)} async-done(((f32[1,9,64,256]{3,2,1,0:T(8,128)}), f32[1,9,256,256]{3,2,1,0:T(8,128)}) %all-gather.3.cloned.1.call-update) | async-done | bytes 2359312 | tf_op jit(solution)/shard_map/all_gather | solution.py:84
  194.0 4.0 %bitcast_add_fusion = (f32[9,256,256]{2,1,0:T(8,128)S(1)}, f32[1,9,256,256]{3,2,1,0:T(8,128)}) fusion(f32[1,9,256,256]{3,2,1,0:T(8,128)} %all-gather.3.cloned.1.call-done, bf16[9,256,256]{2,1,0:T(8,128)(2,1)} %all-reduce.4.cloned.1.call-done, f32[1,9,256,256]{3,2,1,0:T(8,128)S(1)} %copy-done.4), kind=kLoop, calls=%fused_computation.73 | loop fusion | flops 4718592 | bytes 10616832 | tf_op jit(solution)/shard_map/add | solution.py:85
  (244 shorter events, 31.1 us)
Async XLA Ops:
  7.2 2.0 copy-start.9
  7.2 1.9 copy-start.8
  7.2 2.0 copy-start.10
  7.2 160.9 %all-reduce.4.cloned.1.call-start = ((), (), s32[]{:S(2)}) async-start(), calls=%async_computation | async-start | bytes 2359296 | tf_op jit(solution)/shard_map/psum | solution.py:83
  9.2 3.4 %copy-start.2 = (bf16[2,16,16,256]{3,2,0,1:T(8,128)(2,1)}, bf16[2,16,16,256]{3,2,0,1:T(8,128)(2,1)S(1)}, u32[]{:S(2)}) copy-start(bf16[2,16,16,256]{3,2,0,1:T(8,128)(2,1)S(1)} %get-tuple-element.629) | copy-start | bytes 786436 | tf_op jit(solution)/shard_map/while
  9.2 3.4 %copy-start.5 = (bf16[16,16,256]{2,1,0:T(8,128)(2,1)}, bf16[16,16,256]{2,1,0:T(8,128)(2,1)S(1)}, u32[]{:S(2)}) copy-start(bf16[16,16,256]{2,1,0:T(8,128)(2,1)S(1)} %get-tuple-element.607) | copy-start | bytes 393220 | tf_op jit(solution)/shard_map/while
  9.2 4.8 %copy-start = (bf16[9,256,256]{2,1,0:T(8,128)(2,1)}, bf16[9,256,256]{2,1,0:T(8,128)(2,1)S(1)}, u32[]{:S(2)}) copy-start(bf16[9,256,256]{2,1,0:T(8,128)(2,1)S(1)} %get-tuple-element.630) | copy-start | bytes 3538948 | tf_op jit(solution)/shard_map/while
  10.4 2.1 %copy-start.7 = (bf16[9,16,16,256]{3,2,0,1:T(8,128)(2,1)}, bf16[9,16,16,256]{3,2,0,1:T(8,128)(2,1)S(1)}, u32[]{:S(2)}) copy-start(bf16[9,16,16,256]{3,2,0,1:T(8,128)(2,1)S(1)} %fusion.101) | copy-start | bytes 3538948 | tf_op jit(solution)/shard_map/while
  14.0 1.9 copy-start.6
  25.8 5.6 %collective-permute-start = (bf16[16,16,256]{2,1,0:T(8,128)(2,1)S(1)}, bf16[16,16,256]{2,1,0:T(8,128)(2,1)S(1)}, u32[]{:S(2)}, u32[]{:S(2)}) collective-permute-start(bf16[16,16,256]{2,1,0:T(8,128)(2,1)S(1)} %fusion.112), channel_id=1, source_target_pairs={{4,0},{8,4},{12,8},{5,1},{9,5},{13,9},{6,2},{10,6},{14,10},{7,3},{... | collective-permute-start | bytes 393224 | tf_op jit(solution)/shard_map/while/body/eval_jaxpr/ppermute | solution.py:14
  27.9 3.4 %copy-start.1 = (bf16[9,256,256]{2,1,0:T(8,128)(2,1)S(1)}, bf16[9,256,256]{2,1,0:T(8,128)(2,1)}, u32[]{:S(2)}) copy-start(bf16[9,256,256]{2,1,0:T(8,128)(2,1)} %copy-done) | copy-start | bytes 3538948 | tf_op jit(solution)/shard_map/while
  28.0 3.4 %copy-start.3 = (bf16[2,16,16,256]{3,2,0,1:T(8,128)(2,1)S(1)}, bf16[2,16,16,256]{3,2,0,1:T(8,128)(2,1)}, u32[]{:S(2)}) copy-start(bf16[2,16,16,256]{3,2,0,1:T(8,128)(2,1)} %copy-done.2) | copy-start | bytes 786436 | tf_op jit(solution)/shard_map/while
  31.4 3.4 %copy-start.2 = (bf16[2,16,16,256]{3,2,0,1:T(8,128)(2,1)}, bf16[2,16,16,256]{3,2,0,1:T(8,128)(2,1)S(1)}, u32[]{:S(2)}) copy-start(bf16[2,16,16,256]{3,2,0,1:T(8,128)(2,1)S(1)} %get-tuple-element.629) | copy-start | bytes 786436 | tf_op jit(solution)/shard_map/while
  31.4 3.4 %copy-start.5 = (bf16[16,16,256]{2,1,0:T(8,128)(2,1)}, bf16[16,16,256]{2,1,0:T(8,128)(2,1)S(1)}, u32[]{:S(2)}) copy-start(bf16[16,16,256]{2,1,0:T(8,128)(2,1)S(1)} %get-tuple-element.607) | copy-start | bytes 393220 | tf_op jit(solution)/shard_map/while
  31.4 4.8 %copy-start = (bf16[9,256,256]{2,1,0:T(8,128)(2,1)}, bf16[9,256,256]{2,1,0:T(8,128)(2,1)S(1)}, u32[]{:S(2)}) copy-start(bf16[9,256,256]{2,1,0:T(8,128)(2,1)S(1)} %get-tuple-element.630) | copy-start | bytes 3538948 | tf_op jit(solution)/shard_map/while
  32.7 2.1 %copy-start.7 = (bf16[9,16,16,256]{3,2,0,1:T(8,128)(2,1)}, bf16[9,16,16,256]{3,2,0,1:T(8,128)(2,1)S(1)}, u32[]{:S(2)}) copy-start(bf16[9,16,16,256]{3,2,0,1:T(8,128)(2,1)S(1)} %fusion.101) | copy-start | bytes 3538948 | tf_op jit(solution)/shard_map/while
  36.2 1.9 copy-start.6
  48.0 7.1 %collective-permute-start = (bf16[16,16,256]{2,1,0:T(8,128)(2,1)S(1)}, bf16[16,16,256]{2,1,0:T(8,128)(2,1)S(1)}, u32[]{:S(2)}, u32[]{:S(2)}) collective-permute-start(bf16[16,16,256]{2,1,0:T(8,128)(2,1)S(1)} %fusion.112), channel_id=1, source_target_pairs={{4,0},{8,4},{12,8},{5,1},{9,5},{13,9},{6,2},{10,6},{14,10},{7,3},{... | collective-permute-start | bytes 393224 | tf_op jit(solution)/shard_map/while/body/eval_jaxpr/ppermute | solution.py:14
  50.9 4.2 %copy-start.1 = (bf16[9,256,256]{2,1,0:T(8,128)(2,1)S(1)}, bf16[9,256,256]{2,1,0:T(8,128)(2,1)}, u32[]{:S(2)}) copy-start(bf16[9,256,256]{2,1,0:T(8,128)(2,1)} %copy-done) | copy-start | bytes 3538948 | tf_op jit(solution)/shard_map/while
  50.9 4.2 %copy-start.3 = (bf16[2,16,16,256]{3,2,0,1:T(8,128)(2,1)S(1)}, bf16[2,16,16,256]{3,2,0,1:T(8,128)(2,1)}, u32[]{:S(2)}) copy-start(bf16[2,16,16,256]{3,2,0,1:T(8,128)(2,1)} %copy-done.2) | copy-start | bytes 786436 | tf_op jit(solution)/shard_map/while
  55.1 3.4 %copy-start.2 = (bf16[2,16,16,256]{3,2,0,1:T(8,128)(2,1)}, bf16[2,16,16,256]{3,2,0,1:T(8,128)(2,1)S(1)}, u32[]{:S(2)}) copy-start(bf16[2,16,16,256]{3,2,0,1:T(8,128)(2,1)S(1)} %get-tuple-element.629) | copy-start | bytes 786436 | tf_op jit(solution)/shard_map/while
  55.1 3.4 %copy-start.5 = (bf16[16,16,256]{2,1,0:T(8,128)(2,1)}, bf16[16,16,256]{2,1,0:T(8,128)(2,1)S(1)}, u32[]{:S(2)}) copy-start(bf16[16,16,256]{2,1,0:T(8,128)(2,1)S(1)} %get-tuple-element.607) | copy-start | bytes 393220 | tf_op jit(solution)/shard_map/while
  55.1 4.8 %copy-start = (bf16[9,256,256]{2,1,0:T(8,128)(2,1)}, bf16[9,256,256]{2,1,0:T(8,128)(2,1)S(1)}, u32[]{:S(2)}) copy-start(bf16[9,256,256]{2,1,0:T(8,128)(2,1)S(1)} %get-tuple-element.630) | copy-start | bytes 3538948 | tf_op jit(solution)/shard_map/while
  56.4 2.1 %copy-start.7 = (bf16[9,16,16,256]{3,2,0,1:T(8,128)(2,1)}, bf16[9,16,16,256]{3,2,0,1:T(8,128)(2,1)S(1)}, u32[]{:S(2)}) copy-start(bf16[9,16,16,256]{3,2,0,1:T(8,128)(2,1)S(1)} %fusion.101) | copy-start | bytes 3538948 | tf_op jit(solution)/shard_map/while
  59.9 1.9 copy-start.6
  71.7 6.4 %collective-permute-start = (bf16[16,16,256]{2,1,0:T(8,128)(2,1)S(1)}, bf16[16,16,256]{2,1,0:T(8,128)(2,1)S(1)}, u32[]{:S(2)}, u32[]{:S(2)}) collective-permute-start(bf16[16,16,256]{2,1,0:T(8,128)(2,1)S(1)} %fusion.112), channel_id=1, source_target_pairs={{4,0},{8,4},{12,8},{5,1},{9,5},{13,9},{6,2},{10,6},{14,10},{7,3},{... | collective-permute-start | bytes 393224 | tf_op jit(solution)/shard_map/while/body/eval_jaxpr/ppermute | solution.py:14
  73.9 4.2 %copy-start.1 = (bf16[9,256,256]{2,1,0:T(8,128)(2,1)S(1)}, bf16[9,256,256]{2,1,0:T(8,128)(2,1)}, u32[]{:S(2)}) copy-start(bf16[9,256,256]{2,1,0:T(8,128)(2,1)} %copy-done) | copy-start | bytes 3538948 | tf_op jit(solution)/shard_map/while
  73.9 4.2 %copy-start.3 = (bf16[2,16,16,256]{3,2,0,1:T(8,128)(2,1)S(1)}, bf16[2,16,16,256]{3,2,0,1:T(8,128)(2,1)}, u32[]{:S(2)}) copy-start(bf16[2,16,16,256]{3,2,0,1:T(8,128)(2,1)} %copy-done.2) | copy-start | bytes 786436 | tf_op jit(solution)/shard_map/while
  78.1 3.4 %copy-start.2 = (bf16[2,16,16,256]{3,2,0,1:T(8,128)(2,1)}, bf16[2,16,16,256]{3,2,0,1:T(8,128)(2,1)S(1)}, u32[]{:S(2)}) copy-start(bf16[2,16,16,256]{3,2,0,1:T(8,128)(2,1)S(1)} %get-tuple-element.629) | copy-start | bytes 786436 | tf_op jit(solution)/shard_map/while
  78.1 3.4 %copy-start.5 = (bf16[16,16,256]{2,1,0:T(8,128)(2,1)}, bf16[16,16,256]{2,1,0:T(8,128)(2,1)S(1)}, u32[]{:S(2)}) copy-start(bf16[16,16,256]{2,1,0:T(8,128)(2,1)S(1)} %get-tuple-element.607) | copy-start | bytes 393220 | tf_op jit(solution)/shard_map/while
  78.2 4.8 %copy-start = (bf16[9,256,256]{2,1,0:T(8,128)(2,1)}, bf16[9,256,256]{2,1,0:T(8,128)(2,1)S(1)}, u32[]{:S(2)}) copy-start(bf16[9,256,256]{2,1,0:T(8,128)(2,1)S(1)} %get-tuple-element.630) | copy-start | bytes 3538948 | tf_op jit(solution)/shard_map/while
  79.4 2.1 %copy-start.7 = (bf16[9,16,16,256]{3,2,0,1:T(8,128)(2,1)}, bf16[9,16,16,256]{3,2,0,1:T(8,128)(2,1)S(1)}, u32[]{:S(2)}) copy-start(bf16[9,16,16,256]{3,2,0,1:T(8,128)(2,1)S(1)} %fusion.101) | copy-start | bytes 3538948 | tf_op jit(solution)/shard_map/while
  83.0 1.9 copy-start.6
  94.8 6.4 %collective-permute-start = (bf16[16,16,256]{2,1,0:T(8,128)(2,1)S(1)}, bf16[16,16,256]{2,1,0:T(8,128)(2,1)S(1)}, u32[]{:S(2)}, u32[]{:S(2)}) collective-permute-start(bf16[16,16,256]{2,1,0:T(8,128)(2,1)S(1)} %fusion.112), channel_id=1, source_target_pairs={{4,0},{8,4},{12,8},{5,1},{9,5},{13,9},{6,2},{10,6},{14,10},{7,3},{... | collective-permute-start | bytes 393224 | tf_op jit(solution)/shard_map/while/body/eval_jaxpr/ppermute | solution.py:14
  96.9 4.2 %copy-start.1 = (bf16[9,256,256]{2,1,0:T(8,128)(2,1)S(1)}, bf16[9,256,256]{2,1,0:T(8,128)(2,1)}, u32[]{:S(2)}) copy-start(bf16[9,256,256]{2,1,0:T(8,128)(2,1)} %copy-done) | copy-start | bytes 3538948 | tf_op jit(solution)/shard_map/while
  96.9 4.2 %copy-start.3 = (bf16[2,16,16,256]{3,2,0,1:T(8,128)(2,1)S(1)}, bf16[2,16,16,256]{3,2,0,1:T(8,128)(2,1)}, u32[]{:S(2)}) copy-start(bf16[2,16,16,256]{3,2,0,1:T(8,128)(2,1)} %copy-done.2) | copy-start | bytes 786436 | tf_op jit(solution)/shard_map/while
  101.1 3.4 %copy-start.2 = (bf16[2,16,16,256]{3,2,0,1:T(8,128)(2,1)}, bf16[2,16,16,256]{3,2,0,1:T(8,128)(2,1)S(1)}, u32[]{:S(2)}) copy-start(bf16[2,16,16,256]{3,2,0,1:T(8,128)(2,1)S(1)} %get-tuple-element.629) | copy-start | bytes 786436 | tf_op jit(solution)/shard_map/while
  101.1 3.4 %copy-start.5 = (bf16[16,16,256]{2,1,0:T(8,128)(2,1)}, bf16[16,16,256]{2,1,0:T(8,128)(2,1)S(1)}, u32[]{:S(2)}) copy-start(bf16[16,16,256]{2,1,0:T(8,128)(2,1)S(1)} %get-tuple-element.607) | copy-start | bytes 393220 | tf_op jit(solution)/shard_map/while
  101.2 4.8 %copy-start = (bf16[9,256,256]{2,1,0:T(8,128)(2,1)}, bf16[9,256,256]{2,1,0:T(8,128)(2,1)S(1)}, u32[]{:S(2)}) copy-start(bf16[9,256,256]{2,1,0:T(8,128)(2,1)S(1)} %get-tuple-element.630) | copy-start | bytes 3538948 | tf_op jit(solution)/shard_map/while
  102.4 2.1 %copy-start.7 = (bf16[9,16,16,256]{3,2,0,1:T(8,128)(2,1)}, bf16[9,16,16,256]{3,2,0,1:T(8,128)(2,1)S(1)}, u32[]{:S(2)}) copy-start(bf16[9,16,16,256]{3,2,0,1:T(8,128)(2,1)S(1)} %fusion.101) | copy-start | bytes 3538948 | tf_op jit(solution)/shard_map/while
  106.0 1.9 copy-start.6
  117.8 6.2 %collective-permute-start = (bf16[16,16,256]{2,1,0:T(8,128)(2,1)S(1)}, bf16[16,16,256]{2,1,0:T(8,128)(2,1)S(1)}, u32[]{:S(2)}, u32[]{:S(2)}) collective-permute-start(bf16[16,16,256]{2,1,0:T(8,128)(2,1)S(1)} %fusion.112), channel_id=1, source_target_pairs={{4,0},{8,4},{12,8},{5,1},{9,5},{13,9},{6,2},{10,6},{14,10},{7,3},{... | collective-permute-start | bytes 393224 | tf_op jit(solution)/shard_map/while/body/eval_jaxpr/ppermute | solution.py:14
  119.8 4.2 %copy-start.1 = (bf16[9,256,256]{2,1,0:T(8,128)(2,1)S(1)}, bf16[9,256,256]{2,1,0:T(8,128)(2,1)}, u32[]{:S(2)}) copy-start(bf16[9,256,256]{2,1,0:T(8,128)(2,1)} %copy-done) | copy-start | bytes 3538948 | tf_op jit(solution)/shard_map/while
  119.8 4.2 %copy-start.3 = (bf16[2,16,16,256]{3,2,0,1:T(8,128)(2,1)S(1)}, bf16[2,16,16,256]{3,2,0,1:T(8,128)(2,1)}, u32[]{:S(2)}) copy-start(bf16[2,16,16,256]{3,2,0,1:T(8,128)(2,1)} %copy-done.2) | copy-start | bytes 786436 | tf_op jit(solution)/shard_map/while
  124.0 70.0 %copy-start.4 = (f32[1,9,256,256]{3,2,1,0:T(8,128)S(1)}, f32[1,9,256,256]{3,2,1,0:T(8,128)}, u32[]{:S(2)}) copy-start(f32[1,9,256,256]{3,2,1,0:T(8,128)} %param.30) | copy-start | bytes 7077892
  127.5 66.5 %all-gather.3.cloned.1.call-start = ((), (), s32[]{:S(2)}) async-start(), calls=%async_computation.1 | async-start | bytes 2949120 | tf_op jit(solution)/shard_map/all_gather | solution.py:84
Sparse Core Ops, SparseCore 0:
  127.6 40.4 all-reduce.3
  169.6 24.3 all-gather.2
where the time goes:
time: 209 us; the launch traced here: 206 us
  waiting for transfers between devices  66.5 us (32%)
  other arithmetic  40.5 us (19%)
  local copies, waits for them, and re-layouts  35.3 us (17%)
  matrix products  29.7 us (14%)
  between operations  14.1 us (7%)
  starting transfers between devices  11.3 us (5%)
  loops' own time  8.29 us (4%)
    psum x1, waiting for transfers between devices, per_device(): lax.psum(delta.astype(jnp.bfloat16), 'replica').astype(jnp.float32)  39.8 us
    all_gather x1, waiting for transfers between devices, per_device(): mom_whole = lax.all_gather(momentum[0], 'replica', axis=1, tiled=True)  26 us
    scatter-add x35, local copies, waits for them, and re-layouts, backward(): accum = accum.at[a:a + rows, b:b + cols].add(back[3 * a + b])  22.7 us
    dot_general x5, matrix products, backward(): jnp.einsum('krcd,rce->kde', taps, local, preferred_element_type=jnp.float32)  20.2 us
    another operation x15, other arithmetic  13.3 us
    ppermute x5, starting transfers between devices, from_behind(): return lax.ppermute(x, axis, pairs)  11.2 us
    another operation x1, loops' own time, per_device(): unused, grad_total = lax.fori_loop(0, sections + micro - 1, tick, start)  8.29 us
    add x25, other arithmetic, backward(): accum = accum.at[a:a + rows, b:b + cols].add(back[3 * a + b])  7.39 us
  transfers between devices with their start and end apart: 7, of which 2 were waited for; matrix products, arithmetic and copies ran while one was open for 10% of the time, Pallas kernels for 0%

commit v1 on v0

v1 whole, which is shorter than its diff:
```python
import functools
import math

import jax
import jax.numpy as jnp
import numpy as np
from jax import lax
from jax.experimental import pallas as pl
from jax.experimental.pallas import tpu as pltpu
from jax.sharding import PartitionSpec as P

LATS = 721
MIDDLE = (LATS - 1) / 2.0
NORM = float(np.mean(np.cos(math.pi * (np.arange(LATS) - MIDDLE) / (LATS - 1))))
F32 = jnp.float32
BF16 = jnp.bfloat16
NN = (((1,), (0,)), ((), ()))
NT = (((1,), (1,)), ((), ()))
VMEM_LIMIT = 24 << 20


def params_of(**more):
    return pltpu.CompilerParams(vmem_limit_bytes=VMEM_LIMIT, **more)


def spread(ref, at, values, rows, cols):
    length = rows * cols
    column = lax.broadcasted_iota(jnp.int32, values.shape, 0) % cols
    zeros = jnp.zeros((cols, values.shape[1]), BF16)
    for b in range(3):
        if b == 0:
            moved = jnp.where(column == 0, 0.0, pltpu.roll(values, 1, 0))
        elif b == 2:
            moved = jnp.where(column == cols - 1, 0.0, pltpu.roll(values, length - 1, 0))
        else:
            moved = values
        ref[(*at, b, pl.ds(0, cols), slice(None))] = zeros
        ref[(*at, b, pl.ds(cols, length), slice(None))] = moved.astype(BF16)
        ref[(*at, b, pl.ds(cols + length, cols), slice(None))] = zeros


def prepare(crop_rows, inputs, cotangent, weights, rows, cols):
    micro, length, width = inputs.shape
    taps = weights.shape[0]
    scale = (9.0 * width) ** (-0.5)

    def kernel(scalars, x_ref, cot_ref, w_ref, wbf_ref, slope_ref, top_ref, shifted, total):
        step = pl.program_id(0)

        @pl.when(step == 0)
        def _():
            for m in range(micro):
                spread(shifted, (m,), x_ref[m].astype(F32), rows, cols)
                here = lax.broadcasted_iota(jnp.int32, (rows, 128), 0) + scalars[m]
                angle = math.pi * (here.astype(F32) - MIDDLE) / (LATS - 1)
                factor = jnp.cos(angle) / NORM
                factor = jnp.where(scalars[micro] == 1, factor, 0.0)
                for i in range(rows):
                    line = jnp.concatenate([jnp.broadcast_to(factor[i : i + 1], (cols, 128))] * (width // 128), axis=1)
                    part = cot_ref[m, i * cols : (i + 1) * cols, :].astype(F32)
                    top_ref[m, i * cols : (i + 1) * cols, :] = (part * line).astype(BF16)
            total[...] = jnp.zeros_like(total)

        tap = w_ref[0].astype(BF16)
        wbf_ref[0] = tap
        a, b = step // 3, step % 3
        start = pl.multiple_of(a * cols, cols)
        for m in range(micro):
            total[m] += lax.dot_general(
                shifted[m, b, pl.ds(start, length), :], tap, NN, preferred_element_type=F32
            )

        @pl.when(step == taps - 1)
        def _():
            tangent = jnp.tanh(total[...] * scale)
            slope_ref[...] = 1.0 - tangent * tangent

    whole = lambda k, s: (0, 0, 0)
    return pl.pallas_call(
        kernel,
        out_shape=(
            jax.ShapeDtypeStruct((taps, width, width), BF16),
            jax.ShapeDtypeStruct((micro, length, width), F32),
            jax.ShapeDtypeStruct((micro, length, width), BF16),
        ),
        grid_spec=pltpu.PrefetchScalarGridSpec(
            num_scalar_prefetch=1,
            grid=(taps,),
            in_specs=[
                pl.BlockSpec((micro, length, width), whole),
                pl.BlockSpec((micro, length, width), whole),
                pl.BlockSpec((1, width, width), lambda k, s: (k, 0, 0)),
            ],
            out_specs=[
                pl.BlockSpec((1, width, width), lambda k, s: (k, 0, 0)),
                pl.BlockSpec((micro, length, width), whole),
                pl.BlockSpec((micro, length, width), whole),
            ],
            scratch_shapes=[
                pltpu.VMEM((micro, 3, length + 2 * cols, width), BF16),
                pltpu.VMEM((micro, length, width), F32),
            ],
        ),
        compiler_params=params_of(),
        name="prepare",
    )(crop_rows, inputs, cotangent, weights)


def stage(arrived, slope, weights, rows, cols):
    taps, width, _ = weights.shape
    length = rows * cols
    scale = (9.0 * width) ** (-0.5)
    count = len(arrived)

    def kernel(*refs):
        parts, (slope_ref, w_ref, out_ref, shifted) = refs[:count], refs[count:]
        grad = parts[0][...].astype(F32)
        for part in parts[1:]:
            grad += part[...].astype(F32)
        local = (grad * slope_ref[...]).astype(BF16).astype(F32)
        spread(shifted, (), local, rows, cols)
        total = None
        for a in range(3):
            for b in range(3):
                at = (2 - a) * cols
                term = lax.dot_general(
                    shifted[2 - b, at : at + length, :], w_ref[3 * a + b], NT, preferred_element_type=F32
                )
                total = term if total is None else total + term
        out_ref[...] = (grad + scale * total).astype(BF16)

    return pl.pallas_call(
        kernel,
        out_shape=jax.ShapeDtypeStruct((length, width), BF16),
        in_specs=[pl.BlockSpec(memory_space=pltpu.VMEM)] * (count + 2),
        out_specs=pl.BlockSpec(memory_space=pltpu.VMEM),
        scratch_shapes=[pltpu.VMEM((3, length + 2 * cols, width), BF16)],
        compiler_params=params_of(),
        name="stage",
    )(*arrived, slope, weights)


def turned_taps(inputs, rows, cols):
    blocks, length, width = inputs.shape

    def kernel(x_ref, out_ref, shifted):
        spread(shifted, (), x_ref[0].astype(F32), rows, cols)
        for a in range(3):
            for b in range(3):
                out_ref[0, 3 * a + b] = shifted[b, a * cols : a * cols + length, :].T

    return pl.pallas_call(
        kernel,
        grid=(blocks,),
        out_shape=jax.ShapeDtypeStruct((blocks, 9, width, length), BF16),
        in_specs=[pl.BlockSpec((1, length, width), lambda n: (n, 0, 0))],
        out_specs=pl.BlockSpec((1, 9, width, length), lambda n: (n, 0, 0, 0)),
        scratch_shapes=[pltpu.VMEM((3, length + 2 * cols, width), BF16)],
        compiler_params=params_of(),
        name="turned_taps",
    )(inputs)


def contract(base, momentum_base, turned, local, here, gains):
    taps, width, _ = base.shape
    share = momentum_base.shape[1]
    blocks, length, _ = local.shape

    def kernel(scalars, base_ref, mom_ref, t_ref, l_ref, out_ref, mom_out_ref, total):
        acc = None
        for n in range(blocks):
            term = lax.dot_general(t_ref[n, 0], l_ref[n], NN, preferred_element_type=F32)
            acc = term if acc is None else acc + term
        total[...] = acc
        out_ref[0] = base_ref[0] + gains[0] * acc
        own = total[pl.ds(pl.multiple_of(scalars[0], share), share), :]
        mom_out_ref[0] = mom_ref[0] + gains[1] * own

    return pl.pallas_call(
        kernel,
        out_shape=(
            jax.ShapeDtypeStruct(base.shape, F32),
            jax.ShapeDtypeStruct(momentum_base.shape, F32),
        ),
        grid_spec=pltpu.PrefetchScalarGridSpec(
            num_scalar_prefetch=1,
            grid=(taps,),
            in_specs=[
                pl.BlockSpec((1, width, width), lambda k, s: (k, 0, 0)),
                pl.BlockSpec((1, share, width), lambda k, s: (k, 0, 0)),
                pl.BlockSpec((blocks, 1, width, length), lambda k, s: (0, k, 0, 0)),
                pl.BlockSpec((blocks, length, width), lambda k, s: (0, 0, 0)),
            ],
            out_specs=[
                pl.BlockSpec((1, width, width), lambda k, s: (k, 0, 0)),
                pl.BlockSpec((1, share, width), lambda k, s: (k, 0, 0)),
            ],
            scratch_shapes=[pltpu.VMEM((width, width), F32)],
        ),
        compiler_params=params_of(),
        name="contract",
    )(here, base, momentum_base, turned, local)


def per_device(section_inputs, cotangent, crop_rows, drift, params, momentum):
    section, sections = lax.axis_index("section"), lax.axis_size("section")
    here, replicas = lax.axis_index("replica"), lax.axis_size("replica")
    micro, rows, cols, width = section_inputs.shape[2:]
    length = rows * cols
    share = width // replicas
    taps = params.shape[1]
    scale = (9.0 * width) ** (-0.5)
    bits = [1 << n for n in reversed(range((replicas - 1).bit_length()))]
    x = section_inputs.reshape(micro, length, width)

    def swap(value, bit):
        return lax.ppermute(value, "replica", [(i, i ^ bit) for i in range(replicas)])

    def spread_out(value):
        held = [value]
        for bit in bits:
            held += [swap(one, bit) for one in held]
        return held

    def hop(value, step):
        return lax.ppermute(value, "section", [(sections - 1 - step, sections - 2 - step)])

    scalars = jnp.concatenate([crop_rows.reshape(-1), (section == sections - 1).astype(jnp.int32)[None]])
    weights, slope, top = prepare(
        scalars, x, cotangent.reshape(micro, length, width), params[0], rows, cols
    )
    arrived = [[top[m]] for m in range(micro)]
    for step in range(sections - 1):
        for m in range(micro):
            arrived[m].append(hop(stage(arrived[m], slope[m], weights, rows, cols), step))

    held_x = spread_out(x)

    part = drift.reshape(taps, replicas, share, width)
    order = [jnp.bitwise_xor(here, j) for j in range(replicas)]
    parts = [lax.dynamic_index_in_dim(part, order[j], 1, keepdims=False) for j in range(replicas)]
    live = {j: parts[j].astype(F32) for j in range(replicas)}
    for bit in reversed(bits):
        sent = {j: swap(v.astype(BF16), bit) for j, v in live.items() if j & bit}
        live = {j: v + sent[j | bit].astype(F32) for j, v in live.items() if not j & bit}
    drift_mean = live[0] / replicas

    own = momentum[0]
    advance = 1.33 * drift_mean + 0.567 * own
    pieces = spread_out(advance.astype(BF16))
    whole = jnp.zeros((taps, replicas, share, width), BF16)
    for j, piece in enumerate(pieces):
        q = 0
        for n, bit in enumerate(bits):
            if j >> n & 1:
                q |= bit
        whole = lax.dynamic_update_index_in_dim(whole, piece, jnp.bitwise_xor(here, q), 1)
    base = params[0] - whole.reshape(taps, width, width).astype(F32)
    momentum_base = 0.9 * own + drift_mean

    gain = 0.5 * scale / replicas
    gains = (-1.33 * gain, gain)
    start = (here * share).astype(jnp.int32)[None]
    for m in range(micro):
        local = sum(one.astype(F32) for one in arrived[m]) * slope[m]
        held_local = spread_out(local.astype(BF16))
        turned = turned_taps(jnp.stack([one[m] for one in held_x]), rows, cols)
        base, momentum_base = contract(
            base, momentum_base, turned, jnp.stack(held_local), start, gains
        )
    return (base[None], momentum_base[None])


def solution(mesh):
    placed = (
        P(("groups", "replica"), "section", None, None, None, None),
        P(("groups", "replica"), None, None, None, None),
        P(("groups", "replica"), None),
        P(("groups", "replica"), "section", None, None, None),
        P(("groups", "section"), None, None, None),
        P(("groups", "section"), None, "replica", None),
    )
    return jax.shard_map(
        per_device,
        mesh=mesh,
        in_specs=placed,
        out_specs=(
            P(("groups", "section"), None, None, None),
            P(("groups", "section"), None, "replica", None),
        ),
        check_vma=False,
    )
```

time: 209 us -> 68.9 us (0.33)
  the two profiles are of different devices: /device:TPU:27 before, /device:TPU:11 now
where the time goes in v1:
time: 68.9 us; the launch traced here: 68.5 us
  starting transfers between devices  19.6 us (28%)
  Pallas kernels  18.7 us (27%)
  waiting for transfers between devices  17.1 us (25%)
  local copies, waits for them, and re-layouts  9.05 us (13%)
  other arithmetic  2.96 us (4%)
  between operations  1.04 us (2%)
    ppermute x15, waiting for transfers between devices, swap(): lax.ppermute(value, 'replica', [(i, i ^ bit) for i in range(replicas)])  15.7 us
    ppermute x15, starting transfers between devices, swap(): lax.ppermute(value, 'replica', [(i, i ^ bit) for i in range(replicas)])  12.9 us
    pallas_call x2, Pallas kernels, contract(): pl.pallas_call(kernel, out_shape=(jax.ShapeDtypeStruct(base.shape, F32),...  8.55 us
    ppermute x6, starting transfers between devices, hop(): lax.ppermute(value, 'section', [(sections - 1 - step, sections - 2 - step)])  6.65 us
    pallas_call x1, Pallas kernels, prepare(): pl.pallas_call(kernel, out_shape=(jax.ShapeDtypeStruct((taps, width, widt...  4.04 us
    slice x4, local copies, waits for them, and re-layouts, per_device(): turned = turned_taps(jnp.stack([one[m] for one in held_x]), rows, cols)  3.67 us
    unnamed x14, local copies, waits for them, and re-layouts  3.1 us
    pallas_call x6, Pallas kernels, stage(): pl.pallas_call(kernel, out_shape=jax.ShapeDtypeStruct((length, width), BF...  3.09 us
  transfers between devices with their start and end apart: 21, of which 5 were waited for; matrix products, arithmetic and copies ran while one was open for 11% of the time, Pallas kernels for 8%

profile of v1, /device:TPU:11, one launch (start us, length us, event | category | flops | bytes accessed | tf_op | source)
XLA Modules:
  0.0 68.5 jit_solution(1578608270894813305)
XLA Ops:
  0.6 0.7 %pad_add_fusion.scalars = s32[3]{0:T(128)S(1)} fusion(s32[1]{0:T(128)} %bitcast.19, s32[2]{0:T(128)} %bitcast.92), kind=kLoop, calls=%fused_computation.24 | loop fusion | flops 3 | bytes 24 | tf_op jit(solution)/shard_map/concatenate | solution.py:228
  1.4 1.7 %copy-done = f32[1,9,256,256]{3,2,1,0:T(8,128)S(1)} copy-done((f32[1,9,256,256]{3,2,1,0:T(8,128)S(1)}, f32[1,9,256,256]{3,2,1,0:T(8,128)}, u32[]{:S(2)}) %copy-start) | copy-done | bytes 2359320
  3.0 0.9 %copy-done.2 = bf16[1,2,16,16,256]{4,3,2,1,0:T(8,128)(2,1)S(1)} copy-done((bf16[1,2,16,16,256]{4,3,2,1,0:T(8,128)(2,1)S(1)}, bf16[1,2,16,16,256]{4,3,2,1,0:T(8,128)(2,1)}, u32[]{:S(2)}) %copy-start.2) | copy-done | bytes 262168
  4.0 4.0 %prepare.1 = (bf16[9,256,256]{2,1,0:T(8,128)(2,1)S(1)}, f32[2,256,256]{2,1,0:T(8,128)S(1)}, bf16[2,256,256]{2,1,0:T(8,128)(2,1)S(1)}) custom-call(s32[3]{0:T(128)S(1)} %pad_add_fusion.scalars, bf16[2,256,256]{2,1,0:T(8,128)(2,1)} %bitcast.17.x_ref, bf16[2,256,256]{2,1,0:T(8,128)(2,1)S(1)} %bitcast.75, f32[9,256,256]{2,1,0:T(8,128)S(1)} %bitcast.74), custom_call_target="tpu_custom_call" | custom-call | tf_op jit(solution)/shard_map/prepare/pallas_call | solution.py:79
  8.1 0.5 stage.9
  8.6 0.7 collective-permute-start.15
  9.3 0.5 stage.6
  9.8 0.7 collective-permute-start.9
  10.5 0.3 collective-permute-start.6
  10.8 0.9 %collective-permute-start.7 = (bf16[2,256,256]{2,1,0:T(8,128)(2,1)}, bf16[2,256,256]{2,1,0:T(8,128)(2,1)}, u32[]{:S(2)}, u32[]{:S(2)}) collective-permute-start(bf16[2,256,256]{2,1,0:T(8,128)(2,1)} %bitcast.17.x_ref), channel_id=1, source_target_pairs={{0,1},{1,0},{2,3},{3,2},{4,5},{5,4},{6,7},{7,6},{8,9},{9,8},{10,11... | collective-permute-start | bytes 786440 | tf_op jit(solution)/shard_map/ppermute | solution.py:217
  11.7 1.9 %dynamic-slice_bitcast_fusion.1 = (bf16[9,64,256]{2,1,0:T(8,128)(2,1)}, bf16[9,64,256]{2,1,0:T(8,128)(2,1)}) fusion(bf16[9,4,64,256]{3,2,1,0:T(8,128)(2,1)} %bitcast.76, s32[]{:T(128)S(6)} %select_n.19, s32[]{:T(128)S(6)} %select_n.21), kind=kLoop, calls=%fused_computation.17 | loop fusion | bytes 1179656 | tf_op jit(solution)/shard_map/jit(dynamic_index_in_dim)/squeeze | solution.py:241
  13.7 0.5 stage.10
  14.2 1.3 %collective-permute-start.16 = (bf16[256,256]{1,0:T(8,128)(2,1)S(1)}, bf16[256,256]{1,0:T(8,128)(2,1)S(1)}, u32[]{:S(2)}, u32[]{:S(2)}) collective-permute-start(bf16[256,256]{1,0:T(8,128)(2,1)S(1)} %stage.10), channel_id=1, source_target_pairs={{8,4},{9,5},{10,6},{11,7},{24,20},{25,21},{26,22},{27,23}} | collective-permute-start | bytes 393224 | tf_op jit(solution)/shard_map/ppermute | solution.py:226
  15.5 0.5 stage.7
  16.0 1.3 %collective-permute-start.10 = (bf16[256,256]{1,0:T(8,128)(2,1)S(1)}, bf16[256,256]{1,0:T(8,128)(2,1)S(1)}, u32[]{:S(2)}, u32[]{:S(2)}) collective-permute-start(bf16[256,256]{1,0:T(8,128)(2,1)S(1)} %stage.7), channel_id=1, source_target_pairs={{8,4},{9,5},{10,6},{11,7},{24,20},{25,21},{26,22},{27,23}} | collective-permute-start | bytes 393224 | tf_op jit(solution)/shard_map/ppermute | solution.py:226
  17.3 1.7 %fusion.4 = (bf16[1,1,1,16,16,256]{5,4,3,2,1,0:T(8,128)(2,1)}, bf16[1,1,1,16,16,256]{5,4,3,2,1,0:T(8,128)(2,1)}) fusion(bf16[1,1,2,16,16,256]{5,4,3,2,1,0:T(8,128)(2,1)} %param.6), kind=kLoop, calls=%fused_computation.25 | loop fusion | bytes 524288 | tf_op jit(solution)/shard_map/slice | solution.py:267
  19.0 1.4 %collective-permute-done.16.refs_2_ = bf16[256,256]{1,0:T(8,128)(2,1)S(1)} collective-permute-done((bf16[256,256]{1,0:T(8,128)(2,1)S(1)}, bf16[256,256]{1,0:T(8,128)(2,1)S(1)}, u32[]{:S(2)}, u32[]{:S(2)}) %collective-permute-start.16) | collective-permute-done | bytes 131104 | tf_op jit(solution)/shard_map/ppermute | solution.py:226
  20.4 4.5 %collective-permute-start = (bf16[9,64,256]{2,1,0:T(8,128)(2,1)}, bf16[9,64,256]{2,1,0:T(8,128)(2,1)S(1)}, u32[]{:S(2)}, u32[]{:S(2)}) collective-permute-start(bf16[9,64,256]{2,1,0:T(8,128)(2,1)} %get-tuple-element.18), channel_id=1, source_target_pairs={{0,1},{1,0},{2,3},{3,2},{4,5},{5,4},{6,7},{7,6},{8,9},{9,8},{10,11... | collective-permute-start | bytes 884744 | tf_op jit(solution)/shard_map/ppermute | solution.py:217
  24.9 0.5 stage.11
  25.4 1.4 %collective-permute-start.17 = (bf16[256,256]{1,0:T(8,128)(2,1)S(1)}, bf16[256,256]{1,0:T(8,128)(2,1)S(1)}, u32[]{:S(2)}, u32[]{:S(2)}) collective-permute-start(bf16[256,256]{1,0:T(8,128)(2,1)S(1)} %stage.11), channel_id=1, source_target_pairs={{4,0},{5,1},{6,2},{7,3},{20,16},{21,17},{22,18},{23,19}} | collective-permute-start | bytes 393224 | tf_op jit(solution)/shard_map/ppermute | solution.py:226
  26.9 0.5 stage.8
  27.4 1.3 %collective-permute-start.11 = (bf16[256,256]{1,0:T(8,128)(2,1)S(1)}, bf16[256,256]{1,0:T(8,128)(2,1)S(1)}, u32[]{:S(2)}, u32[]{:S(2)}) collective-permute-start(bf16[256,256]{1,0:T(8,128)(2,1)S(1)} %stage.8), channel_id=1, source_target_pairs={{4,0},{5,1},{6,2},{7,3},{20,16},{21,17},{22,18},{23,19}} | collective-permute-start | bytes 393224 | tf_op jit(solution)/shard_map/ppermute | solution.py:226
  28.7 1.0 %fusion.5 = (bf16[1,256,256]{2,1,0:T(8,128)(2,1)S(1)}, bf16[1,256,256]{2,1,0:T(8,128)(2,1)S(1)}) fusion(bf16[2,256,256]{2,1,0:T(8,128)(2,1)} %collective-permute-done.6), kind=kLoop, calls=%fused_computation.26 | loop fusion | bytes 524288 | tf_op jit(solution)/shard_map/slice | solution.py:267
  29.7 1.1 %collective-permute-start.8 = (bf16[2,256,256]{2,1,0:T(8,128)(2,1)}, bf16[2,256,256]{2,1,0:T(8,128)(2,1)S(1)}, u32[]{:S(2)}, u32[]{:S(2)}) collective-permute-start(bf16[2,256,256]{2,1,0:T(8,128)(2,1)} %collective-permute-done.6), channel_id=1, source_target_pairs={{0,1},{1,0},{2,3},{3,2},{4,5},{5,4},{6,7},{7,6},{8,9},{9,8},{10,11... | collective-permute-start | bytes 786440 | tf_op jit(solution)/shard_map/ppermute | solution.py:217
  30.8 1.0 %fusion.6 = (bf16[1,256,256]{2,1,0:T(8,128)(2,1)S(1)}, bf16[1,256,256]{2,1,0:T(8,128)(2,1)S(1)}) fusion(bf16[2,256,256]{2,1,0:T(8,128)(2,1)} %collective-permute-done.7), kind=kLoop, calls=%fused_computation.27 | loop fusion | bytes 524288 | tf_op jit(solution)/shard_map/slice | solution.py:267
  31.8 1.0 %fusion = bf16[9,64,256]{2,1,0:T(8,128)(2,1)S(1)} fusion(bf16[9,64,256]{2,1,0:T(8,128)(2,1)} %collective-permute-done.1, bf16[9,4,64,256]{3,2,1,0:T(8,128)(2,1)S(1)} %bitcast.77, s32[]{:T(128)S(6)} %select_n.20), kind=kLoop, calls=%fused_computation.2 | loop fusion | flops 589824 | bytes 884740 | tf_op jit(solution)/shard_map/convert_element_type | solution.py:244
  32.9 0.3 collective-permute-start.2
  33.3 1.3 %collective-permute-start.12 = (bf16[256,256]{1,0:T(8,128)(2,1)S(1)}, bf16[256,256]{1,0:T(8,128)(2,1)S(1)}, u32[]{:S(2)}, u32[]{:S(2)}) collective-permute-start(bf16[256,256]{1,0:T(8,128)(2,1)S(1)} %get-tuple-element.21), channel_id=1, source_target_pairs={{0,2},{1,3},{2,0},{3,1},{4,6},{5,7},{6,4},{7,5},{8,10},{9,11},{10,... | collective-permute-start | bytes 393224 | tf_op jit(solution)/shard_map/ppermute | solution.py:217
  34.6 0.6 collective-permute-start.13
  35.2 0.2 collective-permute-start.18
  35.5 1.5 %turned_taps.2.t_ref = bf16[4,9,256,256]{3,2,1,0:T(8,128)(2,1)S(1)} custom-call(bf16[4,256,256]{2,1,0:T(8,128)(2,1)S(1)} %pad_maximum_fusion.x_ref), custom_call_target="tpu_custom_call" | custom-call | tf_op jit(solution)/shard_map/turned_taps/pallas_call | solution.py:152
  37.1 1.5 %turned_taps.3.t_ref = bf16[4,9,256,256]{3,2,1,0:T(8,128)(2,1)S(1)} custom-call(bf16[4,256,256]{2,1,0:T(8,128)(2,1)S(1)} %pad_maximum_fusion.2.x_ref), custom_call_target="tpu_custom_call" | custom-call | tf_op jit(solution)/shard_map/turned_taps/pallas_call | solution.py:152
  38.7 0.3 collective-permute-start.19
  39.0 5.3 %collective-permute-done.12 = bf16[256,256]{1,0:T(8,128)(2,1)S(1)} collective-permute-done((bf16[256,256]{1,0:T(8,128)(2,1)S(1)}, bf16[256,256]{1,0:T(8,128)(2,1)S(1)}, u32[]{:S(2)}, u32[]{:S(2)}) %collective-permute-start.12) | collective-permute-done | bytes 131104 | tf_op jit(solution)/shard_map/ppermute | solution.py:217
  44.4 1.2 %collective-permute-start.14 = (bf16[256,256]{1,0:T(8,128)(2,1)S(1)}, bf16[256,256]{1,0:T(8,128)(2,1)S(1)}, u32[]{:S(2)}, u32[]{:S(2)}) collective-permute-start(bf16[256,256]{1,0:T(8,128)(2,1)S(1)} %collective-permute-done.12), channel_id=1, source_target_pairs={{0,1},{1,0},{2,3},{3,2},{4,5},{5,4},{6,7},{7,6},{8,9},{9,8},{10,11... | collective-permute-start | bytes 393224 | tf_op jit(solution)/shard_map/ppermute | solution.py:217
  45.5 1.6 %collective-permute-done.18 = bf16[256,256]{1,0:T(8,128)(2,1)S(1)} collective-permute-done((bf16[256,256]{1,0:T(8,128)(2,1)S(1)}, bf16[256,256]{1,0:T(8,128)(2,1)S(1)}, u32[]{:S(2)}, u32[]{:S(2)}) %collective-permute-start.18) | collective-permute-done | bytes 131104 | tf_op jit(solution)/shard_map/ppermute | solution.py:217
  47.2 0.8 %collective-permute-start.20 = (bf16[256,256]{1,0:T(8,128)(2,1)S(1)}, bf16[256,256]{1,0:T(8,128)(2,1)S(1)}, u32[]{:S(2)}, u32[]{:S(2)}) collective-permute-start(bf16[256,256]{1,0:T(8,128)(2,1)S(1)} %collective-permute-done.18), channel_id=1, source_target_pairs={{0,1},{1,0},{2,3},{3,2},{4,5},{5,4},{6,7},{7,6},{8,9},{9,8},{10,11... | collective-permute-start | bytes 393224 | tf_op jit(solution)/shard_map/ppermute | solution.py:217
  48.1 0.2 bitcast_dynamic-update-slice_fusion.3
  48.3 0.3 collective-permute-start.3
  48.6 0.2 bitcast_add_fusion.mom_ref
  48.8 0.3 collective-permute-start.4
  49.3 7.7 %collective-permute-done.3 = bf16[9,64,256]{2,1,0:T(8,128)(2,1)S(1)} collective-permute-done((bf16[9,64,256]{2,1,0:T(8,128)(2,1)S(1)}, bf16[9,64,256]{2,1,0:T(8,128)(2,1)S(1)}, u32[]{:S(2)}, u32[]{:S(2)}) %collective-permute-start.3) | collective-permute-done | bytes 294944 | tf_op jit(solution)/shard_map/ppermute | solution.py:217
  57.0 0.8 %collective-permute-start.5 = (bf16[9,64,256]{2,1,0:T(8,128)(2,1)S(1)}, bf16[9,64,256]{2,1,0:T(8,128)(2,1)S(1)}, u32[]{:S(2)}, u32[]{:S(2)}) collective-permute-start(bf16[9,64,256]{2,1,0:T(8,128)(2,1)S(1)} %collective-permute-done.3), channel_id=1, source_target_pairs={{0,1},{1,0},{2,3},{3,2},{4,5},{5,4},{6,7},{7,6},{8,9},{9,8},{10,11... | collective-permute-start | bytes 884744 | tf_op jit(solution)/shard_map/ppermute | solution.py:217
  58.0 1.0 %collective-permute-done.5 = bf16[9,64,256]{2,1,0:T(8,128)(2,1)S(1)} collective-permute-done((bf16[9,64,256]{2,1,0:T(8,128)(2,1)S(1)}, bf16[9,64,256]{2,1,0:T(8,128)(2,1)S(1)}, u32[]{:S(2)}, u32[]{:S(2)}) %collective-permute-start.5) | collective-permute-done | bytes 294944 | tf_op jit(solution)/shard_map/ppermute | solution.py:217
  59.0 0.5 copy-done.1
  59.5 0.4 convert_subtract_fusion.base_ref
  59.9 3.2 %contract.2 = (f32[9,256,256]{2,1,0:T(8,128)S(1)}, f32[9,64,256]{2,1,0:T(8,128)S(1)}) custom-call(s32[1]{0:T(128)} %bitcast.scalars, f32[9,256,256]{2,1,0:T(8,128)S(1)} %convert_subtract_fusion.base_ref, f32[9,64,256]{2,1,0:T(8,128)S(1)} %bitcast_add_fusion.mom_ref, bf16[4,9,256,256]{3,2,1,0:T(8,128)(2,1)S(1)} %turned_taps.2.t_ref, ...), custom_call_target="tpu_custom_call" | custom-call | tf_op jit(solution)/shard_map/contract/pallas_call | solution.py:179
  63.2 5.3 %contract.3 = (f32[9,256,256]{2,1,0:T(8,128)}, f32[9,64,256]{2,1,0:T(8,128)}) custom-call(s32[1]{0:T(128)} %bitcast.scalars, f32[9,256,256]{2,1,0:T(8,128)S(1)} %get-tuple-element.12.base_ref, f32[9,64,256]{2,1,0:T(8,128)S(1)} %get-tuple-element.13.mom_ref, bf16[4,9,256,256]{3,2,1,0:T(8,128)(2,1)S(1)} %turned_taps.3.t_ref, ...), custom_call_target="tpu_custom_call" | custom-call | tf_op jit(solution)/shard_map/contract/pallas_call | solution.py:179
  (41 shorter events, 0.9 us)
Async XLA Ops:
  1.4 1.7 %copy-start = (f32[1,9,256,256]{3,2,1,0:T(8,128)S(1)}, f32[1,9,256,256]{3,2,1,0:T(8,128)}, u32[]{:S(2)}) copy-start(f32[1,9,256,256]{3,2,1,0:T(8,128)} %param.10) | copy-start | bytes 7077892
  3.0 0.9 %copy-start.2 = (bf16[1,2,16,16,256]{4,3,2,1,0:T(8,128)(2,1)S(1)}, bf16[1,2,16,16,256]{4,3,2,1,0:T(8,128)(2,1)}, u32[]{:S(2)}) copy-start(bf16[1,2,16,16,256]{4,3,2,1,0:T(8,128)(2,1)} %param.7) | copy-start | bytes 786436
  8.6 5.0 %collective-permute-start.15 = (bf16[256,256]{1,0:T(8,128)(2,1)S(1)}, bf16[256,256]{1,0:T(8,128)(2,1)S(1)}, u32[]{:S(2)}, u32[]{:S(2)}) collective-permute-start(bf16[256,256]{1,0:T(8,128)(2,1)S(1)} %stage.9), channel_id=1, source_target_pairs={{12,8},{13,9},{14,10},{15,11},{28,24},{29,25},{30,26},{31,27}} | collective-permute-start | bytes 393224 | tf_op jit(solution)/shard_map/ppermute | solution.py:226
  9.8 5.7 %collective-permute-start.9 = (bf16[256,256]{1,0:T(8,128)(2,1)S(1)}, bf16[256,256]{1,0:T(8,128)(2,1)S(1)}, u32[]{:S(2)}, u32[]{:S(2)}) collective-permute-start(bf16[256,256]{1,0:T(8,128)(2,1)S(1)} %stage.6), channel_id=1, source_target_pairs={{12,8},{13,9},{14,10},{15,11},{28,24},{29,25},{30,26},{31,27}} | collective-permute-start | bytes 393224 | tf_op jit(solution)/shard_map/ppermute | solution.py:226
  10.5 16.9 %collective-permute-start.6 = (bf16[2,256,256]{2,1,0:T(8,128)(2,1)}, bf16[2,256,256]{2,1,0:T(8,128)(2,1)}, u32[]{:S(2)}, u32[]{:S(2)}) collective-permute-start(bf16[2,256,256]{2,1,0:T(8,128)(2,1)} %bitcast.17.x_ref), channel_id=1, source_target_pairs={{0,2},{1,3},{2,0},{3,1},{4,6},{5,7},{6,4},{7,5},{8,10},{9,11},{10,... | collective-permute-start | bytes 786440 | tf_op jit(solution)/shard_map/ppermute | solution.py:217
  10.8 18.9 %collective-permute-start.7 = (bf16[2,256,256]{2,1,0:T(8,128)(2,1)}, bf16[2,256,256]{2,1,0:T(8,128)(2,1)}, u32[]{:S(2)}, u32[]{:S(2)}) collective-permute-start(bf16[2,256,256]{2,1,0:T(8,128)(2,1)} %bitcast.17.x_ref), channel_id=1, source_target_pairs={{0,1},{1,0},{2,3},{3,2},{4,5},{5,4},{6,7},{7,6},{8,9},{9,8},{10,11... | collective-permute-start | bytes 786440 | tf_op jit(solution)/shard_map/ppermute | solution.py:217
  13.7 18.1 %collective-permute-start.1 = (bf16[9,64,256]{2,1,0:T(8,128)(2,1)}, bf16[9,64,256]{2,1,0:T(8,128)(2,1)}, u32[]{:S(2)}, u32[]{:S(2)}) collective-permute-start(bf16[9,64,256]{2,1,0:T(8,128)(2,1)} %get-tuple-element.19), channel_id=1, source_target_pairs={{0,1},{1,0},{2,3},{3,2},{4,5},{5,4},{6,7},{7,6},{8,9},{9,8},{10,11... | collective-permute-start | bytes 884744 | tf_op jit(solution)/shard_map/ppermute | solution.py:217
  14.2 6.2 %collective-permute-start.16 = (bf16[256,256]{1,0:T(8,128)(2,1)S(1)}, bf16[256,256]{1,0:T(8,128)(2,1)S(1)}, u32[]{:S(2)}, u32[]{:S(2)}) collective-permute-start(bf16[256,256]{1,0:T(8,128)(2,1)S(1)} %stage.10), channel_id=1, source_target_pairs={{8,4},{9,5},{10,6},{11,7},{24,20},{25,21},{26,22},{27,23}} | collective-permute-start | bytes 393224 | tf_op jit(solution)/shard_map/ppermute | solution.py:226
  16.0 9.4 %collective-permute-start.10 = (bf16[256,256]{1,0:T(8,128)(2,1)S(1)}, bf16[256,256]{1,0:T(8,128)(2,1)S(1)}, u32[]{:S(2)}, u32[]{:S(2)}) collective-permute-start(bf16[256,256]{1,0:T(8,128)(2,1)S(1)} %stage.7), channel_id=1, source_target_pairs={{8,4},{9,5},{10,6},{11,7},{24,20},{25,21},{26,22},{27,23}} | collective-permute-start | bytes 393224 | tf_op jit(solution)/shard_map/ppermute | solution.py:226
  20.4 18.3 %collective-permute-start = (bf16[9,64,256]{2,1,0:T(8,128)(2,1)}, bf16[9,64,256]{2,1,0:T(8,128)(2,1)S(1)}, u32[]{:S(2)}, u32[]{:S(2)}) collective-permute-start(bf16[9,64,256]{2,1,0:T(8,128)(2,1)} %get-tuple-element.18), channel_id=1, source_target_pairs={{0,1},{1,0},{2,3},{3,2},{4,5},{5,4},{6,7},{7,6},{8,9},{9,8},{10,11... | collective-permute-start | bytes 884744 | tf_op jit(solution)/shard_map/ppermute | solution.py:217
  25.4 6.4 %copy-start.4 = (bf16[1,1,9,256,256]{4,3,2,1,0:T(8,128)(2,1)S(1)}, bf16[1,1,9,256,256]{4,3,2,1,0:T(8,128)(2,1)}, u32[]{:S(2)}) copy-start(bf16[1,1,9,256,256]{4,3,2,1,0:T(8,128)(2,1)} %param.9) | copy-start | bytes 3538948
  25.4 7.7 %collective-permute-start.17 = (bf16[256,256]{1,0:T(8,128)(2,1)S(1)}, bf16[256,256]{1,0:T(8,128)(2,1)S(1)}, u32[]{:S(2)}, u32[]{:S(2)}) collective-permute-start(bf16[256,256]{1,0:T(8,128)(2,1)S(1)} %stage.11), channel_id=1, source_target_pairs={{4,0},{5,1},{6,2},{7,3},{20,16},{21,17},{22,18},{23,19}} | collective-permute-start | bytes 393224 | tf_op jit(solution)/shard_map/ppermute | solution.py:226
  27.4 5.7 %collective-permute-start.11 = (bf16[256,256]{1,0:T(8,128)(2,1)S(1)}, bf16[256,256]{1,0:T(8,128)(2,1)S(1)}, u32[]{:S(2)}, u32[]{:S(2)}) collective-permute-start(bf16[256,256]{1,0:T(8,128)(2,1)S(1)} %stage.8), channel_id=1, source_target_pairs={{4,0},{5,1},{6,2},{7,3},{20,16},{21,17},{22,18},{23,19}} | collective-permute-start | bytes 393224 | tf_op jit(solution)/shard_map/ppermute | solution.py:226
  29.7 5.5 %collective-permute-start.8 = (bf16[2,256,256]{2,1,0:T(8,128)(2,1)}, bf16[2,256,256]{2,1,0:T(8,128)(2,1)S(1)}, u32[]{:S(2)}, u32[]{:S(2)}) collective-permute-start(bf16[2,256,256]{2,1,0:T(8,128)(2,1)} %collective-permute-done.6), channel_id=1, source_target_pairs={{0,1},{1,0},{2,3},{3,2},{4,5},{5,4},{6,7},{7,6},{8,9},{9,8},{10,11... | collective-permute-start | bytes 786440 | tf_op jit(solution)/shard_map/ppermute | solution.py:217
  32.8 2.6 %copy-start.6 = (bf16[1,1,1,16,16,256]{5,4,3,2,1,0:T(8,128)(2,1)S(1)}, bf16[1,1,1,16,16,256]{5,4,3,2,1,0:T(8,128)(2,1)}, u32[]{:S(2)}) copy-start(bf16[1,1,1,16,16,256]{5,4,3,2,1,0:T(8,128)(2,1)} %get-tuple-element.27) | copy-start | bytes 393220
  32.9 15.1 %collective-permute-start.2 = (bf16[9,64,256]{2,1,0:T(8,128)(2,1)S(1)}, bf16[9,64,256]{2,1,0:T(8,128)(2,1)S(1)}, u32[]{:S(2)}, u32[]{:S(2)}) collective-permute-start(bf16[9,64,256]{2,1,0:T(8,128)(2,1)S(1)} %fusion), channel_id=1, source_target_pairs={{0,2},{1,3},{2,0},{3,1},{4,6},{5,7},{6,4},{7,5},{8,10},{9,11},{10,... | collective-permute-start | bytes 884744 | tf_op jit(solution)/shard_map/ppermute | solution.py:217
  33.3 11.1 %collective-permute-start.12 = (bf16[256,256]{1,0:T(8,128)(2,1)S(1)}, bf16[256,256]{1,0:T(8,128)(2,1)S(1)}, u32[]{:S(2)}, u32[]{:S(2)}) collective-permute-start(bf16[256,256]{1,0:T(8,128)(2,1)S(1)} %get-tuple-element.21), channel_id=1, source_target_pairs={{0,2},{1,3},{2,0},{3,1},{4,6},{5,7},{6,4},{7,5},{8,10},{9,11},{10,... | collective-permute-start | bytes 393224 | tf_op jit(solution)/shard_map/ppermute | solution.py:217
  34.6 14.1 %collective-permute-start.13 = (bf16[256,256]{1,0:T(8,128)(2,1)S(1)}, bf16[256,256]{1,0:T(8,128)(2,1)S(1)}, u32[]{:S(2)}, u32[]{:S(2)}) collective-permute-start(bf16[256,256]{1,0:T(8,128)(2,1)S(1)} %get-tuple-element.21), channel_id=1, source_target_pairs={{0,1},{1,0},{2,3},{3,2},{4,5},{5,4},{6,7},{7,6},{8,9},{9,8},{10,11... | collective-permute-start | bytes 393224 | tf_op jit(solution)/shard_map/ppermute | solution.py:217
  35.2 12.0 %collective-permute-start.18 = (bf16[256,256]{1,0:T(8,128)(2,1)S(1)}, bf16[256,256]{1,0:T(8,128)(2,1)S(1)}, u32[]{:S(2)}, u32[]{:S(2)}) collective-permute-start(bf16[256,256]{1,0:T(8,128)(2,1)S(1)} %get-tuple-element.20), channel_id=1, source_target_pairs={{0,2},{1,3},{2,0},{3,1},{4,6},{5,7},{6,4},{7,5},{8,10},{9,11},{10,... | collective-permute-start | bytes 393224 | tf_op jit(solution)/shard_map/ppermute | solution.py:217
  35.5 1.5 %copy-start.5 = (bf16[1,1,1,16,16,256]{5,4,3,2,1,0:T(8,128)(2,1)S(1)}, bf16[1,1,1,16,16,256]{5,4,3,2,1,0:T(8,128)(2,1)}, u32[]{:S(2)}) copy-start(bf16[1,1,1,16,16,256]{5,4,3,2,1,0:T(8,128)(2,1)} %get-tuple-element.26) | copy-start | bytes 393220
  38.7 9.4 %copy-start.3 = (f32[1,9,64,256]{3,2,1,0:T(8,128)S(1)}, f32[1,9,64,256]{3,2,1,0:T(8,128)}, u32[]{:S(2)}) copy-start(f32[1,9,64,256]{3,2,1,0:T(8,128)} %param.11) | copy-start | bytes 1769476
  38.7 10.5 %collective-permute-start.19 = (bf16[256,256]{1,0:T(8,128)(2,1)S(1)}, bf16[256,256]{1,0:T(8,128)(2,1)S(1)}, u32[]{:S(2)}, u32[]{:S(2)}) collective-permute-start(bf16[256,256]{1,0:T(8,128)(2,1)S(1)} %get-tuple-element.20), channel_id=1, source_target_pairs={{0,1},{1,0},{2,3},{3,2},{4,5},{5,4},{6,7},{7,6},{8,9},{9,8},{10,11... | collective-permute-start | bytes 393224 | tf_op jit(solution)/shard_map/ppermute | solution.py:217
  44.4 4.8 %collective-permute-start.14 = (bf16[256,256]{1,0:T(8,128)(2,1)S(1)}, bf16[256,256]{1,0:T(8,128)(2,1)S(1)}, u32[]{:S(2)}, u32[]{:S(2)}) collective-permute-start(bf16[256,256]{1,0:T(8,128)(2,1)S(1)} %collective-permute-done.12), channel_id=1, source_target_pairs={{0,1},{1,0},{2,3},{3,2},{4,5},{5,4},{6,7},{7,6},{8,9},{9,8},{10,11... | collective-permute-start | bytes 393224 | tf_op jit(solution)/shard_map/ppermute | solution.py:217
  47.2 2.0 %collective-permute-start.20 = (bf16[256,256]{1,0:T(8,128)(2,1)S(1)}, bf16[256,256]{1,0:T(8,128)(2,1)S(1)}, u32[]{:S(2)}, u32[]{:S(2)}) collective-permute-start(bf16[256,256]{1,0:T(8,128)(2,1)S(1)} %collective-permute-done.18), channel_id=1, source_target_pairs={{0,1},{1,0},{2,3},{3,2},{4,5},{5,4},{6,7},{7,6},{8,9},{9,8},{10,11... | collective-permute-start | bytes 393224 | tf_op jit(solution)/shard_map/ppermute | solution.py:217
  48.3 8.7 %collective-permute-start.3 = (bf16[9,64,256]{2,1,0:T(8,128)(2,1)S(1)}, bf16[9,64,256]{2,1,0:T(8,128)(2,1)S(1)}, u32[]{:S(2)}, u32[]{:S(2)}) collective-permute-start(bf16[9,64,256]{2,1,0:T(8,128)(2,1)S(1)} %get-tuple-element.17), channel_id=1, source_target_pairs={{0,2},{1,3},{2,0},{3,1},{4,6},{5,7},{6,4},{7,5},{8,10},{9,11},{10,... | collective-permute-start | bytes 884744 | tf_op jit(solution)/shard_map/ppermute | solution.py:217
  48.8 9.2 %collective-permute-start.4 = (bf16[9,64,256]{2,1,0:T(8,128)(2,1)S(1)}, bf16[9,64,256]{2,1,0:T(8,128)(2,1)S(1)}, u32[]{:S(2)}, u32[]{:S(2)}) collective-permute-start(bf16[9,64,256]{2,1,0:T(8,128)(2,1)S(1)} %get-tuple-element.17), channel_id=1, source_target_pairs={{0,1},{1,0},{2,3},{3,2},{4,5},{5,4},{6,7},{7,6},{8,9},{9,8},{10,11... | collective-permute-start | bytes 884744 | tf_op jit(solution)/shard_map/ppermute | solution.py:217
  57.0 2.0 %collective-permute-start.5 = (bf16[9,64,256]{2,1,0:T(8,128)(2,1)S(1)}, bf16[9,64,256]{2,1,0:T(8,128)(2,1)S(1)}, u32[]{:S(2)}, u32[]{:S(2)}) collective-permute-start(bf16[9,64,256]{2,1,0:T(8,128)(2,1)S(1)} %collective-permute-done.3), channel_id=1, source_target_pairs={{0,1},{1,0},{2,3},{3,2},{4,5},{5,4},{6,7},{7,6},{8,9},{9,8},{10,11... | collective-permute-start | bytes 884744 | tf_op jit(solution)/shard_map/ppermute | solution.py:217
  57.8 1.7 %copy-start.1 = (f32[1,9,256,256]{3,2,1,0:T(8,128)S(1)}, f32[1,9,256,256]{3,2,1,0:T(8,128)}, u32[]{:S(2)}) copy-start(f32[1,9,256,256]{3,2,1,0:T(8,128)} %param.10) | copy-start | bytes 7077892

commit v2 on v1

v2 whole, which is shorter than its diff:
```python
import functools
import math

import jax
import jax.numpy as jnp
import numpy as np
from jax import lax
from jax.experimental import pallas as pl
from jax.experimental.pallas import tpu as pltpu
from jax.sharding import PartitionSpec as P

LATS = 721
MIDDLE = (LATS - 1) / 2.0
NORM = float(np.mean(np.cos(math.pi * (np.arange(LATS) - MIDDLE) / (LATS - 1))))
F32 = jnp.float32
BF16 = jnp.bfloat16
NN = (((1,), (0,)), ((), ()))
NT = (((1,), (1,)), ((), ()))
VMEM_LIMIT = 30 << 20
STAGE_WEIGHT = 8
VMEM = pl.BlockSpec(memory_space=pltpu.VMEM)
HBM = pl.BlockSpec(memory_space=pltpu.HBM)


def params_of(**more):
    return pltpu.CompilerParams(vmem_limit_bytes=VMEM_LIMIT, **more)


def spread(ref, at, values, rows, cols):
    length = rows * cols
    column = lax.broadcasted_iota(jnp.int32, values.shape, 0) % cols
    zeros = jnp.zeros((cols, values.shape[1]), BF16)
    for b in range(3):
        if b == 0:
            moved = jnp.where(column == 0, 0.0, pltpu.roll(values, 1, 0))
        elif b == 2:
            moved = jnp.where(column == cols - 1, 0.0, pltpu.roll(values, length - 1, 0))
        else:
            moved = values
        ref[(*at, b, pl.ds(0, cols), slice(None))] = zeros
        ref[(*at, b, pl.ds(cols, length), slice(None))] = moved.astype(BF16)
        ref[(*at, b, pl.ds(cols + length, cols), slice(None))] = zeros


def stay(value):
    return pltpu.with_memory_space_constraint(value, pltpu.HBM)


def after(value, *others):
    return lax.optimization_barrier((value, *others))[0]


def product_cost(count, length, width, moved):
    return pl.CostEstimate(flops=2 * count * length * width * width, bytes_accessed=moved, transcendentals=0)


def gradient_in(grad, local, shifted, w_ref, rows, cols):
    length, width = grad.shape
    spread(shifted, (), local, rows, cols)
    total = None
    for a in range(3):
        for b in range(3):
            at = (2 - a) * cols
            term = lax.dot_general(
                shifted[2 - b, at : at + length, :], w_ref[3 * a + b], NT, preferred_element_type=F32
            )
            total = term if total is None else total + term
    return grad + (9.0 * width) ** (-0.5) * total


def prepare(crop_rows, inputs, cotangent, weights, rows, cols):
    micro, length, width = inputs.shape
    taps = weights.shape[0]
    scale = (9.0 * width) ** (-0.5)

    def kernel(crop_ref, x_ref, cot_ref, w_ref, wbf_ref, x_now, *refs):
        slopes, tops, refs = refs[:micro], refs[micro : 2 * micro], refs[2 * micro :]
        cot_now, crop_now, shifted, w_now, sems = refs
        load_x = pltpu.make_async_copy(x_ref, x_now, sems.at[0])
        load_cot = pltpu.make_async_copy(cot_ref, cot_now, sems.at[1])
        load_crop = pltpu.make_async_copy(crop_ref, crop_now, sems.at[2])
        loads = [pltpu.make_async_copy(w_ref.at[k], w_now.at[k], sems.at[3 + k]) for k in range(taps)]
        for load in (load_crop, load_x, *loads, load_cot):
            load.start()
        load_crop.wait()
        is_last = lax.axis_index("section") == lax.axis_size("section") - 1
        factors = []
        for m in range(micro):
            here = lax.broadcasted_iota(jnp.int32, (rows, 128), 0) + crop_now[0, m]
            factor = jnp.cos(math.pi * (here.astype(F32) - MIDDLE) / (LATS - 1)) / NORM
            factors.append(jnp.where(is_last, factor, 0.0))
        load_x.wait()
        for m in range(micro):
            spread(shifted, (m,), x_now[m].astype(F32), rows, cols)

        def product(m, k, total):
            a, b = divmod(k, 3)
            term = lax.dot_general(
                shifted[m, b, a * cols : a * cols + length, :], wbf_ref[k], NN, preferred_element_type=F32
            )
            return term if total is None else total + term

        total = None
        for k in range(taps):
            loads[k].wait()
            wbf_ref[k] = w_now[k].astype(BF16)
            total = product(0, k, total)
        for m in range(micro):
            if m:
                total = None
                for k in range(taps):
                    total = product(m, k, total)
            else:
                load_cot.wait()
            tangent = jnp.tanh(total * scale)
            slopes[m][...] = 1.0 - tangent * tangent
            for i in range(rows):
                line = jnp.broadcast_to(factors[m][i : i + 1], (cols, 128))
                line = jnp.concatenate([line] * (width // 128), axis=1)
                at = slice(i * cols, (i + 1) * cols)
                tops[m][at, :] = (cot_now[m, at, :].astype(F32) * line).astype(BF16)

    shapes = [jax.ShapeDtypeStruct(weights.shape, BF16), jax.ShapeDtypeStruct(inputs.shape, BF16)]
    shapes += [jax.ShapeDtypeStruct((length, width), F32)] * micro
    shapes += [jax.ShapeDtypeStruct((length, width), BF16)] * micro
    out = pl.pallas_call(
        kernel,
        out_shape=shapes,
        in_specs=[HBM] * 4,
        out_specs=[VMEM] * len(shapes),
        scratch_shapes=[
            pltpu.VMEM(inputs.shape, BF16),
            pltpu.SMEM(crop_rows.shape, jnp.int32),
            pltpu.VMEM((micro, 3, length + 2 * cols, width), BF16),
            pltpu.VMEM(weights.shape, F32),
            pltpu.SemaphoreType.DMA((3 + taps,)),
        ],
        compiler_params=params_of(),
        name="prepare",
    )(*[stay(one) for one in (crop_rows, inputs, cotangent, weights)])
    return out[0], out[1], out[2 : 2 + micro], out[2 + micro :]


def stage(arrived, slope, weights, rows, cols):
    taps, width, _ = weights.shape
    length = rows * cols
    count = len(arrived)

    def kernel(*refs):
        parts, (slope_ref, w_ref, out_ref, shifted) = refs[:count], refs[count:]
        grad = parts[0][...].astype(F32)
        for part in parts[1:]:
            grad += part[...].astype(F32)
        local = (grad * slope_ref[...]).astype(BF16).astype(F32)
        out_ref[...] = gradient_in(grad, local, shifted, w_ref, rows, cols).astype(BF16)

    return pl.pallas_call(
        kernel,
        out_shape=jax.ShapeDtypeStruct((length, width), BF16),
        in_specs=[VMEM] * (count + 2),
        out_specs=VMEM,
        scratch_shapes=[pltpu.VMEM((3, length + 2 * cols, width), BF16)],
        compiler_params=params_of(),
        cost_estimate=product_cost(STAGE_WEIGHT * taps, length, width, 2 * weights.size),
        name="stage",
    )(*arrived, slope, weights)


def turned_taps(inputs, rows, cols):
    blocks, length, width = inputs.shape

    def kernel(x_ref, out_ref, shifted):
        for n in range(blocks):
            spread(shifted, (), x_ref[n].astype(F32), rows, cols)
            for a in range(3):
                for b in range(3):
                    out_ref[n, 3 * a + b] = shifted[b, a * cols : a * cols + length, :].T

    return pl.pallas_call(
        kernel,
        out_shape=jax.ShapeDtypeStruct((blocks, 9, width, length), BF16),
        in_specs=[VMEM],
        out_specs=VMEM,
        scratch_shapes=[pltpu.VMEM((3, length + 2 * cols, width), BF16)],
        compiler_params=params_of(),
        name="turned_taps",
    )(inputs)


def outgoing(near, far, momentum, last, replicas):
    taps, width, _ = near.shape
    share = momentum.shape[1]

    def kernel(near_ref, far_ref, own_ref, out_ref, rest_ref, total):
        here = lax.axis_index("replica")
        own_rows = pl.ds(pl.multiple_of(here * share, share), share)
        other_rows = pl.ds(pl.multiple_of(jnp.bitwise_xor(here, last) * share, share), share)
        for k in range(taps):
            total[k % 2] = near_ref[k].astype(F32) + far_ref[k].astype(F32)
            mine = total[k % 2, own_rows, :]
            out_ref[k, :share] = (1.33 / replicas * mine + 0.567 * own_ref[k]).astype(BF16)
            out_ref[k, share:] = total[k % 2, other_rows, :].astype(BF16)
            rest_ref[k] = 0.9 * own_ref[k] + mine / replicas

    return pl.pallas_call(
        kernel,
        out_shape=(
            jax.ShapeDtypeStruct((taps, 2 * share, width), BF16),
            jax.ShapeDtypeStruct(momentum.shape, F32),
        ),
        in_specs=[VMEM] * 3,
        out_specs=[VMEM] * 2,
        scratch_shapes=[pltpu.VMEM((2, width, width), F32)],
        compiler_params=params_of(),
        name="outgoing",
    )(near, far, momentum)


def incoming(ours, theirs, rest, replicas):
    share = rest.shape[1]

    def kernel(ours_ref, theirs_ref, rest_ref, out_ref, momentum_ref):
        for k in range(rest.shape[0]):
            mine, there = ours_ref[k].astype(F32), theirs_ref[k].astype(F32)
            out_ref[k, :share] = (mine[:share] + 1.33 / replicas * there[share:]).astype(BF16)
            out_ref[k, share:] = (there[:share] + 1.33 / replicas * mine[share:]).astype(BF16)
            momentum_ref[k] = rest_ref[k] + there[share:] / replicas

    return pl.pallas_call(
        kernel,
        out_shape=(jax.ShapeDtypeStruct(ours.shape, BF16), jax.ShapeDtypeStruct(rest.shape, F32)),
        in_specs=[VMEM] * 3,
        out_specs=[VMEM] * 2,
        compiler_params=params_of(),
        name="incoming",
    )(ours, theirs, rest)


def contract(base, momentum_base, blocks, gains, final, pieces=(), last=0):
    taps, width, _ = base.shape
    share = momentum_base.shape[1]
    count = len(blocks)

    def kernel(base_ref, mom_ref, *refs):
        turned, local, refs = refs[:count], refs[count : 2 * count], refs[2 * count :]
        taken, refs = refs[: len(pieces)], refs[len(pieces) :]
        out_ref, mom_out_ref, total = refs[:3]
        if final:
            out_now, mom_now, sems = refs[3:]
        else:
            out_now, mom_now = out_ref, mom_out_ref
        here = lax.axis_index("replica")
        own = pl.multiple_of(here * share, share)
        copies = []
        for k in range(taps):
            acc = None
            for n in range(count):
                term = lax.dot_general(turned[n][blocks[n][1], k], local[n][...], NN, preferred_element_type=F32)
                acc = term if acc is None else acc + term
            total[k % 2] = acc
            out_now[k] = base_ref[k] + gains[0] * acc
            for (at, _), piece in zip(pieces, taken):
                for n in range(2):
                    where = jnp.bitwise_xor(here, at | n * last) * share
                    lines = pl.ds(pl.multiple_of(where, share), share)
                    out_now[k, lines, :] -= piece[k, n * share : (n + 1) * share].astype(F32)
            mom_now[k] = mom_ref[k] + gains[1] * total[k % 2, pl.ds(own, share), :]
            if final:
                copies.append(pltpu.make_async_copy(out_now.at[k], out_ref.at[k], sems.at[0, k]))
                copies.append(pltpu.make_async_copy(mom_now.at[k], mom_out_ref.at[k], sems.at[1, k]))
                copies[-2].start()
                copies[-1].start()
        for copy in copies:
            copy.wait()

    scratch = [pltpu.VMEM((2, width, width), F32)]
    if final:
        scratch += [
            pltpu.VMEM(base.shape, F32),
            pltpu.VMEM(momentum_base.shape, F32),
            pltpu.SemaphoreType.DMA((2, taps)),
        ]
    return pl.pallas_call(
        kernel,
        out_shape=(
            jax.ShapeDtypeStruct(base.shape, F32),
            jax.ShapeDtypeStruct(momentum_base.shape, F32),
        ),
        in_specs=[VMEM] * (2 + 2 * count + len(pieces)),
        out_specs=[HBM if final else VMEM] * 2,
        scratch_shapes=scratch,
        compiler_params=params_of(),
        name="contract",
    )(base, momentum_base, *[one[0] for one in blocks], *[one[2] for one in blocks], *[one[1] for one in pieces])


def per_device(section_inputs, cotangent, crop_rows, drift, params, momentum):
    sections = lax.axis_size("section")
    here, replicas = lax.axis_index("replica"), lax.axis_size("replica")
    micro, rows, cols, width = section_inputs.shape[2:]
    length = rows * cols
    share = width // replicas
    taps = params.shape[1]
    scale = (9.0 * width) ** (-0.5)
    bits = [1 << n for n in reversed(range((replicas - 1).bit_length()))]
    x = section_inputs.reshape(micro, length, width)
    cot = cotangent.reshape(micro, length, width)

    def swap(value, bit):
        return lax.ppermute(value, "replica", [(i, i ^ bit) for i in range(replicas)])

    def spread_out(value, through):
        held = [(0, value)]
        for bit in through:
            held += [(at | bit, swap(one, bit)) for at, one in held]
        return held

    def hop(value, step):
        return lax.ppermute(value, "section", [(sections - 1 - step, sections - 2 - step)])

    def slice_of(value, relative):
        at = jnp.bitwise_xor(here, relative) * share
        return lax.dynamic_slice_in_dim(value, at, share, 1).astype(F32)

    low, last = bits[1:], bits[0]
    own, near = momentum[0], drift[0, 0]
    far = swap(near, 1) if low else jnp.zeros_like(near)
    weights, x_near, slopes, tops = prepare(crop_rows, x, cot, params[0], rows, cols)
    arrived = [[top] for top in tops]
    for step in range(sections - 1):
        leaving = [stage(arrived[m], slopes[m], weights, rows, cols) for m in range(micro)]
        for m in range(micro):
            arrived[m].append(hop(leaving[m], step))
        if step == 0:
            far, x_sent = after(far, *leaving), after(x_near, *leaving)
            if len(low) < 2:
                ours, rest = outgoing(near, far, own, last, replicas)
            else:
                live = {j: slice_of(near, j) + slice_of(far, j) for j in range(0, replicas, 2)}
                for bit in reversed(low[:-1]):
                    got = {j: swap(v.astype(BF16), bit) for j, v in live.items() if j & bit}
                    live = {j: v + got[j | bit].astype(F32) for j, v in live.items() if not j & bit}
                ours = jnp.concatenate([1.33 / replicas * live[0] + 0.567 * own, live[last]], axis=1).astype(BF16)
                rest = 0.9 * own + live[0] / replicas
        arrived[0][-1] = after(arrived[0][-1], *leaving[1:], *([ours] if step == 0 else []))
    pair, momentum_base = incoming(ours, swap(ours, last), rest, replicas)
    pieces = spread_out(pair, low)
    base = params[0]

    turned = {at: turned_taps(one, rows, cols) for at, one in spread_out(x_sent, bits)}

    gain = 0.5 * scale / replicas
    gains = (-1.33 * gain, gain)
    blocks = []
    arrived[0][-1] = after(arrived[0][-1], *turned.values())
    for m in range(micro):
        local = (sum(one.astype(F32) for one in arrived[m]) * slopes[m]).astype(BF16)
        if m < micro - 1:
            blocks += [(turned[at], m, one) for at, one in spread_out(local, bits)]
            continue
        for at, one in spread_out(local, low):
            blocks.append((turned[at], m, one))
        for at in range(0, len(blocks), 6):
            base, momentum_base = contract(base, momentum_base, blocks[at : at + 6], gains, False, pieces, last)
            pieces = ()
        crossed = after(swap(local, last), base)
        blocks = [(turned[at | last], m, one) for at, one in spread_out(crossed, low)]
    for at in range(0, len(blocks), 2):
        base, momentum_base = contract(base, momentum_base, blocks[at : at + 2], gains, at + 2 >= len(blocks))
    return (base[None], momentum_base[None])


def solution(mesh):
    placed = (
        P(("groups", "replica"), "section", None, None, None, None),
        P(("groups", "replica"), None, None, None, None),
        P(("groups", "replica"), None),
        P(("groups", "replica"), "section", None, None, None),
        P(("groups", "section"), None, None, None),
        P(("groups", "section"), None, "replica", None),
    )
    return jax.shard_map(
        per_device,
        mesh=mesh,
        in_specs=placed,
        out_specs=(
            P(("groups", "section"), None, None, None),
            P(("groups", "section"), None, "replica", None),
        ),
        check_vma=False,
    )
```

time: 68.9 us -> 45.9 us (0.67)
  the two profiles are of different devices: /device:TPU:11 before, /device:TPU:27 now
where the time goes in v2:
time: 45.9 us; the launch traced here: 45.7 us
  waiting for transfers between devices  15.8 us (34%)
  starting transfers between devices  14.8 us (32%)
  Pallas kernels  14 us (31%)
  between operations  0.88 us (2%)
    ppermute x12, waiting for transfers between devices, swap(): lax.ppermute(value, 'replica', [(i, i ^ bit) for i in range(replicas)])  15.8 us
    ppermute x12, starting transfers between devices, swap(): lax.ppermute(value, 'replica', [(i, i ^ bit) for i in range(replicas)])  8.64 us
    ppermute x6, starting transfers between devices, hop(): lax.ppermute(value, 'section', [(sections - 1 - step, sections - 2 - step)])  6.18 us
    pallas_call x2, Pallas kernels, contract(): pl.pallas_call(kernel, out_shape=(jax.ShapeDtypeStruct(base.shape, F32),...  4.51 us
    pallas_call x6, Pallas kernels, stage(): pl.pallas_call(kernel, out_shape=jax.ShapeDtypeStruct((length, width), BF...  3.1 us
    pallas_call x1, Pallas kernels, prepare(): pl.pallas_call(kernel, out_shape=shapes, in_specs=[HBM] * 4, out_specs=[V...  3.02 us
    pallas_call x4, Pallas kernels, turned_taps(): pl.pallas_call(kernel, out_shape=jax.ShapeDtypeStruct((blocks, 9, width,...  2.69 us
  transfers between devices with their start and end apart: 18, of which 6 were waited for; matrix products, arithmetic and copies ran while one was open for 0% of the time, Pallas kernels for 26%

profile of v2, /device:TPU:27, one launch (start us, length us, event | category | flops | bytes accessed | tf_op | source)
XLA Modules:
  0.0 45.7 jit_solution(4059700909991052164)
XLA Ops:
  0.6 0.7 %collective-permute-start = (bf16[9,256,256]{2,1,0:T(8,128)(2,1)}, bf16[9,256,256]{2,1,0:T(8,128)(2,1)S(1)}, u32[]{:S(2)}, u32[]{:S(2)}) collective-permute-start(bf16[9,256,256]{2,1,0:T(8,128)(2,1)} %bitcast.9), channel_id=1, source_target_pairs={{0,1},{1,0},{2,3},{3,2},{4,5},{5,4},{6,7},{7,6},{8,9},{9,8},{10,11... | collective-permute-start | bytes 3538952 | tf_op jit(solution)/shard_map/ppermute | solution.py:310
  1.4 3.0 %prepare.1 = (bf16[9,256,256]{2,1,0:T(8,128)(2,1)S(1)}, bf16[2,256,256]{2,1,0:T(8,128)(2,1)S(1)}, f32[256,256]{1,0:T(8,128)S(1)}, f32[256,256]{1,0:T(8,128)S(1)}...) custom-call(s32[1,2]{1,0:T(1,128)} %crop_ref.1, bf16[2,256,256]{2,1,0:T(8,128)(2,1)} %bitcast.12, ...), custom_call_target="tpu_custom_call" | custom-call | tf_op jit(solution)/shard_map/prepare/pallas_call | solution.py:126
  4.4 0.5 %stage.6 = bf16[256,256]{1,0:T(8,128)(2,1)S(1)} custom-call(bf16[256,256]{1,0:T(8,128)(2,1)S(1)} %get-tuple-element.23.refs_0_, f32[256,256]{1,0:T(8,128)S(1)} %get-tuple-element.24.refs_1_.refs_2_.refs_3_, bf16[9,256,256]{2,1,0:T(8,128)(2,1)S(1)} %get-tuple-element.25.refs_2_.refs_3_.refs_4_), custom_call_target="tpu_custom_call" | custom-call | flops 2415919104 | bytes 1179648 | tf_op jit(solution)/shard_map/stage/pallas_call | solution.py:157
  4.9 2.1 %collective-permute-start.5 = (bf16[256,256]{1,0:T(8,128)(2,1)S(1)}, bf16[256,256]{1,0:T(8,128)(2,1)S(1)}, u32[]{:S(2)}, u32[]{:S(2)}) collective-permute-start(bf16[256,256]{1,0:T(8,128)(2,1)S(1)} %stage.6), channel_id=1, source_target_pairs={{12,8},{13,9},{14,10},{15,11},{28,24},{29,25},{30,26},{31,27}} | collective-permute-start | bytes 393224 | tf_op jit(solution)/shard_map/ppermute | solution.py:319
  7.0 0.5 %stage.7 = bf16[256,256]{1,0:T(8,128)(2,1)S(1)} custom-call(bf16[256,256]{1,0:T(8,128)(2,1)S(1)} %get-tuple-element.26.refs_0_, f32[256,256]{1,0:T(8,128)S(1)} %get-tuple-element.27.refs_1_.refs_2_.refs_3_, bf16[9,256,256]{2,1,0:T(8,128)(2,1)S(1)} %get-tuple-element.25.refs_2_.refs_3_.refs_4_), custom_call_target="tpu_custom_call" | custom-call | flops 2415919104 | bytes 1179648 | tf_op jit(solution)/shard_map/stage/pallas_call | solution.py:157
  7.5 0.0 copy-start.1
  7.5 0.0 copy-start.2
  7.6 1.4 %collective-permute-start.7 = (bf16[256,256]{1,0:T(8,128)(2,1)S(1)}, bf16[256,256]{1,0:T(8,128)(2,1)S(1)}, u32[]{:S(2)}, u32[]{:S(2)}) collective-permute-start(bf16[256,256]{1,0:T(8,128)(2,1)S(1)} %stage.7), channel_id=1, source_target_pairs={{12,8},{13,9},{14,10},{15,11},{28,24},{29,25},{30,26},{31,27}} | collective-permute-start | bytes 393224 | tf_op jit(solution)/shard_map/ppermute | solution.py:319
  9.0 0.3 collective-permute-start.2
  9.3 0.6 %collective-permute-start.3 = (bf16[2,256,256]{2,1,0:T(8,128)(2,1)S(1)}, bf16[2,256,256]{2,1,0:T(8,128)(2,1)S(1)}, u32[]{:S(2)}, u32[]{:S(2)}) collective-permute-start(bf16[2,256,256]{2,1,0:T(8,128)(2,1)S(1)} %get-tuple-element.33.x_ref), channel_id=1, source_target_pairs={{0,1},{1,0},{2,3},{3,2},{4,5},{5,4},{6,7},{7,6},{8,9},{9,8},{10,11... | collective-permute-start | bytes 786440 | tf_op jit(solution)/shard_map/ppermute | solution.py:310
  9.9 0.7 %turned_taps.4.refs_0_.refs_4_ = bf16[2,9,256,256]{3,2,1,0:T(8,128)(2,1)S(1)} custom-call(bf16[2,256,256]{2,1,0:T(8,128)(2,1)S(1)} %get-tuple-element.33.x_ref), custom_call_target="tpu_custom_call" | custom-call | tf_op jit(solution)/shard_map/turned_taps/pallas_call | solution.py:179
  10.6 0.5 %outgoing.1 = (bf16[9,128,256]{2,1,0:T(8,128)(2,1)S(1)}, f32[9,64,256]{2,1,0:T(8,128)S(1)}) custom-call(bf16[9,256,256]{2,1,0:T(8,128)(2,1)S(1)} %bitcast.10, bf16[9,256,256]{2,1,0:T(8,128)(2,1)S(1)} %collective-permute-done.far_ref, f32[9,64,256]{2,1,0:T(8,128)S(1)} %bitcast.11), custom_call_target="tpu_custom_call" | custom-call | tf_op jit(solution)/shard_map/outgoing/pallas_call | solution.py:205
  11.1 1.3 %collective-permute-start.1 = (bf16[9,128,256]{2,1,0:T(8,128)(2,1)S(1)}, bf16[9,128,256]{2,1,0:T(8,128)(2,1)S(1)}, u32[]{:S(2)}, u32[]{:S(2)}) collective-permute-start(bf16[9,128,256]{2,1,0:T(8,128)(2,1)S(1)} %get-tuple-element.29.ours_ref), channel_id=1, source_target_pairs={{0,2},{1,3},{2,0},{3,1},{4,6},{5,7},{6,4},{7,5},{8,10},{9,11},{10,... | collective-permute-start | bytes 1769480 | tf_op jit(solution)/shard_map/ppermute | solution.py:310
  12.4 0.0 collective-permute-done.5.refs_1_
  12.4 0.5 %stage.8 = bf16[256,256]{1,0:T(8,128)(2,1)S(1)} custom-call(bf16[256,256]{1,0:T(8,128)(2,1)S(1)} %get-tuple-element.23.refs_0_, bf16[256,256]{1,0:T(8,128)(2,1)S(1)} %collective-permute-done.5.refs_1_, f32[256,256]{1,0:T(8,128)S(1)} %get-tuple-element.24.refs_1_.refs_2_.refs_3_, bf16[9,256,256]{2,1,0:T(8,128)(2,1)S(1)} %get-tuple-element.25.refs_2_.refs_3_.refs_4_), custom_call_target="tpu_custom_call" | custom-call | flops 2415919104 | bytes 1179648 | tf_op jit(solution)/shard_map/stage/pallas_call | solution.py:157
  12.9 0.7 %collective-permute-start.6 = (bf16[256,256]{1,0:T(8,128)(2,1)S(1)}, bf16[256,256]{1,0:T(8,128)(2,1)S(1)}, u32[]{:S(2)}, u32[]{:S(2)}) collective-permute-start(bf16[256,256]{1,0:T(8,128)(2,1)S(1)} %stage.8), channel_id=1, source_target_pairs={{8,4},{9,5},{10,6},{11,7},{24,20},{25,21},{26,22},{27,23}} | collective-permute-start | bytes 393224 | tf_op jit(solution)/shard_map/ppermute | solution.py:319
  13.6 0.0 collective-permute-done.7.refs_1_
  13.6 0.5 %stage.9 = bf16[256,256]{1,0:T(8,128)(2,1)S(1)} custom-call(bf16[256,256]{1,0:T(8,128)(2,1)S(1)} %get-tuple-element.26.refs_0_, bf16[256,256]{1,0:T(8,128)(2,1)S(1)} %collective-permute-done.7.refs_1_, f32[256,256]{1,0:T(8,128)S(1)} %get-tuple-element.27.refs_1_.refs_2_.refs_3_, bf16[9,256,256]{2,1,0:T(8,128)(2,1)S(1)} %get-tuple-element.25.refs_2_.refs_3_.refs_4_), custom_call_target="tpu_custom_call" | custom-call | flops 2415919104 | bytes 1179648 | tf_op jit(solution)/shard_map/stage/pallas_call | solution.py:157
  14.1 0.7 %collective-permute-start.9 = (bf16[256,256]{1,0:T(8,128)(2,1)S(1)}, bf16[256,256]{1,0:T(8,128)(2,1)S(1)}, u32[]{:S(2)}, u32[]{:S(2)}) collective-permute-start(bf16[256,256]{1,0:T(8,128)(2,1)S(1)} %stage.9), channel_id=1, source_target_pairs={{8,4},{9,5},{10,6},{11,7},{24,20},{25,21},{26,22},{27,23}} | collective-permute-start | bytes 393224 | tf_op jit(solution)/shard_map/ppermute | solution.py:319
  14.8 1.9 %collective-permute-done.2.x_ref = bf16[2,256,256]{2,1,0:T(8,128)(2,1)S(1)} collective-permute-done((bf16[2,256,256]{2,1,0:T(8,128)(2,1)S(1)}, bf16[2,256,256]{2,1,0:T(8,128)(2,1)S(1)}, u32[]{:S(2)}, u32[]{:S(2)}) %collective-permute-start.2) | collective-permute-done | bytes 262176 | tf_op jit(solution)/shard_map/ppermute | solution.py:310
  16.7 1.8 %collective-permute-start.4 = (bf16[2,256,256]{2,1,0:T(8,128)(2,1)S(1)}, bf16[2,256,256]{2,1,0:T(8,128)(2,1)S(1)}, u32[]{:S(2)}, u32[]{:S(2)}) collective-permute-start(bf16[2,256,256]{2,1,0:T(8,128)(2,1)S(1)} %collective-permute-done.2.x_ref), channel_id=1, source_target_pairs={{0,1},{1,0},{2,3},{3,2},{4,5},{5,4},{6,7},{7,6},{8,9},{9,8},{10,11... | collective-permute-start | bytes 786440 | tf_op jit(solution)/shard_map/ppermute | solution.py:310
  18.5 0.0 collective-permute-done.6.refs_2_
  18.5 0.5 %stage.10 = bf16[256,256]{1,0:T(8,128)(2,1)S(1)} custom-call(bf16[256,256]{1,0:T(8,128)(2,1)S(1)} %get-tuple-element.23.refs_0_, bf16[256,256]{1,0:T(8,128)(2,1)S(1)} %collective-permute-done.5.refs_1_, bf16[256,256]{1,0:T(8,128)(2,1)S(1)} %collective-permute-done.6.refs_2_, f32[256,256]{1,0:T(8,128)S(1)} %get-tuple-element.24.refs_1_.refs_2_.refs_3_, ...), custom_call_target="tpu_custom_call" | custom-call | flops 2415919104 | bytes 1179648 | tf_op jit(solution)/shard_map/stage/pallas_call | solution.py:157
  19.0 0.7 %collective-permute-start.8 = (bf16[256,256]{1,0:T(8,128)(2,1)S(1)}, bf16[256,256]{1,0:T(8,128)(2,1)S(1)}, u32[]{:S(2)}, u32[]{:S(2)}) collective-permute-start(bf16[256,256]{1,0:T(8,128)(2,1)S(1)} %stage.10), channel_id=1, source_target_pairs={{4,0},{5,1},{6,2},{7,3},{20,16},{21,17},{22,18},{23,19}} | collective-permute-start | bytes 393224 | tf_op jit(solution)/shard_map/ppermute | solution.py:319
  19.7 0.0 collective-permute-done.9.refs_2_
  19.7 0.5 %stage.11 = bf16[256,256]{1,0:T(8,128)(2,1)S(1)} custom-call(bf16[256,256]{1,0:T(8,128)(2,1)S(1)} %get-tuple-element.26.refs_0_, bf16[256,256]{1,0:T(8,128)(2,1)S(1)} %collective-permute-done.7.refs_1_, bf16[256,256]{1,0:T(8,128)(2,1)S(1)} %collective-permute-done.9.refs_2_, f32[256,256]{1,0:T(8,128)S(1)} %get-tuple-element.27.refs_1_.refs_2_.refs_3_, ...), custom_call_target="tpu_custom_call" | custom-call | flops 2415919104 | bytes 1179648 | tf_op jit(solution)/shard_map/stage/pallas_call | solution.py:157
  20.2 0.7 %collective-permute-start.13 = (bf16[256,256]{1,0:T(8,128)(2,1)S(1)}, bf16[256,256]{1,0:T(8,128)(2,1)S(1)}, u32[]{:S(2)}, u32[]{:S(2)}) collective-permute-start(bf16[256,256]{1,0:T(8,128)(2,1)S(1)} %stage.11), channel_id=1, source_target_pairs={{4,0},{5,1},{6,2},{7,3},{20,16},{21,17},{22,18},{23,19}} | collective-permute-start | bytes 393224 | tf_op jit(solution)/shard_map/ppermute | solution.py:319
  20.9 0.7 %turned_taps.5.refs_1_.refs_0_ = bf16[2,9,256,256]{3,2,1,0:T(8,128)(2,1)S(1)} custom-call(bf16[2,256,256]{2,1,0:T(8,128)(2,1)S(1)} %collective-permute-done.2.x_ref), custom_call_target="tpu_custom_call" | custom-call | tf_op jit(solution)/shard_map/turned_taps/pallas_call | solution.py:179
  21.6 0.7 %turned_taps.6.refs_2_.refs_5_ = bf16[2,9,256,256]{3,2,1,0:T(8,128)(2,1)S(1)} custom-call(bf16[2,256,256]{2,1,0:T(8,128)(2,1)S(1)} %collective-permute-done.3.x_ref), custom_call_target="tpu_custom_call" | custom-call | tf_op jit(solution)/shard_map/turned_taps/pallas_call | solution.py:179
  22.3 0.7 %turned_taps.7.refs_3_.refs_1_ = bf16[2,9,256,256]{3,2,1,0:T(8,128)(2,1)S(1)} custom-call(bf16[2,256,256]{2,1,0:T(8,128)(2,1)S(1)} %collective-permute-done.4.x_ref), custom_call_target="tpu_custom_call" | custom-call | tf_op jit(solution)/shard_map/turned_taps/pallas_call | solution.py:179
  23.0 0.0 copy-start
  23.0 6.3 %collective-permute-done.1.theirs_ref = bf16[9,128,256]{2,1,0:T(8,128)(2,1)S(1)} collective-permute-done((bf16[9,128,256]{2,1,0:T(8,128)(2,1)S(1)}, bf16[9,128,256]{2,1,0:T(8,128)(2,1)S(1)}, u32[]{:S(2)}, u32[]{:S(2)}) %collective-permute-start.1) | collective-permute-done | bytes 589856 | tf_op jit(solution)/shard_map/ppermute | solution.py:310
  29.3 0.2 incoming.1
  29.5 1.2 %collective-permute-start.15 = (bf16[9,128,256]{2,1,0:T(8,128)(2,1)S(1)}, bf16[9,128,256]{2,1,0:T(8,128)(2,1)S(1)}, u32[]{:S(2)}, u32[]{:S(2)}) collective-permute-start(bf16[9,128,256]{2,1,0:T(8,128)(2,1)S(1)} %get-tuple-element.38.refs_12_), channel_id=1, source_target_pairs={{0,1},{1,0},{2,3},{3,2},{4,5},{5,4},{6,7},{7,6},{8,9},{9,8},{10,11... | collective-permute-start | bytes 1769480 | tf_op jit(solution)/shard_map/ppermute | solution.py:310
  30.7 0.1 multiply_convert_fusion.1.refs_6_
  30.8 0.3 collective-permute-start.10
  31.1 0.1 multiply_convert_fusion.refs_10_
  31.2 0.4 collective-permute-start.14
  31.6 0.2 collective-permute-start.11
  31.8 4.2 %collective-permute-done.10.refs_7_ = bf16[256,256]{1,0:T(8,128)(2,1)S(1)} collective-permute-done((bf16[256,256]{1,0:T(8,128)(2,1)S(1)}, bf16[256,256]{1,0:T(8,128)(2,1)S(1)}, u32[]{:S(2)}, u32[]{:S(2)}) %collective-permute-start.10) | collective-permute-done | bytes 131104 | tf_op jit(solution)/shard_map/ppermute | solution.py:310
  36.0 0.8 %collective-permute-start.12 = (bf16[256,256]{1,0:T(8,128)(2,1)S(1)}, bf16[256,256]{1,0:T(8,128)(2,1)S(1)}, u32[]{:S(2)}, u32[]{:S(2)}) collective-permute-start(bf16[256,256]{1,0:T(8,128)(2,1)S(1)} %collective-permute-done.10.refs_7_), channel_id=1, source_target_pairs={{0,1},{1,0},{2,3},{3,2},{4,5},{5,4},{6,7},{7,6},{8,9},{9,8},{10,11... | collective-permute-start | bytes 393224 | tf_op jit(solution)/shard_map/ppermute | solution.py:310
  36.8 0.3 collective-permute-start.16
  37.0 0.7 %collective-permute-done.12.refs_9_ = bf16[256,256]{1,0:T(8,128)(2,1)S(1)} collective-permute-done((bf16[256,256]{1,0:T(8,128)(2,1)S(1)}, bf16[256,256]{1,0:T(8,128)(2,1)S(1)}, u32[]{:S(2)}, u32[]{:S(2)}) %collective-permute-start.12) | collective-permute-done | bytes 131104 | tf_op jit(solution)/shard_map/ppermute | solution.py:310
  37.8 2.5 %contract.2 = (f32[9,256,256]{2,1,0:T(8,128)S(1)}, f32[9,64,256]{2,1,0:T(8,128)S(1)}) custom-call(f32[9,256,256]{2,1,0:T(8,128)S(1)} %bitcast.8, f32[9,64,256]{2,1,0:T(8,128)S(1)} %get-tuple-element.31.mom_ref, bf16[2,9,256,256]{3,2,1,0:T(8,128)(2,1)S(1)} %turned_taps.4.refs_0_.refs_4_, bf16[2,9,256,256]{3,2,1,0:T(8,128)(2,1)S(1)} %turned_taps.5.refs_1_.refs_0_, ...), custom_call_target="tpu_custom_call" | custom-call | tf_op jit(solution)/shard_map/contract/pallas_call | solution.py:283
  40.2 1.7 %collective-permute-done.16.refs_2_ = bf16[256,256]{1,0:T(8,128)(2,1)S(1)} collective-permute-done((bf16[256,256]{1,0:T(8,128)(2,1)S(1)}, bf16[256,256]{1,0:T(8,128)(2,1)S(1)}, u32[]{:S(2)}, u32[]{:S(2)}) %collective-permute-start.16) | collective-permute-done | bytes 131104 | tf_op jit(solution)/shard_map/ppermute | solution.py:310
  41.9 0.8 %collective-permute-start.17 = (bf16[256,256]{1,0:T(8,128)(2,1)S(1)}, bf16[256,256]{1,0:T(8,128)(2,1)S(1)}, u32[]{:S(2)}, u32[]{:S(2)}) collective-permute-start(bf16[256,256]{1,0:T(8,128)(2,1)S(1)} %collective-permute-done.16.refs_2_), channel_id=1, source_target_pairs={{0,1},{1,0},{2,3},{3,2},{4,5},{5,4},{6,7},{7,6},{8,9},{9,8},{10,11... | collective-permute-start | bytes 393224 | tf_op jit(solution)/shard_map/ppermute | solution.py:310
  42.7 1.0 %collective-permute-done.17.refs_3_ = bf16[256,256]{1,0:T(8,128)(2,1)S(1)} collective-permute-done((bf16[256,256]{1,0:T(8,128)(2,1)S(1)}, bf16[256,256]{1,0:T(8,128)(2,1)S(1)}, u32[]{:S(2)}, u32[]{:S(2)}) %collective-permute-start.17) | collective-permute-done | bytes 131104 | tf_op jit(solution)/shard_map/ppermute | solution.py:310
  43.7 2.0 %contract.3 = (f32[9,256,256]{2,1,0:T(8,128)}, f32[9,64,256]{2,1,0:T(8,128)}) custom-call(f32[9,256,256]{2,1,0:T(8,128)S(1)} %get-tuple-element.39.base_ref, f32[9,64,256]{2,1,0:T(8,128)S(1)} %get-tuple-element.40.mom_ref, bf16[2,9,256,256]{3,2,1,0:T(8,128)(2,1)S(1)} %turned_taps.5.refs_1_.refs_0_, bf16[2,9,256,256]{3,2,1,0:T(8,128)(2,1)S(1)} %turned_taps.7.refs_3_.refs_1_, ...), custom_call_target="tpu_custom_call" | custom-call | tf_op jit(solution)/shard_map/contract/pallas_call | solution.py:283
  (11 shorter events, 0.0 us)
Async XLA Ops:
  0.6 9.9 %collective-permute-start = (bf16[9,256,256]{2,1,0:T(8,128)(2,1)}, bf16[9,256,256]{2,1,0:T(8,128)(2,1)S(1)}, u32[]{:S(2)}, u32[]{:S(2)}) collective-permute-start(bf16[9,256,256]{2,1,0:T(8,128)(2,1)} %bitcast.9), channel_id=1, source_target_pairs={{0,1},{1,0},{2,3},{3,2},{4,5},{5,4},{6,7},{7,6},{8,9},{9,8},{10,11... | collective-permute-start | bytes 3538952 | tf_op jit(solution)/shard_map/ppermute | solution.py:310
  4.9 7.5 %collective-permute-start.5 = (bf16[256,256]{1,0:T(8,128)(2,1)S(1)}, bf16[256,256]{1,0:T(8,128)(2,1)S(1)}, u32[]{:S(2)}, u32[]{:S(2)}) collective-permute-start(bf16[256,256]{1,0:T(8,128)(2,1)S(1)} %stage.6), channel_id=1, source_target_pairs={{12,8},{13,9},{14,10},{15,11},{28,24},{29,25},{30,26},{31,27}} | collective-permute-start | bytes 393224 | tf_op jit(solution)/shard_map/ppermute | solution.py:319
  7.5 3.0 %copy-start.1 = (bf16[1,1,9,256,256]{4,3,2,1,0:T(8,128)(2,1)S(1)}, bf16[1,1,9,256,256]{4,3,2,1,0:T(8,128)(2,1)}, u32[]{:S(2)}) copy-start(bf16[1,1,9,256,256]{4,3,2,1,0:T(8,128)(2,1)} %param.9) | copy-start | bytes 3538948
  7.5 3.0 %copy-start.2 = (f32[1,9,64,256]{3,2,1,0:T(8,128)S(1)}, f32[1,9,64,256]{3,2,1,0:T(8,128)}, u32[]{:S(2)}) copy-start(f32[1,9,64,256]{3,2,1,0:T(8,128)} %param.11) | copy-start | bytes 1769476
  7.6 6.0 %collective-permute-start.7 = (bf16[256,256]{1,0:T(8,128)(2,1)S(1)}, bf16[256,256]{1,0:T(8,128)(2,1)S(1)}, u32[]{:S(2)}, u32[]{:S(2)}) collective-permute-start(bf16[256,256]{1,0:T(8,128)(2,1)S(1)} %stage.7), channel_id=1, source_target_pairs={{12,8},{13,9},{14,10},{15,11},{28,24},{29,25},{30,26},{31,27}} | collective-permute-start | bytes 393224 | tf_op jit(solution)/shard_map/ppermute | solution.py:319
  9.0 7.7 %collective-permute-start.2 = (bf16[2,256,256]{2,1,0:T(8,128)(2,1)S(1)}, bf16[2,256,256]{2,1,0:T(8,128)(2,1)S(1)}, u32[]{:S(2)}, u32[]{:S(2)}) collective-permute-start(bf16[2,256,256]{2,1,0:T(8,128)(2,1)S(1)} %get-tuple-element.33.x_ref), channel_id=1, source_target_pairs={{0,2},{1,3},{2,0},{3,1},{4,6},{5,7},{6,4},{7,5},{8,10},{9,11},{10,... | collective-permute-start | bytes 786440 | tf_op jit(solution)/shard_map/ppermute | solution.py:310
  9.3 12.3 %collective-permute-start.3 = (bf16[2,256,256]{2,1,0:T(8,128)(2,1)S(1)}, bf16[2,256,256]{2,1,0:T(8,128)(2,1)S(1)}, u32[]{:S(2)}, u32[]{:S(2)}) collective-permute-start(bf16[2,256,256]{2,1,0:T(8,128)(2,1)S(1)} %get-tuple-element.33.x_ref), channel_id=1, source_target_pairs={{0,1},{1,0},{2,3},{3,2},{4,5},{5,4},{6,7},{7,6},{8,9},{9,8},{10,11... | collective-permute-start | bytes 786440 | tf_op jit(solution)/shard_map/ppermute | solution.py:310
  11.1 18.2 %collective-permute-start.1 = (bf16[9,128,256]{2,1,0:T(8,128)(2,1)S(1)}, bf16[9,128,256]{2,1,0:T(8,128)(2,1)S(1)}, u32[]{:S(2)}, u32[]{:S(2)}) collective-permute-start(bf16[9,128,256]{2,1,0:T(8,128)(2,1)S(1)} %get-tuple-element.29.ours_ref), channel_id=1, source_target_pairs={{0,2},{1,3},{2,0},{3,1},{4,6},{5,7},{6,4},{7,5},{8,10},{9,11},{10,... | collective-permute-start | bytes 1769480 | tf_op jit(solution)/shard_map/ppermute | solution.py:310
  12.9 5.6 %collective-permute-start.6 = (bf16[256,256]{1,0:T(8,128)(2,1)S(1)}, bf16[256,256]{1,0:T(8,128)(2,1)S(1)}, u32[]{:S(2)}, u32[]{:S(2)}) collective-permute-start(bf16[256,256]{1,0:T(8,128)(2,1)S(1)} %stage.8), channel_id=1, source_target_pairs={{8,4},{9,5},{10,6},{11,7},{24,20},{25,21},{26,22},{27,23}} | collective-permute-start | bytes 393224 | tf_op jit(solution)/shard_map/ppermute | solution.py:319
  14.1 5.6 %collective-permute-start.9 = (bf16[256,256]{1,0:T(8,128)(2,1)S(1)}, bf16[256,256]{1,0:T(8,128)(2,1)S(1)}, u32[]{:S(2)}, u32[]{:S(2)}) collective-permute-start(bf16[256,256]{1,0:T(8,128)(2,1)S(1)} %stage.9), channel_id=1, source_target_pairs={{8,4},{9,5},{10,6},{11,7},{24,20},{25,21},{26,22},{27,23}} | collective-permute-start | bytes 393224 | tf_op jit(solution)/shard_map/ppermute | solution.py:319
  16.7 5.6 %collective-permute-start.4 = (bf16[2,256,256]{2,1,0:T(8,128)(2,1)S(1)}, bf16[2,256,256]{2,1,0:T(8,128)(2,1)S(1)}, u32[]{:S(2)}, u32[]{:S(2)}) collective-permute-start(bf16[2,256,256]{2,1,0:T(8,128)(2,1)S(1)} %collective-permute-done.2.x_ref), channel_id=1, source_target_pairs={{0,1},{1,0},{2,3},{3,2},{4,5},{5,4},{6,7},{7,6},{8,9},{9,8},{10,11... | collective-permute-start | bytes 786440 | tf_op jit(solution)/shard_map/ppermute | solution.py:310
  19.0 4.0 %collective-permute-start.8 = (bf16[256,256]{1,0:T(8,128)(2,1)S(1)}, bf16[256,256]{1,0:T(8,128)(2,1)S(1)}, u32[]{:S(2)}, u32[]{:S(2)}) collective-permute-start(bf16[256,256]{1,0:T(8,128)(2,1)S(1)} %stage.10), channel_id=1, source_target_pairs={{4,0},{5,1},{6,2},{7,3},{20,16},{21,17},{22,18},{23,19}} | collective-permute-start | bytes 393224 | tf_op jit(solution)/shard_map/ppermute | solution.py:319
  20.2 10.9 %collective-permute-start.13 = (bf16[256,256]{1,0:T(8,128)(2,1)S(1)}, bf16[256,256]{1,0:T(8,128)(2,1)S(1)}, u32[]{:S(2)}, u32[]{:S(2)}) collective-permute-start(bf16[256,256]{1,0:T(8,128)(2,1)S(1)} %stage.11), channel_id=1, source_target_pairs={{4,0},{5,1},{6,2},{7,3},{20,16},{21,17},{22,18},{23,19}} | collective-permute-start | bytes 393224 | tf_op jit(solution)/shard_map/ppermute | solution.py:319
  23.0 14.8 %copy-start = (f32[1,9,256,256]{3,2,1,0:T(8,128)S(1)}, f32[1,9,256,256]{3,2,1,0:T(8,128)}, u32[]{:S(2)}) copy-start(f32[1,9,256,256]{3,2,1,0:T(8,128)} %param.10) | copy-start | bytes 7077892
  29.5 8.2 %collective-permute-start.15 = (bf16[9,128,256]{2,1,0:T(8,128)(2,1)S(1)}, bf16[9,128,256]{2,1,0:T(8,128)(2,1)S(1)}, u32[]{:S(2)}, u32[]{:S(2)}) collective-permute-start(bf16[9,128,256]{2,1,0:T(8,128)(2,1)S(1)} %get-tuple-element.38.refs_12_), channel_id=1, source_target_pairs={{0,1},{1,0},{2,3},{3,2},{4,5},{5,4},{6,7},{7,6},{8,9},{9,8},{10,11... | collective-permute-start | bytes 1769480 | tf_op jit(solution)/shard_map/ppermute | solution.py:310
  30.8 5.2 %collective-permute-start.10 = (bf16[256,256]{1,0:T(8,128)(2,1)S(1)}, bf16[256,256]{1,0:T(8,128)(2,1)S(1)}, u32[]{:S(2)}, u32[]{:S(2)}) collective-permute-start(bf16[256,256]{1,0:T(8,128)(2,1)S(1)} %multiply_convert_fusion.1.refs_6_), channel_id=1, source_target_pairs={{0,2},{1,3},{2,0},{3,1},{4,6},{5,7},{6,4},{7,5},{8,10},{9,11},{10,... | collective-permute-start | bytes 393224 | tf_op jit(solution)/shard_map/ppermute | solution.py:310
  31.2 5.8 %collective-permute-start.14 = (bf16[256,256]{1,0:T(8,128)(2,1)S(1)}, bf16[256,256]{1,0:T(8,128)(2,1)S(1)}, u32[]{:S(2)}, u32[]{:S(2)}) collective-permute-start(bf16[256,256]{1,0:T(8,128)(2,1)S(1)} %multiply_convert_fusion.refs_10_), channel_id=1, source_target_pairs={{0,1},{1,0},{2,3},{3,2},{4,5},{5,4},{6,7},{7,6},{8,9},{9,8},{10,11... | collective-permute-start | bytes 393224 | tf_op jit(solution)/shard_map/ppermute | solution.py:310
  31.6 5.5 %collective-permute-start.11 = (bf16[256,256]{1,0:T(8,128)(2,1)S(1)}, bf16[256,256]{1,0:T(8,128)(2,1)S(1)}, u32[]{:S(2)}, u32[]{:S(2)}) collective-permute-start(bf16[256,256]{1,0:T(8,128)(2,1)S(1)} %multiply_convert_fusion.1.refs_6_), channel_id=1, source_target_pairs={{0,1},{1,0},{2,3},{3,2},{4,5},{5,4},{6,7},{7,6},{8,9},{9,8},{10,11... | collective-permute-start | bytes 393224 | tf_op jit(solution)/shard_map/ppermute | solution.py:310
  36.0 1.8 %collective-permute-start.12 = (bf16[256,256]{1,0:T(8,128)(2,1)S(1)}, bf16[256,256]{1,0:T(8,128)(2,1)S(1)}, u32[]{:S(2)}, u32[]{:S(2)}) collective-permute-start(bf16[256,256]{1,0:T(8,128)(2,1)S(1)} %collective-permute-done.10.refs_7_), channel_id=1, source_target_pairs={{0,1},{1,0},{2,3},{3,2},{4,5},{5,4},{6,7},{7,6},{8,9},{9,8},{10,11... | collective-permute-start | bytes 393224 | tf_op jit(solution)/shard_map/ppermute | solution.py:310
  36.8 5.1 %collective-permute-start.16 = (bf16[256,256]{1,0:T(8,128)(2,1)S(1)}, bf16[256,256]{1,0:T(8,128)(2,1)S(1)}, u32[]{:S(2)}, u32[]{:S(2)}) collective-permute-start(bf16[256,256]{1,0:T(8,128)(2,1)S(1)} %multiply_convert_fusion.refs_10_), channel_id=1, source_target_pairs={{0,2},{1,3},{2,0},{3,1},{4,6},{5,7},{6,4},{7,5},{8,10},{9,11},{10,... | collective-permute-start | bytes 393224 | tf_op jit(solution)/shard_map/ppermute | solution.py:310
  41.9 1.8 %collective-permute-start.17 = (bf16[256,256]{1,0:T(8,128)(2,1)S(1)}, bf16[256,256]{1,0:T(8,128)(2,1)S(1)}, u32[]{:S(2)}, u32[]{:S(2)}) collective-permute-start(bf16[256,256]{1,0:T(8,128)(2,1)S(1)} %collective-permute-done.16.refs_2_), channel_id=1, source_target_pairs={{0,1},{1,0},{2,3},{3,2},{4,5},{5,4},{6,7},{7,6},{8,9},{9,8},{10,11... | collective-permute-start | bytes 393224 | tf_op jit(solution)/shard_map/ppermute | solution.py:310

commit v3 on v2

--- a/solution.py
+++ b/solution.py
@@ -17,7 +17,8 @@
 NN = (((1,), (0,)), ((), ()))
 NT = (((1,), (1,)), ((), ()))
 VMEM_LIMIT = 30 << 20
-STAGE_WEIGHT = 8
+STAGE_WEIGHT = 6
+CONTRACT_COST = 300_000_000
 VMEM = pl.BlockSpec(memory_space=pltpu.VMEM)
 HBM = pl.BlockSpec(memory_space=pltpu.HBM)
 
@@ -141,18 +142,21 @@
     return out[0], out[1], out[2 : 2 + micro], out[2 + micro :]
 
 
-def stage(arrived, slope, weights, rows, cols):
+def stage(step, arrived, slope, weights, rows, cols):
     taps, width, _ = weights.shape
     length = rows * cols
     count = len(arrived)
 
     def kernel(*refs):
         parts, (slope_ref, w_ref, out_ref, shifted) = refs[:count], refs[count:]
-        grad = parts[0][...].astype(F32)
-        for part in parts[1:]:
-            grad += part[...].astype(F32)
-        local = (grad * slope_ref[...]).astype(BF16).astype(F32)
-        out_ref[...] = gradient_in(grad, local, shifted, w_ref, rows, cols).astype(BF16)
+
+        @pl.when(lax.axis_index("section") == lax.axis_size("section") - 1 - step)
+        def _():
+            grad = parts[0][...].astype(F32)
+            for part in parts[1:]:
+                grad += part[...].astype(F32)
+            local = (grad * slope_ref[...]).astype(BF16).astype(F32)
+            out_ref[...] = gradient_in(grad, local, shifted, w_ref, rows, cols).astype(BF16)
 
     return pl.pallas_call(
         kernel,
@@ -236,7 +240,7 @@
     )(ours, theirs, rest)
 
 
-def contract(base, momentum_base, blocks, gains, final, pieces=(), last=0):
+def contract(base, momentum_base, blocks, gains, final, pieces=(), last=0, cost=0):
     taps, width, _ = base.shape
     share = momentum_base.shape[1]
     count = len(blocks)
@@ -259,11 +263,12 @@
                 acc = term if acc is None else acc + term
             total[k % 2] = acc
             out_now[k] = base_ref[k] + gains[0] * acc
-            for (at, _), piece in zip(pieces, taken):
-                for n in range(2):
+            for (at, low_tap, _), piece in zip(pieces, taken):
+                j = k - low_tap
+                for n in range(2 if 0 <= j < piece.shape[0] else 0):
                     where = jnp.bitwise_xor(here, at | n * last) * share
                     lines = pl.ds(pl.multiple_of(where, share), share)
-                    out_now[k, lines, :] -= piece[k, n * share : (n + 1) * share].astype(F32)
+                    out_now[k, lines, :] -= piece[j, n * share : (n + 1) * share].astype(F32)
             mom_now[k] = mom_ref[k] + gains[1] * total[k % 2, pl.ds(own, share), :]
             if final:
                 copies.append(pltpu.make_async_copy(out_now.at[k], out_ref.at[k], sems.at[0, k]))
@@ -290,8 +295,9 @@
         out_specs=[HBM if final else VMEM] * 2,
         scratch_shapes=scratch,
         compiler_params=params_of(),
+        cost_estimate=pl.CostEstimate(flops=cost, bytes_accessed=0, transcendentals=0),
         name="contract",
-    )(base, momentum_base, *[one[0] for one in blocks], *[one[2] for one in blocks], *[one[1] for one in pieces])
+    )(base, momentum_base, *[one[0] for one in blocks], *[one[2] for one in blocks], *[one[2] for one in pieces])
 
 
 def per_device(section_inputs, cotangent, crop_rows, drift, params, momentum):
@@ -328,7 +334,7 @@
     weights, x_near, slopes, tops = prepare(crop_rows, x, cot, params[0], rows, cols)
     arrived = [[top] for top in tops]
     for step in range(sections - 1):
-        leaving = [stage(arrived[m], slopes[m], weights, rows, cols) for m in range(micro)]
+        leaving = [stage(step, arrived[m], slopes[m], weights, rows, cols) for m in range(micro)]
         for m in range(micro):
             arrived[m].append(hop(leaving[m], step))
         if step == 0:
@@ -343,30 +349,39 @@
                 ours = jnp.concatenate([1.33 / replicas * live[0] + 0.567 * own, live[last]], axis=1).astype(BF16)
                 rest = 0.9 * own + live[0] / replicas
         arrived[0][-1] = after(arrived[0][-1], *leaving[1:], *([ours] if step == 0 else []))
-    pair, momentum_base = incoming(ours, swap(ours, last), rest, replicas)
-    pieces = spread_out(pair, low)
-    base = params[0]
+    theirs = swap(ours, last)
 
     turned = {at: turned_taps(one, rows, cols) for at, one in spread_out(x_sent, bits)}
 
     gain = 0.5 * scale / replicas
     gains = (-1.33 * gain, gain)
-    blocks = []
     arrived[0][-1] = after(arrived[0][-1], *turned.values())
+    near, crossed = [], []
     for m in range(micro):
         local = (sum(one.astype(F32) for one in arrived[m]) * slopes[m]).astype(BF16)
-        if m < micro - 1:
-            blocks += [(turned[at], m, one) for at, one in spread_out(local, bits)]
-            continue
-        for at, one in spread_out(local, low):
-            blocks.append((turned[at], m, one))
-        for at in range(0, len(blocks), 6):
-            base, momentum_base = contract(base, momentum_base, blocks[at : at + 6], gains, False, pieces, last)
-            pieces = ()
-        crossed = after(swap(local, last), base)
-        blocks = [(turned[at | last], m, one) for at, one in spread_out(crossed, low)]
-    for at in range(0, len(blocks), 2):
-        base, momentum_base = contract(base, momentum_base, blocks[at : at + 2], gains, at + 2 >= len(blocks))
+        crossed.append(swap(local, last))
+        near.append([(turned[at], m, one) for at, one in spread_out(local, low)])
+    base, momentum_base = params[0], rest
+    for m in range(micro):
+        if m:
+            at, _, one = near[m][-1]
+            near[m][-1] = (at, m, after(one, base))
+        else:
+            base = after(base, crossed[0])
+        base, momentum_base = contract(base, momentum_base, near[m], gains, False, cost=CONTRACT_COST)
+        if m == 0:
+            pair, momentum_base = incoming(ours, after(theirs, base), momentum_base, replicas)
+    blocks = []
+    for m in range(micro):
+        blocks += [(turned[at | last], m, one) for at, one in spread_out(after(crossed[m], base), low)]
+    pieces = []
+    for k in range(0, taps, 3):
+        pieces += [(at, k, one) for at, one in spread_out(pair[k : k + 3], low)]
+    for at in range(0, len(blocks), 4):
+        base, momentum_base = contract(
+            base, momentum_base, blocks[at : at + 4], gains, at + 4 >= len(blocks), pieces, last
+        )
+        pieces = ()
     return (base[None], momentum_base[None])
 
 

time: 45.9 us -> 43.8 us (0.954)
  Pallas kernels: 14 us -> 12.2 us
  starting transfers between devices: 14.8 us -> 13.4 us
  waiting for transfers between devices: 15.8 us -> 16.7 us
    pallas_call x6, Pallas kernels: 3.1 us -> 1.09 us  [stage(): pl.pallas_call(kernel, out_shape=jax.ShapeDtypeStruct((length, width), BF...]
    ppermute x12 -> x14, starting transfers between devices: 8.64 us -> 7.58 us  [swap(): lax.ppermute(value, 'replica', [(i, i ^ bit) for i in range(replicas)])]
    ppermute x6, waiting for transfers between devices: 0.02 us -> 0.88 us  [hop(): lax.ppermute(value, 'section', [(sections - 1 - step, sections - 2 - step)])]
    pallas_call x2 -> x3, Pallas kernels: 4.51 us -> 4.75 us  [contract(): pl.pallas_call(kernel, out_shape=(jax.ShapeDtypeStruct(base.shape, F32),...]
    ppermute x12 -> x14, waiting for transfers between devices: 15.8 us -> 15.8 us  [swap(): lax.ppermute(value, 'replica', [(i, i ^ bit) for i in range(replicas)])]
  transfers between devices with their start and end apart: 18 -> 20, of which waited for: 6 -> 5; matrix products, arithmetic and copies ran while one was open for 0% -> 0% of each run, Pallas kernels for 26% -> 22%
where the time goes in v3:
time: 43.8 us; the launch traced here: 43.6 us
  waiting for transfers between devices  16.7 us (38%)
  starting transfers between devices  13.4 us (31%)
  Pallas kernels  12.2 us (28%)
  between operations  1.07 us (2%)
    ppermute x14, waiting for transfers between devices, swap(): lax.ppermute(value, 'replica', [(i, i ^ bit) for i in range(replicas)])  15.8 us
    ppermute x14, starting transfers between devices, swap(): lax.ppermute(value, 'replica', [(i, i ^ bit) for i in range(replicas)])  7.58 us
    ppermute x6, starting transfers between devices, hop(): lax.ppermute(value, 'section', [(sections - 1 - step, sections - 2 - step)])  5.83 us
    pallas_call x3, Pallas kernels, contract(): pl.pallas_call(kernel, out_shape=(jax.ShapeDtypeStruct(base.shape, F32),...  4.75 us
    pallas_call x1, Pallas kernels, prepare(): pl.pallas_call(kernel, out_shape=shapes, in_specs=[HBM] * 4, out_specs=[V...  3.01 us
    pallas_call x4, Pallas kernels, turned_taps(): pl.pallas_call(kernel, out_shape=jax.ShapeDtypeStruct((blocks, 9, width,...  2.69 us
    pallas_call x6, Pallas kernels, stage(): pl.pallas_call(kernel, out_shape=jax.ShapeDtypeStruct((length, width), BF...  1.09 us
    ppermute x6, waiting for transfers between devices, hop(): lax.ppermute(value, 'section', [(sections - 1 - step, sections - 2 - step)])  0.88 us
  transfers between devices with their start and end apart: 20, of which 5 were waited for; matrix products, arithmetic and copies ran while one was open for 0% of the time, Pallas kernels for 22%

profile of v3, /device:TPU:27, one launch (start us, length us, event | category | flops | bytes accessed | tf_op | source)
XLA Modules:
  0.0 43.6 jit_solution(11600445245103239248)
XLA Ops:
  0.6 0.7 %collective-permute-start.1 = (bf16[9,256,256]{2,1,0:T(8,128)(2,1)}, bf16[9,256,256]{2,1,0:T(8,128)(2,1)S(1)}, u32[]{:S(2)}, u32[]{:S(2)}) collective-permute-start(bf16[9,256,256]{2,1,0:T(8,128)(2,1)} %bitcast.9), channel_id=1, source_target_pairs={{0,1},{1,0},{2,3},{3,2},{4,5},{5,4},{6,7},{7,6},{8,9},{9,8},{10,11... | collective-permute-start | bytes 3538952 | tf_op jit(solution)/shard_map/ppermute | solution.py:316
  1.4 3.0 %prepare.1 = (bf16[9,256,256]{2,1,0:T(8,128)(2,1)S(1)}, bf16[2,256,256]{2,1,0:T(8,128)(2,1)S(1)}, f32[256,256]{1,0:T(8,128)S(1)}, f32[256,256]{1,0:T(8,128)S(1)}...) custom-call(s32[1,2]{1,0:T(1,128)} %crop_ref.1, bf16[2,256,256]{2,1,0:T(8,128)(2,1)} %bitcast.12, ...), custom_call_target="tpu_custom_call" | custom-call | tf_op jit(solution)/shard_map/prepare/pallas_call | solution.py:127
  4.4 0.5 %stage.6 = bf16[256,256]{1,0:T(8,128)(2,1)S(1)} custom-call(bf16[256,256]{1,0:T(8,128)(2,1)S(1)} %get-tuple-element.29.refs_0_, f32[256,256]{1,0:T(8,128)S(1)} %get-tuple-element.30.refs_1_.refs_2_.refs_3_, bf16[9,256,256]{2,1,0:T(8,128)(2,1)S(1)} %get-tuple-element.31.refs_2_.refs_3_.refs_4_), custom_call_target="tpu_custom_call" | custom-call | flops 1811939328 | bytes 1179648 | tf_op jit(solution)/shard_map/stage/pallas_call | solution.py:161
  4.9 1.6 %collective-permute-start = (bf16[256,256]{1,0:T(8,128)(2,1)S(1)}, bf16[256,256]{1,0:T(8,128)(2,1)S(1)}, u32[]{:S(2)}, u32[]{:S(2)}) collective-permute-start(bf16[256,256]{1,0:T(8,128)(2,1)S(1)} %stage.6), channel_id=1, source_target_pairs={{12,8},{13,9},{14,10},{15,11},{28,24},{29,25},{30,26},{31,27}} | collective-permute-start | bytes 393224 | tf_op jit(solution)/shard_map/ppermute | solution.py:325
  6.5 0.5 %stage.7 = bf16[256,256]{1,0:T(8,128)(2,1)S(1)} custom-call(bf16[256,256]{1,0:T(8,128)(2,1)S(1)} %get-tuple-element.32.refs_0_, f32[256,256]{1,0:T(8,128)S(1)} %get-tuple-element.33.refs_1_.refs_2_.refs_3_, bf16[9,256,256]{2,1,0:T(8,128)(2,1)S(1)} %get-tuple-element.31.refs_2_.refs_3_.refs_4_), custom_call_target="tpu_custom_call" | custom-call | flops 1811939328 | bytes 1179648 | tf_op jit(solution)/shard_map/stage/pallas_call | solution.py:161
  7.0 0.0 copy-start.1
  7.0 0.0 copy-start.2
  7.1 1.4 %collective-permute-start.3 = (bf16[256,256]{1,0:T(8,128)(2,1)S(1)}, bf16[256,256]{1,0:T(8,128)(2,1)S(1)}, u32[]{:S(2)}, u32[]{:S(2)}) collective-permute-start(bf16[256,256]{1,0:T(8,128)(2,1)S(1)} %stage.7), channel_id=1, source_target_pairs={{12,8},{13,9},{14,10},{15,11},{28,24},{29,25},{30,26},{31,27}} | collective-permute-start | bytes 393224 | tf_op jit(solution)/shard_map/ppermute | solution.py:325
  8.5 0.3 collective-permute-start.6
  8.8 0.6 %collective-permute-start.7 = (bf16[2,256,256]{2,1,0:T(8,128)(2,1)S(1)}, bf16[2,256,256]{2,1,0:T(8,128)(2,1)S(1)}, u32[]{:S(2)}, u32[]{:S(2)}) collective-permute-start(bf16[2,256,256]{2,1,0:T(8,128)(2,1)S(1)} %get-tuple-element.40.x_ref), channel_id=1, source_target_pairs={{0,1},{1,0},{2,3},{3,2},{4,5},{5,4},{6,7},{7,6},{8,9},{9,8},{10,11... | collective-permute-start | bytes 786440 | tf_op jit(solution)/shard_map/ppermute | solution.py:316
  9.4 0.7 %turned_taps.4.refs_0_ = bf16[2,9,256,256]{3,2,1,0:T(8,128)(2,1)S(1)} custom-call(bf16[2,256,256]{2,1,0:T(8,128)(2,1)S(1)} %get-tuple-element.40.x_ref), custom_call_target="tpu_custom_call" | custom-call | tf_op jit(solution)/shard_map/turned_taps/pallas_call | solution.py:183
  10.1 0.0 collective-permute-done.1.far_ref
  10.1 0.5 %outgoing.1 = (bf16[9,128,256]{2,1,0:T(8,128)(2,1)S(1)}, f32[9,64,256]{2,1,0:T(8,128)S(1)}) custom-call(bf16[9,256,256]{2,1,0:T(8,128)(2,1)S(1)} %bitcast.10, bf16[9,256,256]{2,1,0:T(8,128)(2,1)S(1)} %collective-permute-done.1.far_ref, f32[9,64,256]{2,1,0:T(8,128)S(1)} %bitcast.11), custom_call_target="tpu_custom_call" | custom-call | tf_op jit(solution)/shard_map/outgoing/pallas_call | solution.py:209
  10.6 0.0 collective-permute-done.refs_1_
  10.7 0.7 %collective-permute-start.2 = (bf16[256,256]{1,0:T(8,128)(2,1)S(1)}, bf16[256,256]{1,0:T(8,128)(2,1)S(1)}, u32[]{:S(2)}, u32[]{:S(2)}) collective-permute-start(bf16[256,256]{1,0:T(8,128)(2,1)S(1)} %stage.8), channel_id=1, source_target_pairs={{8,4},{9,5},{10,6},{11,7},{24,20},{25,21},{26,22},{27,23}} | collective-permute-start | bytes 393224 | tf_op jit(solution)/shard_map/ppermute | solution.py:325
  11.3 0.9 %collective-permute-done.3.refs_1_ = bf16[256,256]{1,0:T(8,128)(2,1)S(1)} collective-permute-done((bf16[256,256]{1,0:T(8,128)(2,1)S(1)}, bf16[256,256]{1,0:T(8,128)(2,1)S(1)}, u32[]{:S(2)}, u32[]{:S(2)}) %collective-permute-start.3) | collective-permute-done | bytes 131104 | tf_op jit(solution)/shard_map/ppermute | solution.py:325
  12.2 0.7 %collective-permute-start.5 = (bf16[256,256]{1,0:T(8,128)(2,1)S(1)}, bf16[256,256]{1,0:T(8,128)(2,1)S(1)}, u32[]{:S(2)}, u32[]{:S(2)}) collective-permute-start(bf16[256,256]{1,0:T(8,128)(2,1)S(1)} %stage.9), channel_id=1, source_target_pairs={{8,4},{9,5},{10,6},{11,7},{24,20},{25,21},{26,22},{27,23}} | collective-permute-start | bytes 393224 | tf_op jit(solution)/shard_map/ppermute | solution.py:325
  12.9 3.3 %collective-permute-done.6.x_ref = bf16[2,256,256]{2,1,0:T(8,128)(2,1)S(1)} collective-permute-done((bf16[2,256,256]{2,1,0:T(8,128)(2,1)S(1)}, bf16[2,256,256]{2,1,0:T(8,128)(2,1)S(1)}, u32[]{:S(2)}, u32[]{:S(2)}) %collective-permute-start.6) | collective-permute-done | bytes 262176 | tf_op jit(solution)/shard_map/ppermute | solution.py:316
  16.1 1.1 %collective-permute-start.8 = (bf16[2,256,256]{2,1,0:T(8,128)(2,1)S(1)}, bf16[2,256,256]{2,1,0:T(8,128)(2,1)S(1)}, u32[]{:S(2)}, u32[]{:S(2)}) collective-permute-start(bf16[2,256,256]{2,1,0:T(8,128)(2,1)S(1)} %collective-permute-done.6.x_ref), channel_id=1, source_target_pairs={{0,1},{1,0},{2,3},{3,2},{4,5},{5,4},{6,7},{7,6},{8,9},{9,8},{10,11... | collective-permute-start | bytes 786440 | tf_op jit(solution)/shard_map/ppermute | solution.py:316
  17.3 0.3 collective-permute-start.11
  17.5 0.7 %collective-permute-start.4 = (bf16[256,256]{1,0:T(8,128)(2,1)S(1)}, bf16[256,256]{1,0:T(8,128)(2,1)S(1)}, u32[]{:S(2)}, u32[]{:S(2)}) collective-permute-start(bf16[256,256]{1,0:T(8,128)(2,1)S(1)} %stage.10), channel_id=1, source_target_pairs={{4,0},{5,1},{6,2},{7,3},{20,16},{21,17},{22,18},{23,19}} | collective-permute-start | bytes 393224 | tf_op jit(solution)/shard_map/ppermute | solution.py:325
  18.2 0.8 %collective-permute-start.12 = (bf16[256,256]{1,0:T(8,128)(2,1)S(1)}, bf16[256,256]{1,0:T(8,128)(2,1)S(1)}, u32[]{:S(2)}, u32[]{:S(2)}) collective-permute-start(bf16[256,256]{1,0:T(8,128)(2,1)S(1)} %stage.11), channel_id=1, source_target_pairs={{4,0},{5,1},{6,2},{7,3},{20,16},{21,17},{22,18},{23,19}} | collective-permute-start | bytes 393224 | tf_op jit(solution)/shard_map/ppermute | solution.py:325
  19.1 0.7 %turned_taps.5.refs_0_.refs_2_ = bf16[2,9,256,256]{3,2,1,0:T(8,128)(2,1)S(1)} custom-call(bf16[2,256,256]{2,1,0:T(8,128)(2,1)S(1)} %collective-permute-done.6.x_ref), custom_call_target="tpu_custom_call" | custom-call | tf_op jit(solution)/shard_map/turned_taps/pallas_call | solution.py:183
  19.8 0.0 collective-permute-done.7.x_ref
  19.8 0.7 %turned_taps.6.refs_1_ = bf16[2,9,256,256]{3,2,1,0:T(8,128)(2,1)S(1)} custom-call(bf16[2,256,256]{2,1,0:T(8,128)(2,1)S(1)} %collective-permute-done.7.x_ref), custom_call_target="tpu_custom_call" | custom-call | tf_op jit(solution)/shard_map/turned_taps/pallas_call | solution.py:183
  20.5 0.0 copy-start
  20.5 0.0 collective-permute-done.8.x_ref
  20.5 0.7 %turned_taps.7.refs_1_.refs_3_ = bf16[2,9,256,256]{3,2,1,0:T(8,128)(2,1)S(1)} custom-call(bf16[2,256,256]{2,1,0:T(8,128)(2,1)S(1)} %collective-permute-done.8.x_ref), custom_call_target="tpu_custom_call" | custom-call | tf_op jit(solution)/shard_map/turned_taps/pallas_call | solution.py:183
  21.2 0.0 collective-permute-done.4
  21.2 0.1 multiply_convert_fusion.1.refs_2_
  21.3 1.3 %collective-permute-start.9 = (bf16[256,256]{1,0:T(8,128)(2,1)S(1)}, bf16[256,256]{1,0:T(8,128)(2,1)S(1)}, u32[]{:S(2)}, u32[]{:S(2)}) collective-permute-start(bf16[256,256]{1,0:T(8,128)(2,1)S(1)} %multiply_convert_fusion.1.refs_2_), channel_id=1, source_target_pairs={{0,2},{1,3},{2,0},{3,1},{4,6},{5,7},{6,4},{7,5},{8,10},{9,11},{10,... | collective-permute-start | bytes 393224 | tf_op jit(solution)/shard_map/ppermute | solution.py:316
  22.5 0.6 %collective-permute-start.10 = (bf16[256,256]{1,0:T(8,128)(2,1)S(1)}, bf16[256,256]{1,0:T(8,128)(2,1)S(1)}, u32[]{:S(2)}, u32[]{:S(2)}) collective-permute-start(bf16[256,256]{1,0:T(8,128)(2,1)S(1)} %multiply_convert_fusion.1.refs_2_), channel_id=1, source_target_pairs={{0,1},{1,0},{2,3},{3,2},{4,5},{5,4},{6,7},{7,6},{8,9},{9,8},{10,11... | collective-permute-start | bytes 393224 | tf_op jit(solution)/shard_map/ppermute | solution.py:316
  23.1 0.1 multiply_convert_fusion.refs_2_
  23.2 0.1 collective-permute-start.13
  23.3 0.3 collective-permute-start.15
  23.6 11.5 %collective-permute-done.9.refs_4_ = bf16[256,256]{1,0:T(8,128)(2,1)S(1)} collective-permute-done((bf16[256,256]{1,0:T(8,128)(2,1)S(1)}, bf16[256,256]{1,0:T(8,128)(2,1)S(1)}, u32[]{:S(2)}, u32[]{:S(2)}) %collective-permute-start.9) | collective-permute-done | bytes 131104 | tf_op jit(solution)/shard_map/ppermute | solution.py:316
  35.1 0.0 collective-permute-done.10.refs_3_
  35.1 1.0 %contract.3 = (f32[9,256,256]{2,1,0:T(8,128)S(1)}, f32[9,64,256]{2,1,0:T(8,128)S(1)}) custom-call(f32[9,256,256]{2,1,0:T(8,128)S(1)} %bitcast.8, f32[9,64,256]{2,1,0:T(8,128)S(1)} %get-tuple-element.43.mom_ref, bf16[2,9,256,256]{3,2,1,0:T(8,128)(2,1)S(1)} %turned_taps.4.refs_0_, bf16[2,9,256,256]{3,2,1,0:T(8,128)(2,1)S(1)} %turned_taps.6.refs_1_, ...), custom_call_target="tpu_custom_call" | custom-call | flops 300000000 | tf_op jit(solution)/shard_map/contract/pallas_call | solution.py:288
  36.1 0.2 incoming.1
  36.3 1.2 %collective-permute-start.17 = (bf16[3,128,256]{2,1,0:T(8,128)(2,1)S(1)}, bf16[3,128,256]{2,1,0:T(8,128)(2,1)S(1)}, u32[]{:S(2)}, u32[]{:S(2)}) collective-permute-start(bf16[3,128,256]{2,1,0:T(8,128)(2,1)S(1)} %get-tuple-element.58.refs_8_), channel_id=1, source_target_pairs={{0,1},{1,0},{2,3},{3,2},{4,5},{5,4},{6,7},{7,6},{8,9},{9,8},{10,11... | collective-permute-start | bytes 589832 | tf_op jit(solution)/shard_map/ppermute | solution.py:316
  37.6 0.1 collective-permute-start.18
  37.6 0.4 collective-permute-start.19
  38.1 1.0 %contract.4 = (f32[9,256,256]{2,1,0:T(8,128)S(1)}, f32[9,64,256]{2,1,0:T(8,128)S(1)}) custom-call(f32[9,256,256]{2,1,0:T(8,128)S(1)} %get-tuple-element.44.base_ref, f32[9,64,256]{2,1,0:T(8,128)S(1)} %get-tuple-element.47.mom_ref, bf16[2,9,256,256]{3,2,1,0:T(8,128)(2,1)S(1)} %turned_taps.4.refs_0_, bf16[2,9,256,256]{3,2,1,0:T(8,128)(2,1)S(1)} %turned_taps.6.refs_1_, ...), custom_call_target="tpu_custom_call" | custom-call | flops 300000000 | tf_op jit(solution)/shard_map/contract/pallas_call | solution.py:288
  39.1 0.1 collective-permute-start.16
  39.2 0.4 collective-permute-start.14
  39.6 0.8 %collective-permute-done.16.refs_7_ = bf16[256,256]{1,0:T(8,128)(2,1)S(1)} collective-permute-done((bf16[256,256]{1,0:T(8,128)(2,1)S(1)}, bf16[256,256]{1,0:T(8,128)(2,1)S(1)}, u32[]{:S(2)}, u32[]{:S(2)}) %collective-permute-start.16) | collective-permute-done | bytes 131104 | tf_op jit(solution)/shard_map/ppermute | solution.py:316
  40.5 0.2 collective-permute-done.14.refs_5_
  40.7 2.8 %contract.5 = (f32[9,256,256]{2,1,0:T(8,128)}, f32[9,64,256]{2,1,0:T(8,128)}) custom-call(f32[9,256,256]{2,1,0:T(8,128)S(1)} %get-tuple-element.49.base_ref, f32[9,64,256]{2,1,0:T(8,128)S(1)} %get-tuple-element.50.mom_ref, bf16[2,9,256,256]{3,2,1,0:T(8,128)(2,1)S(1)} %turned_taps.5.refs_0_.refs_2_, bf16[2,9,256,256]{3,2,1,0:T(8,128)(2,1)S(1)} %turned_taps.7.refs_1_.refs_3_, ...), custom_call_target="tpu_custom_call" | custom-call | tf_op jit(solution)/shard_map/contract/pallas_call | solution.py:288
  (17 shorter events, 0.1 us)
Async XLA Ops:
  0.6 9.5 %collective-permute-start.1 = (bf16[9,256,256]{2,1,0:T(8,128)(2,1)}, bf16[9,256,256]{2,1,0:T(8,128)(2,1)S(1)}, u32[]{:S(2)}, u32[]{:S(2)}) collective-permute-start(bf16[9,256,256]{2,1,0:T(8,128)(2,1)} %bitcast.9), channel_id=1, source_target_pairs={{0,1},{1,0},{2,3},{3,2},{4,5},{5,4},{6,7},{7,6},{8,9},{9,8},{10,11... | collective-permute-start | bytes 3538952 | tf_op jit(solution)/shard_map/ppermute | solution.py:316
  4.9 5.7 %collective-permute-start = (bf16[256,256]{1,0:T(8,128)(2,1)S(1)}, bf16[256,256]{1,0:T(8,128)(2,1)S(1)}, u32[]{:S(2)}, u32[]{:S(2)}) collective-permute-start(bf16[256,256]{1,0:T(8,128)(2,1)S(1)} %stage.6), channel_id=1, source_target_pairs={{12,8},{13,9},{14,10},{15,11},{28,24},{29,25},{30,26},{31,27}} | collective-permute-start | bytes 393224 | tf_op jit(solution)/shard_map/ppermute | solution.py:325
  7.0 3.1 %copy-start.1 = (bf16[1,1,9,256,256]{4,3,2,1,0:T(8,128)(2,1)S(1)}, bf16[1,1,9,256,256]{4,3,2,1,0:T(8,128)(2,1)}, u32[]{:S(2)}) copy-start(bf16[1,1,9,256,256]{4,3,2,1,0:T(8,128)(2,1)} %param.9) | copy-start | bytes 3538948
  7.0 3.1 %copy-start.2 = (f32[1,9,64,256]{3,2,1,0:T(8,128)S(1)}, f32[1,9,64,256]{3,2,1,0:T(8,128)}, u32[]{:S(2)}) copy-start(f32[1,9,64,256]{3,2,1,0:T(8,128)} %param.11) | copy-start | bytes 1769476
  7.1 5.1 %collective-permute-start.3 = (bf16[256,256]{1,0:T(8,128)(2,1)S(1)}, bf16[256,256]{1,0:T(8,128)(2,1)S(1)}, u32[]{:S(2)}, u32[]{:S(2)}) collective-permute-start(bf16[256,256]{1,0:T(8,128)(2,1)S(1)} %stage.7), channel_id=1, source_target_pairs={{12,8},{13,9},{14,10},{15,11},{28,24},{29,25},{30,26},{31,27}} | collective-permute-start | bytes 393224 | tf_op jit(solution)/shard_map/ppermute | solution.py:325
  8.5 7.7 %collective-permute-start.6 = (bf16[2,256,256]{2,1,0:T(8,128)(2,1)S(1)}, bf16[2,256,256]{2,1,0:T(8,128)(2,1)S(1)}, u32[]{:S(2)}, u32[]{:S(2)}) collective-permute-start(bf16[2,256,256]{2,1,0:T(8,128)(2,1)S(1)} %get-tuple-element.40.x_ref), channel_id=1, source_target_pairs={{0,2},{1,3},{2,0},{3,1},{4,6},{5,7},{6,4},{7,5},{8,10},{9,11},{10,... | collective-permute-start | bytes 786440 | tf_op jit(solution)/shard_map/ppermute | solution.py:316
  8.8 11.0 %collective-permute-start.7 = (bf16[2,256,256]{2,1,0:T(8,128)(2,1)S(1)}, bf16[2,256,256]{2,1,0:T(8,128)(2,1)S(1)}, u32[]{:S(2)}, u32[]{:S(2)}) collective-permute-start(bf16[2,256,256]{2,1,0:T(8,128)(2,1)S(1)} %get-tuple-element.40.x_ref), channel_id=1, source_target_pairs={{0,1},{1,0},{2,3},{3,2},{4,5},{5,4},{6,7},{7,6},{8,9},{9,8},{10,11... | collective-permute-start | bytes 786440 | tf_op jit(solution)/shard_map/ppermute | solution.py:316
  10.7 6.9 %collective-permute-start.2 = (bf16[256,256]{1,0:T(8,128)(2,1)S(1)}, bf16[256,256]{1,0:T(8,128)(2,1)S(1)}, u32[]{:S(2)}, u32[]{:S(2)}) collective-permute-start(bf16[256,256]{1,0:T(8,128)(2,1)S(1)} %stage.8), channel_id=1, source_target_pairs={{8,4},{9,5},{10,6},{11,7},{24,20},{25,21},{26,22},{27,23}} | collective-permute-start | bytes 393224 | tf_op jit(solution)/shard_map/ppermute | solution.py:325
  12.2 6.0 %collective-permute-start.5 = (bf16[256,256]{1,0:T(8,128)(2,1)S(1)}, bf16[256,256]{1,0:T(8,128)(2,1)S(1)}, u32[]{:S(2)}, u32[]{:S(2)}) collective-permute-start(bf16[256,256]{1,0:T(8,128)(2,1)S(1)} %stage.9), channel_id=1, source_target_pairs={{8,4},{9,5},{10,6},{11,7},{24,20},{25,21},{26,22},{27,23}} | collective-permute-start | bytes 393224 | tf_op jit(solution)/shard_map/ppermute | solution.py:325
  16.1 4.3 %collective-permute-start.8 = (bf16[2,256,256]{2,1,0:T(8,128)(2,1)S(1)}, bf16[2,256,256]{2,1,0:T(8,128)(2,1)S(1)}, u32[]{:S(2)}, u32[]{:S(2)}) collective-permute-start(bf16[2,256,256]{2,1,0:T(8,128)(2,1)S(1)} %collective-permute-done.6.x_ref), channel_id=1, source_target_pairs={{0,1},{1,0},{2,3},{3,2},{4,5},{5,4},{6,7},{7,6},{8,9},{9,8},{10,11... | collective-permute-start | bytes 786440 | tf_op jit(solution)/shard_map/ppermute | solution.py:316
  17.3 18.8 %collective-permute-start.11 = (bf16[9,128,256]{2,1,0:T(8,128)(2,1)S(1)}, bf16[9,128,256]{2,1,0:T(8,128)(2,1)S(1)}, u32[]{:S(2)}, u32[]{:S(2)}) collective-permute-start(bf16[9,128,256]{2,1,0:T(8,128)(2,1)S(1)} %get-tuple-element.35.ours_ref), channel_id=1, source_target_pairs={{0,2},{1,3},{2,0},{3,1},{4,6},{5,7},{6,4},{7,5},{8,10},{9,11},{10,... | collective-permute-start | bytes 1769480 | tf_op jit(solution)/shard_map/ppermute | solution.py:316
  17.5 3.6 %collective-permute-start.4 = (bf16[256,256]{1,0:T(8,128)(2,1)S(1)}, bf16[256,256]{1,0:T(8,128)(2,1)S(1)}, u32[]{:S(2)}, u32[]{:S(2)}) collective-permute-start(bf16[256,256]{1,0:T(8,128)(2,1)S(1)} %stage.10), channel_id=1, source_target_pairs={{4,0},{5,1},{6,2},{7,3},{20,16},{21,17},{22,18},{23,19}} | collective-permute-start | bytes 393224 | tf_op jit(solution)/shard_map/ppermute | solution.py:325
  18.2 4.9 %collective-permute-start.12 = (bf16[256,256]{1,0:T(8,128)(2,1)S(1)}, bf16[256,256]{1,0:T(8,128)(2,1)S(1)}, u32[]{:S(2)}, u32[]{:S(2)}) collective-permute-start(bf16[256,256]{1,0:T(8,128)(2,1)S(1)} %stage.11), channel_id=1, source_target_pairs={{4,0},{5,1},{6,2},{7,3},{20,16},{21,17},{22,18},{23,19}} | collective-permute-start | bytes 393224 | tf_op jit(solution)/shard_map/ppermute | solution.py:325
  20.5 14.6 %copy-start = (f32[1,9,256,256]{3,2,1,0:T(8,128)S(1)}, f32[1,9,256,256]{3,2,1,0:T(8,128)}, u32[]{:S(2)}) copy-start(f32[1,9,256,256]{3,2,1,0:T(8,128)} %param.10) | copy-start | bytes 7077892
  21.3 13.8 %collective-permute-start.9 = (bf16[256,256]{1,0:T(8,128)(2,1)S(1)}, bf16[256,256]{1,0:T(8,128)(2,1)S(1)}, u32[]{:S(2)}, u32[]{:S(2)}) collective-permute-start(bf16[256,256]{1,0:T(8,128)(2,1)S(1)} %multiply_convert_fusion.1.refs_2_), channel_id=1, source_target_pairs={{0,2},{1,3},{2,0},{3,1},{4,6},{5,7},{6,4},{7,5},{8,10},{9,11},{10,... | collective-permute-start | bytes 393224 | tf_op jit(solution)/shard_map/ppermute | solution.py:316
  22.5 12.5 %collective-permute-start.10 = (bf16[256,256]{1,0:T(8,128)(2,1)S(1)}, bf16[256,256]{1,0:T(8,128)(2,1)S(1)}, u32[]{:S(2)}, u32[]{:S(2)}) collective-permute-start(bf16[256,256]{1,0:T(8,128)(2,1)S(1)} %multiply_convert_fusion.1.refs_2_), channel_id=1, source_target_pairs={{0,1},{1,0},{2,3},{3,2},{4,5},{5,4},{6,7},{7,6},{8,9},{9,8},{10,11... | collective-permute-start | bytes 393224 | tf_op jit(solution)/shard_map/ppermute | solution.py:316
  23.2 14.9 %collective-permute-start.13 = (bf16[256,256]{1,0:T(8,128)(2,1)S(1)}, bf16[256,256]{1,0:T(8,128)(2,1)S(1)}, u32[]{:S(2)}, u32[]{:S(2)}) collective-permute-start(bf16[256,256]{1,0:T(8,128)(2,1)S(1)} %multiply_convert_fusion.refs_2_), channel_id=1, source_target_pairs={{0,1},{1,0},{2,3},{3,2},{4,5},{5,4},{6,7},{7,6},{8,9},{9,8},{10,11... | collective-permute-start | bytes 393224 | tf_op jit(solution)/shard_map/ppermute | solution.py:316
  23.3 15.8 %collective-permute-start.15 = (bf16[256,256]{1,0:T(8,128)(2,1)S(1)}, bf16[256,256]{1,0:T(8,128)(2,1)S(1)}, u32[]{:S(2)}, u32[]{:S(2)}) collective-permute-start(bf16[256,256]{1,0:T(8,128)(2,1)S(1)} %multiply_convert_fusion.refs_2_), channel_id=1, source_target_pairs={{0,2},{1,3},{2,0},{3,1},{4,6},{5,7},{6,4},{7,5},{8,10},{9,11},{10,... | collective-permute-start | bytes 393224 | tf_op jit(solution)/shard_map/ppermute | solution.py:316
  36.3 4.3 %collective-permute-start.17 = (bf16[3,128,256]{2,1,0:T(8,128)(2,1)S(1)}, bf16[3,128,256]{2,1,0:T(8,128)(2,1)S(1)}, u32[]{:S(2)}, u32[]{:S(2)}) collective-permute-start(bf16[3,128,256]{2,1,0:T(8,128)(2,1)S(1)} %get-tuple-element.58.refs_8_), channel_id=1, source_target_pairs={{0,1},{1,0},{2,3},{3,2},{4,5},{5,4},{6,7},{7,6},{8,9},{9,8},{10,11... | collective-permute-start | bytes 589832 | tf_op jit(solution)/shard_map/ppermute | solution.py:316
  37.6 3.1 %collective-permute-start.18 = (bf16[3,128,256]{2,1,0:T(8,128)(2,1)S(1)}, bf16[3,128,256]{2,1,0:T(8,128)(2,1)S(1)}, u32[]{:S(2)}, u32[]{:S(2)}) collective-permute-start(bf16[3,128,256]{2,1,0:T(8,128)(2,1)S(1)} %get-tuple-element.57.refs_10_), channel_id=1, source_target_pairs={{0,1},{1,0},{2,3},{3,2},{4,5},{5,4},{6,7},{7,6},{8,9},{9,8},{10,11... | collective-permute-start | bytes 589832 | tf_op jit(solution)/shard_map/ppermute | solution.py:316
  37.6 3.0 %collective-permute-start.19 = (bf16[3,128,256]{2,1,0:T(8,128)(2,1)S(1)}, bf16[3,128,256]{2,1,0:T(8,128)(2,1)S(1)}, u32[]{:S(2)}, u32[]{:S(2)}) collective-permute-start(bf16[3,128,256]{2,1,0:T(8,128)(2,1)S(1)} %get-tuple-element.56.refs_12_), channel_id=1, source_target_pairs={{0,1},{1,0},{2,3},{3,2},{4,5},{5,4},{6,7},{7,6},{8,9},{9,8},{10,11... | collective-permute-start | bytes 589832 | tf_op jit(solution)/shard_map/ppermute | solution.py:316
  39.1 1.4 %collective-permute-start.16 = (bf16[256,256]{1,0:T(8,128)(2,1)S(1)}, bf16[256,256]{1,0:T(8,128)(2,1)S(1)}, u32[]{:S(2)}, u32[]{:S(2)}) collective-permute-start(bf16[256,256]{1,0:T(8,128)(2,1)S(1)} %collective-permute-done.15.refs_6_), channel_id=1, source_target_pairs={{0,1},{1,0},{2,3},{3,2},{4,5},{5,4},{6,7},{7,6},{8,9},{9,8},{10,11... | collective-permute-start | bytes 393224 | tf_op jit(solution)/shard_map/ppermute | solution.py:316
  39.2 1.5 %collective-permute-start.14 = (bf16[256,256]{1,0:T(8,128)(2,1)S(1)}, bf16[256,256]{1,0:T(8,128)(2,1)S(1)}, u32[]{:S(2)}, u32[]{:S(2)}) collective-permute-start(bf16[256,256]{1,0:T(8,128)(2,1)S(1)} %collective-permute-done.9.refs_4_), channel_id=1, source_target_pairs={{0,1},{1,0},{2,3},{3,2},{4,5},{5,4},{6,7},{7,6},{8,9},{9,8},{10,11... | collective-permute-start | bytes 393224 | tf_op jit(solution)/shard_map/ppermute | solution.py:316

commit v4 on v3

--- a/solution.py
+++ b/solution.py
@@ -17,7 +17,9 @@
 NN = (((1,), (0,)), ((), ()))
 NT = (((1,), (1,)), ((), ()))
 VMEM_LIMIT = 30 << 20
+FIRST_WEIGHT = 0
 STAGE_WEIGHT = 6
+LATER_WEIGHT = 1
 CONTRACT_COST = 300_000_000
 VMEM = pl.BlockSpec(memory_space=pltpu.VMEM)
 HBM = pl.BlockSpec(memory_space=pltpu.HBM)
@@ -142,7 +144,7 @@
     return out[0], out[1], out[2 : 2 + micro], out[2 + micro :]
 
 
-def stage(step, arrived, slope, weights, rows, cols):
+def stage(step, arrived, slope, weights, rows, cols, weight):
     taps, width, _ = weights.shape
     length = rows * cols
     count = len(arrived)
@@ -165,7 +167,7 @@
         out_specs=VMEM,
         scratch_shapes=[pltpu.VMEM((3, length + 2 * cols, width), BF16)],
         compiler_params=params_of(),
-        cost_estimate=product_cost(STAGE_WEIGHT * taps, length, width, 2 * weights.size),
+        cost_estimate=product_cost(weight * taps, length, width, 2 * weights.size),
         name="stage",
     )(*arrived, slope, weights)
 
@@ -191,48 +193,54 @@
     )(inputs)
 
 
-def outgoing(near, far, momentum, last, replicas):
+def outgoing(inputs, near, far, momentum, last, replicas):
     taps, width, _ = near.shape
     share = momentum.shape[1]
-
-    def kernel(near_ref, far_ref, own_ref, out_ref, rest_ref, total):
+    head = inputs.shape[0] * inputs.shape[1]
+
+    def kernel(x_ref, near_ref, far_ref, own_ref, out_ref, rest_ref, total):
+        for m in range(inputs.shape[0]):
+            out_ref[m * inputs.shape[1] : (m + 1) * inputs.shape[1]] = x_ref[m]
         here = lax.axis_index("replica")
         own_rows = pl.ds(pl.multiple_of(here * share, share), share)
         other_rows = pl.ds(pl.multiple_of(jnp.bitwise_xor(here, last) * share, share), share)
         for k in range(taps):
             total[k % 2] = near_ref[k].astype(F32) + far_ref[k].astype(F32)
             mine = total[k % 2, own_rows, :]
-            out_ref[k, :share] = (1.33 / replicas * mine + 0.567 * own_ref[k]).astype(BF16)
-            out_ref[k, share:] = total[k % 2, other_rows, :].astype(BF16)
+            at = head + k * 2 * share
+            out_ref[at : at + share] = (1.33 / replicas * mine + 0.567 * own_ref[k]).astype(BF16)
+            out_ref[at + share : at + 2 * share] = total[k % 2, other_rows, :].astype(BF16)
             rest_ref[k] = 0.9 * own_ref[k] + mine / replicas
 
     return pl.pallas_call(
         kernel,
         out_shape=(
-            jax.ShapeDtypeStruct((taps, 2 * share, width), BF16),
+            jax.ShapeDtypeStruct((head + taps * 2 * share, width), BF16),
             jax.ShapeDtypeStruct(momentum.shape, F32),
         ),
-        in_specs=[VMEM] * 3,
+        in_specs=[VMEM] * 4,
         out_specs=[VMEM] * 2,
         scratch_shapes=[pltpu.VMEM((2, width, width), F32)],
         compiler_params=params_of(),
         name="outgoing",
-    )(near, far, momentum)
+    )(inputs, near, far, momentum)
 
 
 def incoming(ours, theirs, rest, replicas):
-    share = rest.shape[1]
+    taps, share, width = rest.shape
+    head = ours.shape[0] - taps * 2 * share
 
     def kernel(ours_ref, theirs_ref, rest_ref, out_ref, momentum_ref):
-        for k in range(rest.shape[0]):
-            mine, there = ours_ref[k].astype(F32), theirs_ref[k].astype(F32)
+        for k in range(taps):
+            lines = slice(head + k * 2 * share, head + (k + 1) * 2 * share)
+            mine, there = ours_ref[lines].astype(F32), theirs_ref[lines].astype(F32)
             out_ref[k, :share] = (mine[:share] + 1.33 / replicas * there[share:]).astype(BF16)
             out_ref[k, share:] = (there[:share] + 1.33 / replicas * mine[share:]).astype(BF16)
             momentum_ref[k] = rest_ref[k] + there[share:] / replicas
 
     return pl.pallas_call(
         kernel,
-        out_shape=(jax.ShapeDtypeStruct(ours.shape, BF16), jax.ShapeDtypeStruct(rest.shape, F32)),
+        out_shape=(jax.ShapeDtypeStruct((taps, 2 * share, width), BF16), jax.ShapeDtypeStruct(rest.shape, F32)),
         in_specs=[VMEM] * 3,
         out_specs=[VMEM] * 2,
         compiler_params=params_of(),
@@ -334,28 +342,34 @@
     weights, x_near, slopes, tops = prepare(crop_rows, x, cot, params[0], rows, cols)
     arrived = [[top] for top in tops]
     for step in range(sections - 1):
-        leaving = [stage(step, arrived[m], slopes[m], weights, rows, cols) for m in range(micro)]
+        hints = [LATER_WEIGHT if step else STAGE_WEIGHT] * micro
+        hints[0] = hints[0] if step else FIRST_WEIGHT
+        leaving = [stage(step, arrived[m], slopes[m], weights, rows, cols, hints[m]) for m in range(micro)]
         for m in range(micro):
             arrived[m].append(hop(leaving[m], step))
         if step == 0:
             far, x_sent = after(far, *leaving), after(x_near, *leaving)
             if len(low) < 2:
-                ours, rest = outgoing(near, far, own, last, replicas)
+                ours, rest = outgoing(x_sent, near, far, own, last, replicas)
             else:
                 live = {j: slice_of(near, j) + slice_of(far, j) for j in range(0, replicas, 2)}
                 for bit in reversed(low[:-1]):
                     got = {j: swap(v.astype(BF16), bit) for j, v in live.items() if j & bit}
                     live = {j: v + got[j | bit].astype(F32) for j, v in live.items() if not j & bit}
                 ours = jnp.concatenate([1.33 / replicas * live[0] + 0.567 * own, live[last]], axis=1).astype(BF16)
+                ours = jnp.concatenate([x_sent.reshape(-1, width), ours.reshape(-1, width)])
                 rest = 0.9 * own + live[0] / replicas
         arrived[0][-1] = after(arrived[0][-1], *leaving[1:], *([ours] if step == 0 else []))
     theirs = swap(ours, last)
 
-    turned = {at: turned_taps(one, rows, cols) for at, one in spread_out(x_sent, bits)}
+
+    x_there = theirs[: micro * length].reshape(x.shape)
+    x_all = spread_out(x_sent, low) + [(at | last, one) for at, one in spread_out(x_there, low)]
+    turned = {at: turned_taps(one, rows, cols) for at, one in x_all}
 
     gain = 0.5 * scale / replicas
     gains = (-1.33 * gain, gain)
-    arrived[0][-1] = after(arrived[0][-1], *turned.values())
+    arrived[0][-1] = after(arrived[0][-1], *[one for at, one in turned.items() if at < last])
     near, crossed = [], []
     for m in range(micro):
         local = (sum(one.astype(F32) for one in arrived[m]) * slopes[m]).astype(BF16)
@@ -370,7 +384,7 @@
             base = after(base, crossed[0])
         base, momentum_base = contract(base, momentum_base, near[m], gains, False, cost=CONTRACT_COST)
         if m == 0:
-            pair, momentum_base = incoming(ours, after(theirs, base), momentum_base, replicas)
+            pair, momentum_base = incoming(ours, theirs, momentum_base, replicas)
     blocks = []
     for m in range(micro):
         blocks += [(turned[at | last], m, one) for at, one in spread_out(after(crossed[m], base), low)]

time: 43.8 us -> 41.6 us (0.950)
  waiting for transfers between devices: 16.7 us -> 13.2 us
  local copies, waits for them, and re-layouts: 0.06 us -> 0.92 us
    ppermute x14 -> x13, waiting for transfers between devices: 15.8 us -> 12 us  [swap(): lax.ppermute(value, 'replica', [(i, i ^ bit) for i in range(replicas)])]
    unnamed x6, local copies, waits for them, and re-layouts: 0.02 us -> 0.86 us
    ppermute x14 -> x13, starting transfers between devices: 7.58 us -> 7.86 us  [swap(): lax.ppermute(value, 'replica', [(i, i ^ bit) for i in range(replicas)])]
  transfers between devices with their start and end apart: 20 -> 19, of which waited for: 5 -> 2; matrix products, arithmetic and copies ran while one was open for 0% -> 1% of each run, Pallas kernels for 22% -> 23%
where the time goes in v4:
time: 41.6 us; the launch traced here: 41.3 us
  starting transfers between devices  13.7 us (33%)
  waiting for transfers between devices  13.2 us (32%)
  Pallas kernels  12.3 us (30%)
  between operations  1.1 us (3%)
  local copies, waits for them, and re-layouts  0.92 us (2%)
    ppermute x13, waiting for transfers between devices, swap(): lax.ppermute(value, 'replica', [(i, i ^ bit) for i in range(replicas)])  12 us
    ppermute x13, starting transfers between devices, swap(): lax.ppermute(value, 'replica', [(i, i ^ bit) for i in range(replicas)])  7.86 us
    ppermute x6, starting transfers between devices, hop(): lax.ppermute(value, 'section', [(sections - 1 - step, sections - 2 - step)])  5.83 us
    pallas_call x3, Pallas kernels, contract(): pl.pallas_call(kernel, out_shape=(jax.ShapeDtypeStruct(base.shape, F32),...  4.75 us
    pallas_call x1, Pallas kernels, prepare(): pl.pallas_call(kernel, out_shape=shapes, in_specs=[HBM] * 4, out_specs=[V...  3.01 us
    pallas_call x4, Pallas kernels, turned_taps(): pl.pallas_call(kernel, out_shape=jax.ShapeDtypeStruct((blocks, 9, width,...  2.69 us
    ppermute x6, waiting for transfers between devices, hop(): lax.ppermute(value, 'section', [(sections - 1 - step, sections - 2 - step)])  1.23 us
    pallas_call x6, Pallas kernels, stage(): pl.pallas_call(kernel, out_shape=jax.ShapeDtypeStruct((length, width), BF...  1.11 us
  transfers between devices with their start and end apart: 19, of which 2 were waited for; matrix products, arithmetic and copies ran while one was open for 1% of the time, Pallas kernels for 23%

profile of v4, /device:TPU:27, one launch (start us, length us, event | category | flops | bytes accessed | tf_op | source)
XLA Modules:
  0.0 41.3 jit_solution(16956912208041418478)
XLA Ops:
  0.6 0.7 %collective-permute-start.1 = (bf16[9,256,256]{2,1,0:T(8,128)(2,1)}, bf16[9,256,256]{2,1,0:T(8,128)(2,1)S(1)}, u32[]{:S(2)}, u32[]{:S(2)}) collective-permute-start(bf16[9,256,256]{2,1,0:T(8,128)(2,1)} %bitcast.10), channel_id=1, source_target_pairs={{0,1},{1,0},{2,3},{3,2},{4,5},{5,4},{6,7},{7,6},{8,9},{9,8},{10,11... | collective-permute-start | bytes 3538952 | tf_op jit(solution)/shard_map/ppermute | solution.py:324
  1.4 3.0 %prepare.1 = (bf16[9,256,256]{2,1,0:T(8,128)(2,1)S(1)}, bf16[2,256,256]{2,1,0:T(8,128)(2,1)S(1)}, f32[256,256]{1,0:T(8,128)S(1)}, f32[256,256]{1,0:T(8,128)S(1)}...) custom-call(s32[1,2]{1,0:T(1,128)} %crop_ref.1, bf16[2,256,256]{2,1,0:T(8,128)(2,1)} %bitcast.15, ...), custom_call_target="tpu_custom_call" | custom-call | tf_op jit(solution)/shard_map/prepare/pallas_call | solution.py:129
  4.4 0.5 %stage.6 = bf16[256,256]{1,0:T(8,128)(2,1)S(1)} custom-call(bf16[256,256]{1,0:T(8,128)(2,1)S(1)} %get-tuple-element.28.refs_0_, f32[256,256]{1,0:T(8,128)S(1)} %get-tuple-element.29.refs_1_.refs_2_.refs_3_, bf16[9,256,256]{2,1,0:T(8,128)(2,1)S(1)} %get-tuple-element.30.refs_2_.refs_3_.refs_4_), custom_call_target="tpu_custom_call" | custom-call | bytes 1179648 | tf_op jit(solution)/shard_map/stage/pallas_call | solution.py:163
  4.9 1.6 %collective-permute-start = (bf16[256,256]{1,0:T(8,128)(2,1)S(1)}, bf16[256,256]{1,0:T(8,128)(2,1)S(1)}, u32[]{:S(2)}, u32[]{:S(2)}) collective-permute-start(bf16[256,256]{1,0:T(8,128)(2,1)S(1)} %stage.6), channel_id=1, source_target_pairs={{12,8},{13,9},{14,10},{15,11},{28,24},{29,25},{30,26},{31,27}} | collective-permute-start | bytes 393224 | tf_op jit(solution)/shard_map/ppermute | solution.py:333
  6.5 0.0 copy-start.1
  6.5 0.0 copy-start.2
  6.5 0.5 %stage.7 = bf16[256,256]{1,0:T(8,128)(2,1)S(1)} custom-call(bf16[256,256]{1,0:T(8,128)(2,1)S(1)} %get-tuple-element.31.refs_0_, f32[256,256]{1,0:T(8,128)S(1)} %get-tuple-element.32.refs_1_.refs_2_.refs_3_, bf16[9,256,256]{2,1,0:T(8,128)(2,1)S(1)} %get-tuple-element.30.refs_2_.refs_3_.refs_4_), custom_call_target="tpu_custom_call" | custom-call | flops 1811939328 | bytes 1179648 | tf_op jit(solution)/shard_map/stage/pallas_call | solution.py:163
  7.1 0.0 collective-permute-done.1.far_ref
  7.1 0.7 %copy-done.1 = bf16[1,1,9,256,256]{4,3,2,1,0:T(8,128)(2,1)S(1)} copy-done((bf16[1,1,9,256,256]{4,3,2,1,0:T(8,128)(2,1)S(1)}, bf16[1,1,9,256,256]{4,3,2,1,0:T(8,128)(2,1)}, u32[]{:S(2)}) %copy-start.1) | copy-done | bytes 1179672
  7.8 0.1 copy-done.2
  7.9 0.5 %outgoing.1 = (bf16[1664,256]{1,0:T(8,128)(2,1)S(1)}, f32[9,64,256]{2,1,0:T(8,128)S(1)}) custom-call(bf16[2,256,256]{2,1,0:T(8,128)(2,1)S(1)} %get-tuple-element.34.x_ref, bf16[9,256,256]{2,1,0:T(8,128)(2,1)S(1)} %bitcast.11, bf16[9,256,256]{2,1,0:T(8,128)(2,1)S(1)} %collective-permute-done.1.far_ref, f32[9,64,256]{2,1,0:T(8,128)S(1)} %bitcast.14), custom_call_target="tpu_custom_call" | custom-call | tf_op jit(solution)/shard_map/outgoing/pallas_call | solution.py:215
  8.4 0.3 collective-permute-start.9
  8.8 1.3 %collective-permute-start.3 = (bf16[256,256]{1,0:T(8,128)(2,1)S(1)}, bf16[256,256]{1,0:T(8,128)(2,1)S(1)}, u32[]{:S(2)}, u32[]{:S(2)}) collective-permute-start(bf16[256,256]{1,0:T(8,128)(2,1)S(1)} %stage.7), channel_id=1, source_target_pairs={{12,8},{13,9},{14,10},{15,11},{28,24},{29,25},{30,26},{31,27}} | collective-permute-start | bytes 393224 | tf_op jit(solution)/shard_map/ppermute | solution.py:333
  10.0 0.0 collective-permute-done.refs_1_
  10.1 0.7 %collective-permute-start.2 = (bf16[256,256]{1,0:T(8,128)(2,1)S(1)}, bf16[256,256]{1,0:T(8,128)(2,1)S(1)}, u32[]{:S(2)}, u32[]{:S(2)}) collective-permute-start(bf16[256,256]{1,0:T(8,128)(2,1)S(1)} %stage.8), channel_id=1, source_target_pairs={{8,4},{9,5},{10,6},{11,7},{24,20},{25,21},{26,22},{27,23}} | collective-permute-start | bytes 393224 | tf_op jit(solution)/shard_map/ppermute | solution.py:333
  10.8 0.6 %collective-permute-start.6 = (bf16[2,256,256]{2,1,0:T(8,128)(2,1)S(1)}, bf16[2,256,256]{2,1,0:T(8,128)(2,1)S(1)}, u32[]{:S(2)}, u32[]{:S(2)}) collective-permute-start(bf16[2,256,256]{2,1,0:T(8,128)(2,1)S(1)} %get-tuple-element.34.x_ref), channel_id=1, source_target_pairs={{0,1},{1,0},{2,3},{3,2},{4,5},{5,4},{6,7},{7,6},{8,9},{9,8},{10,11... | collective-permute-start | bytes 786440 | tf_op jit(solution)/shard_map/ppermute | solution.py:324
  11.4 1.2 %collective-permute-done.3.refs_1_ = bf16[256,256]{1,0:T(8,128)(2,1)S(1)} collective-permute-done((bf16[256,256]{1,0:T(8,128)(2,1)S(1)}, bf16[256,256]{1,0:T(8,128)(2,1)S(1)}, u32[]{:S(2)}, u32[]{:S(2)}) %collective-permute-start.3) | collective-permute-done | bytes 131104 | tf_op jit(solution)/shard_map/ppermute | solution.py:333
  12.6 0.7 %collective-permute-start.5 = (bf16[256,256]{1,0:T(8,128)(2,1)S(1)}, bf16[256,256]{1,0:T(8,128)(2,1)S(1)}, u32[]{:S(2)}, u32[]{:S(2)}) collective-permute-start(bf16[256,256]{1,0:T(8,128)(2,1)S(1)} %stage.9), channel_id=1, source_target_pairs={{8,4},{9,5},{10,6},{11,7},{24,20},{25,21},{26,22},{27,23}} | collective-permute-start | bytes 393224 | tf_op jit(solution)/shard_map/ppermute | solution.py:333
  13.3 0.0 collective-permute-done.2.refs_2_
  13.3 0.7 %collective-permute-start.4 = (bf16[256,256]{1,0:T(8,128)(2,1)S(1)}, bf16[256,256]{1,0:T(8,128)(2,1)S(1)}, u32[]{:S(2)}, u32[]{:S(2)}) collective-permute-start(bf16[256,256]{1,0:T(8,128)(2,1)S(1)} %stage.10), channel_id=1, source_target_pairs={{4,0},{5,1},{6,2},{7,3},{20,16},{21,17},{22,18},{23,19}} | collective-permute-start | bytes 393224 | tf_op jit(solution)/shard_map/ppermute | solution.py:333
  14.0 0.7 %turned_taps.4.refs_0_ = bf16[2,9,256,256]{3,2,1,0:T(8,128)(2,1)S(1)} custom-call(bf16[2,256,256]{2,1,0:T(8,128)(2,1)S(1)} %get-tuple-element.34.x_ref), custom_call_target="tpu_custom_call" | custom-call | tf_op jit(solution)/shard_map/turned_taps/pallas_call | solution.py:185
  14.7 0.0 collective-permute-done.5.refs_2_
  14.7 0.0 copy-start
  14.7 1.0 %collective-permute-start.10 = (bf16[256,256]{1,0:T(8,128)(2,1)S(1)}, bf16[256,256]{1,0:T(8,128)(2,1)S(1)}, u32[]{:S(2)}, u32[]{:S(2)}) collective-permute-start(bf16[256,256]{1,0:T(8,128)(2,1)S(1)} %stage.11), channel_id=1, source_target_pairs={{4,0},{5,1},{6,2},{7,3},{20,16},{21,17},{22,18},{23,19}} | collective-permute-start | bytes 393224 | tf_op jit(solution)/shard_map/ppermute | solution.py:333
  15.7 0.7 %turned_taps.5.refs_1_ = bf16[2,9,256,256]{3,2,1,0:T(8,128)(2,1)S(1)} custom-call(bf16[2,256,256]{2,1,0:T(8,128)(2,1)S(1)} %collective-permute-done.6.x_ref), custom_call_target="tpu_custom_call" | custom-call | tf_op jit(solution)/shard_map/turned_taps/pallas_call | solution.py:185
  16.4 0.1 multiply_convert_fusion.1.refs_2_
  16.5 1.3 %collective-permute-start.7 = (bf16[256,256]{1,0:T(8,128)(2,1)S(1)}, bf16[256,256]{1,0:T(8,128)(2,1)S(1)}, u32[]{:S(2)}, u32[]{:S(2)}) collective-permute-start(bf16[256,256]{1,0:T(8,128)(2,1)S(1)} %multiply_convert_fusion.1.refs_2_), channel_id=1, source_target_pairs={{0,2},{1,3},{2,0},{3,1},{4,6},{5,7},{6,4},{7,5},{8,10},{9,11},{10,... | collective-permute-start | bytes 393224 | tf_op jit(solution)/shard_map/ppermute | solution.py:324
  17.8 1.4 %collective-permute-start.8 = (bf16[256,256]{1,0:T(8,128)(2,1)S(1)}, bf16[256,256]{1,0:T(8,128)(2,1)S(1)}, u32[]{:S(2)}, u32[]{:S(2)}) collective-permute-start(bf16[256,256]{1,0:T(8,128)(2,1)S(1)} %multiply_convert_fusion.1.refs_2_), channel_id=1, source_target_pairs={{0,1},{1,0},{2,3},{3,2},{4,5},{5,4},{6,7},{7,6},{8,9},{9,8},{10,11... | collective-permute-start | bytes 393224 | tf_op jit(solution)/shard_map/ppermute | solution.py:324
  19.2 0.1 multiply_convert_fusion.refs_2_
  19.3 0.1 collective-permute-start.11
  19.3 0.3 collective-permute-start.14
  19.7 11.9 %collective-permute-done.7.refs_4_ = bf16[256,256]{1,0:T(8,128)(2,1)S(1)} collective-permute-done((bf16[256,256]{1,0:T(8,128)(2,1)S(1)}, bf16[256,256]{1,0:T(8,128)(2,1)S(1)}, u32[]{:S(2)}, u32[]{:S(2)}) %collective-permute-start.7) | collective-permute-done | bytes 131104 | tf_op jit(solution)/shard_map/ppermute | solution.py:324
  31.6 1.0 %contract.3 = (f32[9,256,256]{2,1,0:T(8,128)S(1)}, f32[9,64,256]{2,1,0:T(8,128)S(1)}) custom-call(f32[9,256,256]{2,1,0:T(8,128)S(1)} %bitcast.9, f32[9,64,256]{2,1,0:T(8,128)S(1)} %get-tuple-element.42.mom_ref, bf16[2,9,256,256]{3,2,1,0:T(8,128)(2,1)S(1)} %turned_taps.4.refs_0_, bf16[2,9,256,256]{3,2,1,0:T(8,128)(2,1)S(1)} %turned_taps.5.refs_1_, ...), custom_call_target="tpu_custom_call" | custom-call | flops 300000000 | tf_op jit(solution)/shard_map/contract/pallas_call | solution.py:296
  32.6 1.9 %collective-permute-start.12 = (bf16[2,256,256]{2,1,0:T(8,128)(2,1)S(1)}, bf16[2,256,256]{2,1,0:T(8,128)(2,1)S(1)}, u32[]{:S(2)}, u32[]{:S(2)}) collective-permute-start(bf16[2,256,256]{2,1,0:T(8,128)(2,1)S(1)} %bitcast.12), channel_id=1, source_target_pairs={{0,1},{1,0},{2,3},{3,2},{4,5},{5,4},{6,7},{7,6},{8,9},{9,8},{10,11... | collective-permute-start | bytes 786440 | tf_op jit(solution)/shard_map/ppermute | solution.py:324
  34.5 0.2 incoming.1
  34.7 0.1 collective-permute-start.16
  34.8 0.5 %collective-permute-start.17 = (bf16[3,128,256]{2,1,0:T(8,128)(2,1)S(1)}, bf16[3,128,256]{2,1,0:T(8,128)(2,1)S(1)}, u32[]{:S(2)}, u32[]{:S(2)}) collective-permute-start(bf16[3,128,256]{2,1,0:T(8,128)(2,1)S(1)} %get-tuple-element.55.refs_10_), channel_id=1, source_target_pairs={{0,1},{1,0},{2,3},{3,2},{4,5},{5,4},{6,7},{7,6},{8,9},{9,8},{10,11... | collective-permute-start | bytes 589832 | tf_op jit(solution)/shard_map/ppermute | solution.py:324
  35.3 0.1 collective-permute-start.18
  35.4 1.0 %contract.4 = (f32[9,256,256]{2,1,0:T(8,128)S(1)}, f32[9,64,256]{2,1,0:T(8,128)S(1)}) custom-call(f32[9,256,256]{2,1,0:T(8,128)S(1)} %get-tuple-element.43.base_ref, f32[9,64,256]{2,1,0:T(8,128)S(1)} %get-tuple-element.45.mom_ref, bf16[2,9,256,256]{3,2,1,0:T(8,128)(2,1)S(1)} %turned_taps.4.refs_0_, bf16[2,9,256,256]{3,2,1,0:T(8,128)(2,1)S(1)} %turned_taps.5.refs_1_, ...), custom_call_target="tpu_custom_call" | custom-call | flops 300000000 | tf_op jit(solution)/shard_map/contract/pallas_call | solution.py:296
  36.4 0.5 %collective-permute-start.15 = (bf16[256,256]{1,0:T(8,128)(2,1)S(1)}, bf16[256,256]{1,0:T(8,128)(2,1)S(1)}, u32[]{:S(2)}, u32[]{:S(2)}) collective-permute-start(bf16[256,256]{1,0:T(8,128)(2,1)S(1)} %collective-permute-done.14.refs_6_), channel_id=1, source_target_pairs={{0,1},{1,0},{2,3},{3,2},{4,5},{5,4},{6,7},{7,6},{8,9},{9,8},{10,11... | collective-permute-start | bytes 393224 | tf_op jit(solution)/shard_map/ppermute | solution.py:324
  36.9 0.0 collective-permute-done.12.x_ref
  36.9 0.1 collective-permute-start.13
  37.0 0.7 %turned_taps.6.refs_0_.refs_2_ = bf16[2,9,256,256]{3,2,1,0:T(8,128)(2,1)S(1)} custom-call(bf16[2,256,256]{2,1,0:T(8,128)(2,1)S(1)} %bitcast.13), custom_call_target="tpu_custom_call" | custom-call | tf_op jit(solution)/shard_map/turned_taps/pallas_call | solution.py:185
  37.7 0.7 %turned_taps.7.refs_1_.refs_3_ = bf16[2,9,256,256]{3,2,1,0:T(8,128)(2,1)S(1)} custom-call(bf16[2,256,256]{2,1,0:T(8,128)(2,1)S(1)} %collective-permute-done.12.x_ref), custom_call_target="tpu_custom_call" | custom-call | tf_op jit(solution)/shard_map/turned_taps/pallas_call | solution.py:185
  38.3 0.0 collective-permute-done.15.refs_7_
  38.4 0.0 collective-permute-done.16.refs_9_
  38.4 0.0 collective-permute-done.17.refs_11_
  38.4 2.8 %contract.5 = (f32[9,256,256]{2,1,0:T(8,128)}, f32[9,64,256]{2,1,0:T(8,128)}) custom-call(f32[9,256,256]{2,1,0:T(8,128)S(1)} %get-tuple-element.47.base_ref, f32[9,64,256]{2,1,0:T(8,128)S(1)} %get-tuple-element.48.mom_ref, bf16[2,9,256,256]{3,2,1,0:T(8,128)(2,1)S(1)} %turned_taps.6.refs_0_.refs_2_, bf16[2,9,256,256]{3,2,1,0:T(8,128)(2,1)S(1)} %turned_taps.7.refs_1_.refs_3_, ...), custom_call_target="tpu_custom_call" | custom-call | tf_op jit(solution)/shard_map/contract/pallas_call | solution.py:296
  (16 shorter events, 0.1 us)
Async XLA Ops:
  0.6 6.4 %collective-permute-start.1 = (bf16[9,256,256]{2,1,0:T(8,128)(2,1)}, bf16[9,256,256]{2,1,0:T(8,128)(2,1)S(1)}, u32[]{:S(2)}, u32[]{:S(2)}) collective-permute-start(bf16[9,256,256]{2,1,0:T(8,128)(2,1)} %bitcast.10), channel_id=1, source_target_pairs={{0,1},{1,0},{2,3},{3,2},{4,5},{5,4},{6,7},{7,6},{8,9},{9,8},{10,11... | collective-permute-start | bytes 3538952 | tf_op jit(solution)/shard_map/ppermute | solution.py:324
  4.9 5.1 %collective-permute-start = (bf16[256,256]{1,0:T(8,128)(2,1)S(1)}, bf16[256,256]{1,0:T(8,128)(2,1)S(1)}, u32[]{:S(2)}, u32[]{:S(2)}) collective-permute-start(bf16[256,256]{1,0:T(8,128)(2,1)S(1)} %stage.6), channel_id=1, source_target_pairs={{12,8},{13,9},{14,10},{15,11},{28,24},{29,25},{30,26},{31,27}} | collective-permute-start | bytes 393224 | tf_op jit(solution)/shard_map/ppermute | solution.py:333
  6.5 1.3 %copy-start.1 = (bf16[1,1,9,256,256]{4,3,2,1,0:T(8,128)(2,1)S(1)}, bf16[1,1,9,256,256]{4,3,2,1,0:T(8,128)(2,1)}, u32[]{:S(2)}) copy-start(bf16[1,1,9,256,256]{4,3,2,1,0:T(8,128)(2,1)} %param.9) | copy-start | bytes 3538948
  6.5 1.4 %copy-start.2 = (f32[1,9,64,256]{3,2,1,0:T(8,128)S(1)}, f32[1,9,64,256]{3,2,1,0:T(8,128)}, u32[]{:S(2)}) copy-start(f32[1,9,64,256]{3,2,1,0:T(8,128)} %param.11) | copy-start | bytes 1769476
  8.4 24.1 %collective-permute-start.9 = (bf16[1664,256]{1,0:T(8,128)(2,1)S(1)}, bf16[1664,256]{1,0:T(8,128)(2,1)S(1)}, u32[]{:S(2)}, u32[]{:S(2)}) collective-permute-start(bf16[1664,256]{1,0:T(8,128)(2,1)S(1)} %get-tuple-element.36.ours_ref), channel_id=1, source_target_pairs={{0,2},{1,3},{2,0},{3,1},{4,6},{5,7},{6,4},{7,5},{8,10},{9,11},{10,... | collective-permute-start | bytes 2555912 | tf_op jit(solution)/shard_map/ppermute | solution.py:324
  8.8 3.9 %collective-permute-start.3 = (bf16[256,256]{1,0:T(8,128)(2,1)S(1)}, bf16[256,256]{1,0:T(8,128)(2,1)S(1)}, u32[]{:S(2)}, u32[]{:S(2)}) collective-permute-start(bf16[256,256]{1,0:T(8,128)(2,1)S(1)} %stage.7), channel_id=1, source_target_pairs={{12,8},{13,9},{14,10},{15,11},{28,24},{29,25},{30,26},{31,27}} | collective-permute-start | bytes 393224 | tf_op jit(solution)/shard_map/ppermute | solution.py:333
  10.1 3.2 %collective-permute-start.2 = (bf16[256,256]{1,0:T(8,128)(2,1)S(1)}, bf16[256,256]{1,0:T(8,128)(2,1)S(1)}, u32[]{:S(2)}, u32[]{:S(2)}) collective-permute-start(bf16[256,256]{1,0:T(8,128)(2,1)S(1)} %stage.8), channel_id=1, source_target_pairs={{8,4},{9,5},{10,6},{11,7},{24,20},{25,21},{26,22},{27,23}} | collective-permute-start | bytes 393224 | tf_op jit(solution)/shard_map/ppermute | solution.py:333
  10.8 5.0 %collective-permute-start.6 = (bf16[2,256,256]{2,1,0:T(8,128)(2,1)S(1)}, bf16[2,256,256]{2,1,0:T(8,128)(2,1)S(1)}, u32[]{:S(2)}, u32[]{:S(2)}) collective-permute-start(bf16[2,256,256]{2,1,0:T(8,128)(2,1)S(1)} %get-tuple-element.34.x_ref), channel_id=1, source_target_pairs={{0,1},{1,0},{2,3},{3,2},{4,5},{5,4},{6,7},{7,6},{8,9},{9,8},{10,11... | collective-permute-start | bytes 786440 | tf_op jit(solution)/shard_map/ppermute | solution.py:324
  12.6 2.1 %collective-permute-start.5 = (bf16[256,256]{1,0:T(8,128)(2,1)S(1)}, bf16[256,256]{1,0:T(8,128)(2,1)S(1)}, u32[]{:S(2)}, u32[]{:S(2)}) collective-permute-start(bf16[256,256]{1,0:T(8,128)(2,1)S(1)} %stage.9), channel_id=1, source_target_pairs={{8,4},{9,5},{10,6},{11,7},{24,20},{25,21},{26,22},{27,23}} | collective-permute-start | bytes 393224 | tf_op jit(solution)/shard_map/ppermute | solution.py:333
  13.3 3.1 %collective-permute-start.4 = (bf16[256,256]{1,0:T(8,128)(2,1)S(1)}, bf16[256,256]{1,0:T(8,128)(2,1)S(1)}, u32[]{:S(2)}, u32[]{:S(2)}) collective-permute-start(bf16[256,256]{1,0:T(8,128)(2,1)S(1)} %stage.10), channel_id=1, source_target_pairs={{4,0},{5,1},{6,2},{7,3},{20,16},{21,17},{22,18},{23,19}} | collective-permute-start | bytes 393224 | tf_op jit(solution)/shard_map/ppermute | solution.py:333
  14.7 16.9 %copy-start = (f32[1,9,256,256]{3,2,1,0:T(8,128)S(1)}, f32[1,9,256,256]{3,2,1,0:T(8,128)}, u32[]{:S(2)}) copy-start(f32[1,9,256,256]{3,2,1,0:T(8,128)} %param.10) | copy-start | bytes 7077892
  14.7 4.5 %collective-permute-start.10 = (bf16[256,256]{1,0:T(8,128)(2,1)S(1)}, bf16[256,256]{1,0:T(8,128)(2,1)S(1)}, u32[]{:S(2)}, u32[]{:S(2)}) collective-permute-start(bf16[256,256]{1,0:T(8,128)(2,1)S(1)} %stage.11), channel_id=1, source_target_pairs={{4,0},{5,1},{6,2},{7,3},{20,16},{21,17},{22,18},{23,19}} | collective-permute-start | bytes 393224 | tf_op jit(solution)/shard_map/ppermute | solution.py:333
  16.5 15.1 %collective-permute-start.7 = (bf16[256,256]{1,0:T(8,128)(2,1)S(1)}, bf16[256,256]{1,0:T(8,128)(2,1)S(1)}, u32[]{:S(2)}, u32[]{:S(2)}) collective-permute-start(bf16[256,256]{1,0:T(8,128)(2,1)S(1)} %multiply_convert_fusion.1.refs_2_), channel_id=1, source_target_pairs={{0,2},{1,3},{2,0},{3,1},{4,6},{5,7},{6,4},{7,5},{8,10},{9,11},{10,... | collective-permute-start | bytes 393224 | tf_op jit(solution)/shard_map/ppermute | solution.py:324
  17.8 13.8 %collective-permute-start.8 = (bf16[256,256]{1,0:T(8,128)(2,1)S(1)}, bf16[256,256]{1,0:T(8,128)(2,1)S(1)}, u32[]{:S(2)}, u32[]{:S(2)}) collective-permute-start(bf16[256,256]{1,0:T(8,128)(2,1)S(1)} %multiply_convert_fusion.1.refs_2_), channel_id=1, source_target_pairs={{0,1},{1,0},{2,3},{3,2},{4,5},{5,4},{6,7},{7,6},{8,9},{9,8},{10,11... | collective-permute-start | bytes 393224 | tf_op jit(solution)/shard_map/ppermute | solution.py:324
  19.3 16.1 %collective-permute-start.11 = (bf16[256,256]{1,0:T(8,128)(2,1)S(1)}, bf16[256,256]{1,0:T(8,128)(2,1)S(1)}, u32[]{:S(2)}, u32[]{:S(2)}) collective-permute-start(bf16[256,256]{1,0:T(8,128)(2,1)S(1)} %multiply_convert_fusion.refs_2_), channel_id=1, source_target_pairs={{0,1},{1,0},{2,3},{3,2},{4,5},{5,4},{6,7},{7,6},{8,9},{9,8},{10,11... | collective-permute-start | bytes 393224 | tf_op jit(solution)/shard_map/ppermute | solution.py:324
  19.3 17.0 %collective-permute-start.14 = (bf16[256,256]{1,0:T(8,128)(2,1)S(1)}, bf16[256,256]{1,0:T(8,128)(2,1)S(1)}, u32[]{:S(2)}, u32[]{:S(2)}) collective-permute-start(bf16[256,256]{1,0:T(8,128)(2,1)S(1)} %multiply_convert_fusion.refs_2_), channel_id=1, source_target_pairs={{0,2},{1,3},{2,0},{3,1},{4,6},{5,7},{6,4},{7,5},{8,10},{9,11},{10,... | collective-permute-start | bytes 393224 | tf_op jit(solution)/shard_map/ppermute | solution.py:324
  32.6 4.3 %collective-permute-start.12 = (bf16[2,256,256]{2,1,0:T(8,128)(2,1)S(1)}, bf16[2,256,256]{2,1,0:T(8,128)(2,1)S(1)}, u32[]{:S(2)}, u32[]{:S(2)}) collective-permute-start(bf16[2,256,256]{2,1,0:T(8,128)(2,1)S(1)} %bitcast.12), channel_id=1, source_target_pairs={{0,1},{1,0},{2,3},{3,2},{4,5},{5,4},{6,7},{7,6},{8,9},{9,8},{10,11... | collective-permute-start | bytes 786440 | tf_op jit(solution)/shard_map/ppermute | solution.py:324
  34.7 3.6 %collective-permute-start.16 = (bf16[3,128,256]{2,1,0:T(8,128)(2,1)S(1)}, bf16[3,128,256]{2,1,0:T(8,128)(2,1)S(1)}, u32[]{:S(2)}, u32[]{:S(2)}) collective-permute-start(bf16[3,128,256]{2,1,0:T(8,128)(2,1)S(1)} %get-tuple-element.56.refs_8_), channel_id=1, source_target_pairs={{0,1},{1,0},{2,3},{3,2},{4,5},{5,4},{6,7},{7,6},{8,9},{9,8},{10,11... | collective-permute-start | bytes 589832 | tf_op jit(solution)/shard_map/ppermute | solution.py:324
  34.8 3.5 %collective-permute-start.17 = (bf16[3,128,256]{2,1,0:T(8,128)(2,1)S(1)}, bf16[3,128,256]{2,1,0:T(8,128)(2,1)S(1)}, u32[]{:S(2)}, u32[]{:S(2)}) collective-permute-start(bf16[3,128,256]{2,1,0:T(8,128)(2,1)S(1)} %get-tuple-element.55.refs_10_), channel_id=1, source_target_pairs={{0,1},{1,0},{2,3},{3,2},{4,5},{5,4},{6,7},{7,6},{8,9},{9,8},{10,11... | collective-permute-start | bytes 589832 | tf_op jit(solution)/shard_map/ppermute | solution.py:324
  35.3 3.1 %collective-permute-start.18 = (bf16[3,128,256]{2,1,0:T(8,128)(2,1)S(1)}, bf16[3,128,256]{2,1,0:T(8,128)(2,1)S(1)}, u32[]{:S(2)}, u32[]{:S(2)}) collective-permute-start(bf16[3,128,256]{2,1,0:T(8,128)(2,1)S(1)} %get-tuple-element.54.refs_12_), channel_id=1, source_target_pairs={{0,1},{1,0},{2,3},{3,2},{4,5},{5,4},{6,7},{7,6},{8,9},{9,8},{10,11... | collective-permute-start | bytes 589832 | tf_op jit(solution)/shard_map/ppermute | solution.py:324
  36.4 1.9 %collective-permute-start.15 = (bf16[256,256]{1,0:T(8,128)(2,1)S(1)}, bf16[256,256]{1,0:T(8,128)(2,1)S(1)}, u32[]{:S(2)}, u32[]{:S(2)}) collective-permute-start(bf16[256,256]{1,0:T(8,128)(2,1)S(1)} %collective-permute-done.14.refs_6_), channel_id=1, source_target_pairs={{0,1},{1,0},{2,3},{3,2},{4,5},{5,4},{6,7},{7,6},{8,9},{9,8},{10,11... | collective-permute-start | bytes 393224 | tf_op jit(solution)/shard_map/ppermute | solution.py:324
  36.9 1.5 %collective-permute-start.13 = (bf16[256,256]{1,0:T(8,128)(2,1)S(1)}, bf16[256,256]{1,0:T(8,128)(2,1)S(1)}, u32[]{:S(2)}, u32[]{:S(2)}) collective-permute-start(bf16[256,256]{1,0:T(8,128)(2,1)S(1)} %collective-permute-done.7.refs_4_), channel_id=1, source_target_pairs={{0,1},{1,0},{2,3},{3,2},{4,5},{5,4},{6,7},{7,6},{8,9},{9,8},{10,11... | collective-permute-start | bytes 393224 | tf_op jit(solution)/shard_map/ppermute | solution.py:324

commit v5 on v4

--- a/solution.py
+++ b/solution.py
@@ -248,7 +248,7 @@
     )(ours, theirs, rest)
 
 
-def contract(base, momentum_base, blocks, gains, final, pieces=(), last=0, cost=0):
+def contract(base, momentum_base, blocks, gains, final, pieces=(), last=0, cost=0, grid=(0, 0)):
     taps, width, _ = base.shape
     share = momentum_base.shape[1]
     count = len(blocks)
@@ -258,7 +258,10 @@
         taken, refs = refs[: len(pieces)], refs[len(pieces) :]
         out_ref, mom_out_ref, total = refs[:3]
         if final:
-            out_now, mom_now, sems = refs[3:]
+            out_now, mom_now, sems, shifted = refs[3:]
+            for n, (one, m, _) in enumerate(blocks):
+                if one.ndim == 3:
+                    spread(shifted, (n,), turned[n][m].astype(F32), *grid)
         else:
             out_now, mom_now = out_ref, mom_out_ref
         here = lax.axis_index("replica")
@@ -267,7 +270,12 @@
         for k in range(taps):
             acc = None
             for n in range(count):
-                term = lax.dot_general(turned[n][blocks[n][1], k], local[n][...], NN, preferred_element_type=F32)
+                if blocks[n][0].ndim == 3:
+                    first = k // 3 * grid[1]
+                    left = shifted[n, k % 3, first : first + grid[0] * grid[1], :].T
+                else:
+                    left = turned[n][blocks[n][1], k]
+                term = lax.dot_general(left, local[n][...], NN, preferred_element_type=F32)
                 acc = term if acc is None else acc + term
             total[k % 2] = acc
             out_now[k] = base_ref[k] + gains[0] * acc
@@ -292,6 +300,7 @@
             pltpu.VMEM(base.shape, F32),
             pltpu.VMEM(momentum_base.shape, F32),
             pltpu.SemaphoreType.DMA((2, taps)),
+            pltpu.VMEM((count, 3, (grid[0] + 2) * grid[1], width), BF16),
         ]
     return pl.pallas_call(
         kernel,
@@ -364,9 +373,9 @@
 
 
     x_there = theirs[: micro * length].reshape(x.shape)
-    x_all = spread_out(x_sent, low) + [(at | last, one) for at, one in spread_out(x_there, low)]
-    turned = {at: turned_taps(one, rows, cols) for at, one in x_all}
-
+    turned = {at: turned_taps(one, rows, cols) for at, one in spread_out(x_sent, low)}
+    x_far = spread_out(x_there, low)
+    turned |= {at | last: one if replicas <= 4 and at == 0 else turned_taps(one, rows, cols) for at, one in x_far}
     gain = 0.5 * scale / replicas
     gains = (-1.33 * gain, gain)
     arrived[0][-1] = after(arrived[0][-1], *[one for at, one in turned.items() if at < last])
@@ -392,8 +401,9 @@
     for k in range(0, taps, 3):
         pieces += [(at, k, one) for at, one in spread_out(pair[k : k + 3], low)]
     for at in range(0, len(blocks), 4):
+        end = at + 4 >= len(blocks)
         base, momentum_base = contract(
-            base, momentum_base, blocks[at : at + 4], gains, at + 4 >= len(blocks), pieces, last
+            base, momentum_base, blocks[at : at + 4], gains, end, pieces, last, grid=(rows, cols)
         )
         pieces = ()
     return (base[None], momentum_base[None])

time: 41.6 us -> 41.3 us (level)
  waiting for transfers between devices: 13.2 us -> 13.9 us
  Pallas kernels: 12.3 us -> 11.7 us
    ppermute x13, waiting for transfers between devices: 12 us -> 12.7 us  [swap(): lax.ppermute(value, 'replica', [(i, i ^ bit) for i in range(replicas)])]
    pallas_call x4 -> x3, Pallas kernels: 2.69 us -> 2.02 us  [turned_taps(): pl.pallas_call(kernel, out_shape=jax.ShapeDtypeStruct((blocks, 9, width,...]
  transfers between devices with their start and end apart: 19 -> 19, of which waited for: 2 -> 4; matrix products, arithmetic and copies ran while one was open for 1% -> 1% of each run, Pallas kernels for 23% -> 21%
where the time goes in v5:
time: 41.3 us; the launch traced here: 41.1 us
  waiting for transfers between devices  13.9 us (34%)
  starting transfers between devices  13.5 us (33%)
  Pallas kernels  11.7 us (28%)
  local copies, waits for them, and re-layouts  0.92 us (2%)
  between operations  0.9 us (2%)
    ppermute x13, waiting for transfers between devices, swap(): lax.ppermute(value, 'replica', [(i, i ^ bit) for i in range(replicas)])  12.7 us
    ppermute x13, starting transfers between devices, swap(): lax.ppermute(value, 'replica', [(i, i ^ bit) for i in range(replicas)])  7.86 us
    ppermute x6, starting transfers between devices, hop(): lax.ppermute(value, 'section', [(sections - 1 - step, sections - 2 - step)])  5.65 us
    pallas_call x3, Pallas kernels, contract(): pl.pallas_call(kernel, out_shape=(jax.ShapeDtypeStruct(base.shape, F32),...  4.79 us
    pallas_call x1, Pallas kernels, prepare(): pl.pallas_call(kernel, out_shape=shapes, in_specs=[HBM] * 4, out_specs=[V...  3.02 us
    pallas_call x3, Pallas kernels, turned_taps(): pl.pallas_call(kernel, out_shape=jax.ShapeDtypeStruct((blocks, 9, width,...  2.02 us
    ppermute x6, waiting for transfers between devices, hop(): lax.ppermute(value, 'section', [(sections - 1 - step, sections - 2 - step)])  1.23 us
    pallas_call x6, Pallas kernels, stage(): pl.pallas_call(kernel, out_shape=jax.ShapeDtypeStruct((length, width), BF...  1.11 us
  transfers between devices with their start and end apart: 19, of which 4 were waited for; matrix products, arithmetic and copies ran while one was open for 1% of the time, Pallas kernels for 21%

profile of v5, /device:TPU:27, one launch (start us, length us, event | category | flops | bytes accessed | tf_op | source)
XLA Modules:
  0.0 41.1 jit_solution(16595961152914981366)
XLA Ops:
  0.6 0.7 %collective-permute-start.1 = (bf16[9,256,256]{2,1,0:T(8,128)(2,1)}, bf16[9,256,256]{2,1,0:T(8,128)(2,1)S(1)}, u32[]{:S(2)}, u32[]{:S(2)}) collective-permute-start(bf16[9,256,256]{2,1,0:T(8,128)(2,1)} %bitcast.13), channel_id=1, source_target_pairs={{0,1},{1,0},{2,3},{3,2},{4,5},{5,4},{6,7},{7,6},{8,9},{9,8},{10,11... | collective-permute-start | bytes 3538952 | tf_op jit(solution)/shard_map/ppermute | solution.py:333
  1.4 3.0 %prepare.1 = (bf16[9,256,256]{2,1,0:T(8,128)(2,1)S(1)}, bf16[2,256,256]{2,1,0:T(8,128)(2,1)S(1)}, f32[256,256]{1,0:T(8,128)S(1)}, f32[256,256]{1,0:T(8,128)S(1)}...) custom-call(s32[1,2]{1,0:T(1,128)} %crop_ref.1, bf16[2,256,256]{2,1,0:T(8,128)(2,1)} %bitcast.16, ...), custom_call_target="tpu_custom_call" | custom-call | tf_op jit(solution)/shard_map/prepare/pallas_call | solution.py:129
  4.4 0.5 %stage.6 = bf16[256,256]{1,0:T(8,128)(2,1)S(1)} custom-call(bf16[256,256]{1,0:T(8,128)(2,1)S(1)} %get-tuple-element.28.refs_0_, f32[256,256]{1,0:T(8,128)S(1)} %get-tuple-element.29.refs_1_.refs_2_.refs_3_, bf16[9,256,256]{2,1,0:T(8,128)(2,1)S(1)} %get-tuple-element.30.refs_2_.refs_3_.refs_4_), custom_call_target="tpu_custom_call" | custom-call | bytes 1179648 | tf_op jit(solution)/shard_map/stage/pallas_call | solution.py:163
  4.9 1.6 %collective-permute-start = (bf16[256,256]{1,0:T(8,128)(2,1)S(1)}, bf16[256,256]{1,0:T(8,128)(2,1)S(1)}, u32[]{:S(2)}, u32[]{:S(2)}) collective-permute-start(bf16[256,256]{1,0:T(8,128)(2,1)S(1)} %stage.6), channel_id=1, source_target_pairs={{12,8},{13,9},{14,10},{15,11},{28,24},{29,25},{30,26},{31,27}} | collective-permute-start | bytes 393224 | tf_op jit(solution)/shard_map/ppermute | solution.py:342
  6.5 0.0 copy-start.1
  6.5 0.0 copy-start.2
  6.5 0.5 %stage.7 = bf16[256,256]{1,0:T(8,128)(2,1)S(1)} custom-call(bf16[256,256]{1,0:T(8,128)(2,1)S(1)} %get-tuple-element.31.refs_0_, f32[256,256]{1,0:T(8,128)S(1)} %get-tuple-element.32.refs_1_.refs_2_.refs_3_, bf16[9,256,256]{2,1,0:T(8,128)(2,1)S(1)} %get-tuple-element.30.refs_2_.refs_3_.refs_4_), custom_call_target="tpu_custom_call" | custom-call | flops 1811939328 | bytes 1179648 | tf_op jit(solution)/shard_map/stage/pallas_call | solution.py:163
  7.1 0.0 collective-permute-done.1.far_ref
  7.1 0.7 %copy-done.1 = bf16[1,1,9,256,256]{4,3,2,1,0:T(8,128)(2,1)S(1)} copy-done((bf16[1,1,9,256,256]{4,3,2,1,0:T(8,128)(2,1)S(1)}, bf16[1,1,9,256,256]{4,3,2,1,0:T(8,128)(2,1)}, u32[]{:S(2)}) %copy-start.1) | copy-done | bytes 1179672
  7.8 0.1 copy-done.2
  7.9 0.5 %outgoing.1 = (bf16[1664,256]{1,0:T(8,128)(2,1)S(1)}, f32[9,64,256]{2,1,0:T(8,128)S(1)}) custom-call(bf16[2,256,256]{2,1,0:T(8,128)(2,1)S(1)} %get-tuple-element.34.x_ref, bf16[9,256,256]{2,1,0:T(8,128)(2,1)S(1)} %bitcast.14, bf16[9,256,256]{2,1,0:T(8,128)(2,1)S(1)} %collective-permute-done.1.far_ref, f32[9,64,256]{2,1,0:T(8,128)S(1)} %bitcast.15), custom_call_target="tpu_custom_call" | custom-call | tf_op jit(solution)/shard_map/outgoing/pallas_call | solution.py:215
  8.4 0.3 collective-permute-start.9
  8.8 1.3 %collective-permute-start.3 = (bf16[256,256]{1,0:T(8,128)(2,1)S(1)}, bf16[256,256]{1,0:T(8,128)(2,1)S(1)}, u32[]{:S(2)}, u32[]{:S(2)}) collective-permute-start(bf16[256,256]{1,0:T(8,128)(2,1)S(1)} %stage.7), channel_id=1, source_target_pairs={{12,8},{13,9},{14,10},{15,11},{28,24},{29,25},{30,26},{31,27}} | collective-permute-start | bytes 393224 | tf_op jit(solution)/shard_map/ppermute | solution.py:342
  10.0 0.0 collective-permute-done.refs_1_
  10.1 0.7 %collective-permute-start.2 = (bf16[256,256]{1,0:T(8,128)(2,1)S(1)}, bf16[256,256]{1,0:T(8,128)(2,1)S(1)}, u32[]{:S(2)}, u32[]{:S(2)}) collective-permute-start(bf16[256,256]{1,0:T(8,128)(2,1)S(1)} %stage.8), channel_id=1, source_target_pairs={{8,4},{9,5},{10,6},{11,7},{24,20},{25,21},{26,22},{27,23}} | collective-permute-start | bytes 393224 | tf_op jit(solution)/shard_map/ppermute | solution.py:342
  10.8 0.6 %collective-permute-start.6 = (bf16[2,256,256]{2,1,0:T(8,128)(2,1)S(1)}, bf16[2,256,256]{2,1,0:T(8,128)(2,1)S(1)}, u32[]{:S(2)}, u32[]{:S(2)}) collective-permute-start(bf16[2,256,256]{2,1,0:T(8,128)(2,1)S(1)} %get-tuple-element.34.x_ref), channel_id=1, source_target_pairs={{0,1},{1,0},{2,3},{3,2},{4,5},{5,4},{6,7},{7,6},{8,9},{9,8},{10,11... | collective-permute-start | bytes 786440 | tf_op jit(solution)/shard_map/ppermute | solution.py:333
  11.4 1.2 %collective-permute-done.3.refs_1_ = bf16[256,256]{1,0:T(8,128)(2,1)S(1)} collective-permute-done((bf16[256,256]{1,0:T(8,128)(2,1)S(1)}, bf16[256,256]{1,0:T(8,128)(2,1)S(1)}, u32[]{:S(2)}, u32[]{:S(2)}) %collective-permute-start.3) | collective-permute-done | bytes 131104 | tf_op jit(solution)/shard_map/ppermute | solution.py:342
  12.6 0.7 %collective-permute-start.5 = (bf16[256,256]{1,0:T(8,128)(2,1)S(1)}, bf16[256,256]{1,0:T(8,128)(2,1)S(1)}, u32[]{:S(2)}, u32[]{:S(2)}) collective-permute-start(bf16[256,256]{1,0:T(8,128)(2,1)S(1)} %stage.9), channel_id=1, source_target_pairs={{8,4},{9,5},{10,6},{11,7},{24,20},{25,21},{26,22},{27,23}} | collective-permute-start | bytes 393224 | tf_op jit(solution)/shard_map/ppermute | solution.py:342
  13.3 0.7 %collective-permute-start.4 = (bf16[256,256]{1,0:T(8,128)(2,1)S(1)}, bf16[256,256]{1,0:T(8,128)(2,1)S(1)}, u32[]{:S(2)}, u32[]{:S(2)}) collective-permute-start(bf16[256,256]{1,0:T(8,128)(2,1)S(1)} %stage.10), channel_id=1, source_target_pairs={{4,0},{5,1},{6,2},{7,3},{20,16},{21,17},{22,18},{23,19}} | collective-permute-start | bytes 393224 | tf_op jit(solution)/shard_map/ppermute | solution.py:342
  14.0 0.7 %turned_taps.3.refs_0_ = bf16[2,9,256,256]{3,2,1,0:T(8,128)(2,1)S(1)} custom-call(bf16[2,256,256]{2,1,0:T(8,128)(2,1)S(1)} %get-tuple-element.34.x_ref), custom_call_target="tpu_custom_call" | custom-call | tf_op jit(solution)/shard_map/turned_taps/pallas_call | solution.py:185
  14.7 0.0 copy-start
  14.7 0.8 %collective-permute-start.10 = (bf16[256,256]{1,0:T(8,128)(2,1)S(1)}, bf16[256,256]{1,0:T(8,128)(2,1)S(1)}, u32[]{:S(2)}, u32[]{:S(2)}) collective-permute-start(bf16[256,256]{1,0:T(8,128)(2,1)S(1)} %stage.11), channel_id=1, source_target_pairs={{4,0},{5,1},{6,2},{7,3},{20,16},{21,17},{22,18},{23,19}} | collective-permute-start | bytes 393224 | tf_op jit(solution)/shard_map/ppermute | solution.py:342
  15.5 0.0 collective-permute-done.6.x_ref
  15.5 0.7 %turned_taps.4.refs_1_ = bf16[2,9,256,256]{3,2,1,0:T(8,128)(2,1)S(1)} custom-call(bf16[2,256,256]{2,1,0:T(8,128)(2,1)S(1)} %collective-permute-done.6.x_ref), custom_call_target="tpu_custom_call" | custom-call | tf_op jit(solution)/shard_map/turned_taps/pallas_call | solution.py:185
  16.2 0.0 collective-permute-done.4
  16.2 0.1 multiply_convert_fusion.1.refs_2_
  16.3 1.3 %collective-permute-start.7 = (bf16[256,256]{1,0:T(8,128)(2,1)S(1)}, bf16[256,256]{1,0:T(8,128)(2,1)S(1)}, u32[]{:S(2)}, u32[]{:S(2)}) collective-permute-start(bf16[256,256]{1,0:T(8,128)(2,1)S(1)} %multiply_convert_fusion.1.refs_2_), channel_id=1, source_target_pairs={{0,2},{1,3},{2,0},{3,1},{4,6},{5,7},{6,4},{7,5},{8,10},{9,11},{10,... | collective-permute-start | bytes 393224 | tf_op jit(solution)/shard_map/ppermute | solution.py:333
  17.6 1.4 %collective-permute-start.8 = (bf16[256,256]{1,0:T(8,128)(2,1)S(1)}, bf16[256,256]{1,0:T(8,128)(2,1)S(1)}, u32[]{:S(2)}, u32[]{:S(2)}) collective-permute-start(bf16[256,256]{1,0:T(8,128)(2,1)S(1)} %multiply_convert_fusion.1.refs_2_), channel_id=1, source_target_pairs={{0,1},{1,0},{2,3},{3,2},{4,5},{5,4},{6,7},{7,6},{8,9},{9,8},{10,11... | collective-permute-start | bytes 393224 | tf_op jit(solution)/shard_map/ppermute | solution.py:333
  19.0 0.0 collective-permute-done.10
  19.0 0.1 multiply_convert_fusion.refs_2_
  19.1 0.1 collective-permute-start.11
  19.2 0.3 collective-permute-start.14
  19.5 12.1 %collective-permute-done.7.refs_4_ = bf16[256,256]{1,0:T(8,128)(2,1)S(1)} collective-permute-done((bf16[256,256]{1,0:T(8,128)(2,1)S(1)}, bf16[256,256]{1,0:T(8,128)(2,1)S(1)}, u32[]{:S(2)}, u32[]{:S(2)}) %collective-permute-start.7) | collective-permute-done | bytes 131104 | tf_op jit(solution)/shard_map/ppermute | solution.py:333
  31.6 1.0 %contract.3 = (f32[9,256,256]{2,1,0:T(8,128)S(1)}, f32[9,64,256]{2,1,0:T(8,128)S(1)}) custom-call(f32[9,256,256]{2,1,0:T(8,128)S(1)} %bitcast.9, f32[9,64,256]{2,1,0:T(8,128)S(1)} %get-tuple-element.42.mom_ref, bf16[2,9,256,256]{3,2,1,0:T(8,128)(2,1)S(1)} %turned_taps.3.refs_0_, bf16[2,9,256,256]{3,2,1,0:T(8,128)(2,1)S(1)} %turned_taps.4.refs_1_, ...), custom_call_target="tpu_custom_call" | custom-call | flops 300000000 | tf_op jit(solution)/shard_map/contract/pallas_call | solution.py:305
  32.6 0.0 collective-permute-done.9.theirs_ref
  32.6 1.9 %collective-permute-start.12 = (bf16[2,256,256]{2,1,0:T(8,128)(2,1)S(1)}, bf16[2,256,256]{2,1,0:T(8,128)(2,1)S(1)}, u32[]{:S(2)}, u32[]{:S(2)}) collective-permute-start(bf16[2,256,256]{2,1,0:T(8,128)(2,1)S(1)} %bitcast.10), channel_id=1, source_target_pairs={{0,1},{1,0},{2,3},{3,2},{4,5},{5,4},{6,7},{7,6},{8,9},{9,8},{10,11... | collective-permute-start | bytes 786440 | tf_op jit(solution)/shard_map/ppermute | solution.py:333
  34.5 0.2 incoming.1
  34.7 0.1 collective-permute-start.16
  34.8 0.5 %collective-permute-start.17 = (bf16[3,128,256]{2,1,0:T(8,128)(2,1)S(1)}, bf16[3,128,256]{2,1,0:T(8,128)(2,1)S(1)}, u32[]{:S(2)}, u32[]{:S(2)}) collective-permute-start(bf16[3,128,256]{2,1,0:T(8,128)(2,1)S(1)} %get-tuple-element.55.refs_10_), channel_id=1, source_target_pairs={{0,1},{1,0},{2,3},{3,2},{4,5},{5,4},{6,7},{7,6},{8,9},{9,8},{10,11... | collective-permute-start | bytes 589832 | tf_op jit(solution)/shard_map/ppermute | solution.py:333
  35.3 0.1 collective-permute-start.18
  35.4 1.0 %contract.4 = (f32[9,256,256]{2,1,0:T(8,128)S(1)}, f32[9,64,256]{2,1,0:T(8,128)S(1)}) custom-call(f32[9,256,256]{2,1,0:T(8,128)S(1)} %get-tuple-element.43.base_ref, f32[9,64,256]{2,1,0:T(8,128)S(1)} %get-tuple-element.45.mom_ref, bf16[2,9,256,256]{3,2,1,0:T(8,128)(2,1)S(1)} %turned_taps.3.refs_0_, bf16[2,9,256,256]{3,2,1,0:T(8,128)(2,1)S(1)} %turned_taps.4.refs_1_, ...), custom_call_target="tpu_custom_call" | custom-call | flops 300000000 | tf_op jit(solution)/shard_map/contract/pallas_call | solution.py:305
  36.4 0.5 %collective-permute-start.15 = (bf16[256,256]{1,0:T(8,128)(2,1)S(1)}, bf16[256,256]{1,0:T(8,128)(2,1)S(1)}, u32[]{:S(2)}, u32[]{:S(2)}) collective-permute-start(bf16[256,256]{1,0:T(8,128)(2,1)S(1)} %collective-permute-done.14.refs_6_), channel_id=1, source_target_pairs={{0,1},{1,0},{2,3},{3,2},{4,5},{5,4},{6,7},{7,6},{8,9},{9,8},{10,11... | collective-permute-start | bytes 393224 | tf_op jit(solution)/shard_map/ppermute | solution.py:333
  36.9 0.0 collective-permute-done.12.x_ref
  36.9 0.1 collective-permute-start.13
  37.0 0.7 %turned_taps.5.refs_1_.refs_3_ = bf16[2,9,256,256]{3,2,1,0:T(8,128)(2,1)S(1)} custom-call(bf16[2,256,256]{2,1,0:T(8,128)(2,1)S(1)} %collective-permute-done.12.x_ref), custom_call_target="tpu_custom_call" | custom-call | tf_op jit(solution)/shard_map/turned_taps/pallas_call | solution.py:185
  37.7 0.2 collective-permute-done.15.refs_7_
  37.9 0.4 collective-permute-done.13.refs_5_
  38.2 2.8 %contract.5 = (f32[9,256,256]{2,1,0:T(8,128)}, f32[9,64,256]{2,1,0:T(8,128)}) custom-call(f32[9,256,256]{2,1,0:T(8,128)S(1)} %get-tuple-element.47.base_ref, f32[9,64,256]{2,1,0:T(8,128)S(1)} %get-tuple-element.48.mom_ref, bf16[2,256,256]{2,1,0:T(8,128)(2,1)S(1)} %bitcast.11, bf16[2,9,256,256]{3,2,1,0:T(8,128)(2,1)S(1)} %turned_taps.5.refs_1_.refs_3_, ...), custom_call_target="tpu_custom_call" | custom-call | tf_op jit(solution)/shard_map/contract/pallas_call | solution.py:305
  (15 shorter events, 0.1 us)
Async XLA Ops:
  0.6 6.4 %collective-permute-start.1 = (bf16[9,256,256]{2,1,0:T(8,128)(2,1)}, bf16[9,256,256]{2,1,0:T(8,128)(2,1)S(1)}, u32[]{:S(2)}, u32[]{:S(2)}) collective-permute-start(bf16[9,256,256]{2,1,0:T(8,128)(2,1)} %bitcast.13), channel_id=1, source_target_pairs={{0,1},{1,0},{2,3},{3,2},{4,5},{5,4},{6,7},{7,6},{8,9},{9,8},{10,11... | collective-permute-start | bytes 3538952 | tf_op jit(solution)/shard_map/ppermute | solution.py:333
  4.9 5.1 %collective-permute-start = (bf16[256,256]{1,0:T(8,128)(2,1)S(1)}, bf16[256,256]{1,0:T(8,128)(2,1)S(1)}, u32[]{:S(2)}, u32[]{:S(2)}) collective-permute-start(bf16[256,256]{1,0:T(8,128)(2,1)S(1)} %stage.6), channel_id=1, source_target_pairs={{12,8},{13,9},{14,10},{15,11},{28,24},{29,25},{30,26},{31,27}} | collective-permute-start | bytes 393224 | tf_op jit(solution)/shard_map/ppermute | solution.py:342
  6.5 1.3 %copy-start.1 = (bf16[1,1,9,256,256]{4,3,2,1,0:T(8,128)(2,1)S(1)}, bf16[1,1,9,256,256]{4,3,2,1,0:T(8,128)(2,1)}, u32[]{:S(2)}) copy-start(bf16[1,1,9,256,256]{4,3,2,1,0:T(8,128)(2,1)} %param.9) | copy-start | bytes 3538948
  6.5 1.4 %copy-start.2 = (f32[1,9,64,256]{3,2,1,0:T(8,128)S(1)}, f32[1,9,64,256]{3,2,1,0:T(8,128)}, u32[]{:S(2)}) copy-start(f32[1,9,64,256]{3,2,1,0:T(8,128)} %param.11) | copy-start | bytes 1769476
  8.4 24.1 %collective-permute-start.9 = (bf16[1664,256]{1,0:T(8,128)(2,1)S(1)}, bf16[1664,256]{1,0:T(8,128)(2,1)S(1)}, u32[]{:S(2)}, u32[]{:S(2)}) collective-permute-start(bf16[1664,256]{1,0:T(8,128)(2,1)S(1)} %get-tuple-element.36.ours_ref), channel_id=1, source_target_pairs={{0,2},{1,3},{2,0},{3,1},{4,6},{5,7},{6,4},{7,5},{8,10},{9,11},{10,... | collective-permute-start | bytes 2555912 | tf_op jit(solution)/shard_map/ppermute | solution.py:333
  8.8 3.9 %collective-permute-start.3 = (bf16[256,256]{1,0:T(8,128)(2,1)S(1)}, bf16[256,256]{1,0:T(8,128)(2,1)S(1)}, u32[]{:S(2)}, u32[]{:S(2)}) collective-permute-start(bf16[256,256]{1,0:T(8,128)(2,1)S(1)} %stage.7), channel_id=1, source_target_pairs={{12,8},{13,9},{14,10},{15,11},{28,24},{29,25},{30,26},{31,27}} | collective-permute-start | bytes 393224 | tf_op jit(solution)/shard_map/ppermute | solution.py:342
  10.1 3.2 %collective-permute-start.2 = (bf16[256,256]{1,0:T(8,128)(2,1)S(1)}, bf16[256,256]{1,0:T(8,128)(2,1)S(1)}, u32[]{:S(2)}, u32[]{:S(2)}) collective-permute-start(bf16[256,256]{1,0:T(8,128)(2,1)S(1)} %stage.8), channel_id=1, source_target_pairs={{8,4},{9,5},{10,6},{11,7},{24,20},{25,21},{26,22},{27,23}} | collective-permute-start | bytes 393224 | tf_op jit(solution)/shard_map/ppermute | solution.py:342
  10.8 4.8 %collective-permute-start.6 = (bf16[2,256,256]{2,1,0:T(8,128)(2,1)S(1)}, bf16[2,256,256]{2,1,0:T(8,128)(2,1)S(1)}, u32[]{:S(2)}, u32[]{:S(2)}) collective-permute-start(bf16[2,256,256]{2,1,0:T(8,128)(2,1)S(1)} %get-tuple-element.34.x_ref), channel_id=1, source_target_pairs={{0,1},{1,0},{2,3},{3,2},{4,5},{5,4},{6,7},{7,6},{8,9},{9,8},{10,11... | collective-permute-start | bytes 786440 | tf_op jit(solution)/shard_map/ppermute | solution.py:333
  12.6 2.1 %collective-permute-start.5 = (bf16[256,256]{1,0:T(8,128)(2,1)S(1)}, bf16[256,256]{1,0:T(8,128)(2,1)S(1)}, u32[]{:S(2)}, u32[]{:S(2)}) collective-permute-start(bf16[256,256]{1,0:T(8,128)(2,1)S(1)} %stage.9), channel_id=1, source_target_pairs={{8,4},{9,5},{10,6},{11,7},{24,20},{25,21},{26,22},{27,23}} | collective-permute-start | bytes 393224 | tf_op jit(solution)/shard_map/ppermute | solution.py:342
  13.3 2.9 %collective-permute-start.4 = (bf16[256,256]{1,0:T(8,128)(2,1)S(1)}, bf16[256,256]{1,0:T(8,128)(2,1)S(1)}, u32[]{:S(2)}, u32[]{:S(2)}) collective-permute-start(bf16[256,256]{1,0:T(8,128)(2,1)S(1)} %stage.10), channel_id=1, source_target_pairs={{4,0},{5,1},{6,2},{7,3},{20,16},{21,17},{22,18},{23,19}} | collective-permute-start | bytes 393224 | tf_op jit(solution)/shard_map/ppermute | solution.py:342
  14.7 16.9 %copy-start = (f32[1,9,256,256]{3,2,1,0:T(8,128)S(1)}, f32[1,9,256,256]{3,2,1,0:T(8,128)}, u32[]{:S(2)}) copy-start(f32[1,9,256,256]{3,2,1,0:T(8,128)} %param.10) | copy-start | bytes 7077892
  14.7 4.3 %collective-permute-start.10 = (bf16[256,256]{1,0:T(8,128)(2,1)S(1)}, bf16[256,256]{1,0:T(8,128)(2,1)S(1)}, u32[]{:S(2)}, u32[]{:S(2)}) collective-permute-start(bf16[256,256]{1,0:T(8,128)(2,1)S(1)} %stage.11), channel_id=1, source_target_pairs={{4,0},{5,1},{6,2},{7,3},{20,16},{21,17},{22,18},{23,19}} | collective-permute-start | bytes 393224 | tf_op jit(solution)/shard_map/ppermute | solution.py:342
  16.3 15.3 %collective-permute-start.7 = (bf16[256,256]{1,0:T(8,128)(2,1)S(1)}, bf16[256,256]{1,0:T(8,128)(2,1)S(1)}, u32[]{:S(2)}, u32[]{:S(2)}) collective-permute-start(bf16[256,256]{1,0:T(8,128)(2,1)S(1)} %multiply_convert_fusion.1.refs_2_), channel_id=1, source_target_pairs={{0,2},{1,3},{2,0},{3,1},{4,6},{5,7},{6,4},{7,5},{8,10},{9,11},{10,... | collective-permute-start | bytes 393224 | tf_op jit(solution)/shard_map/ppermute | solution.py:333
  17.6 14.0 %collective-permute-start.8 = (bf16[256,256]{1,0:T(8,128)(2,1)S(1)}, bf16[256,256]{1,0:T(8,128)(2,1)S(1)}, u32[]{:S(2)}, u32[]{:S(2)}) collective-permute-start(bf16[256,256]{1,0:T(8,128)(2,1)S(1)} %multiply_convert_fusion.1.refs_2_), channel_id=1, source_target_pairs={{0,1},{1,0},{2,3},{3,2},{4,5},{5,4},{6,7},{7,6},{8,9},{9,8},{10,11... | collective-permute-start | bytes 393224 | tf_op jit(solution)/shard_map/ppermute | solution.py:333
  19.1 16.2 %collective-permute-start.11 = (bf16[256,256]{1,0:T(8,128)(2,1)S(1)}, bf16[256,256]{1,0:T(8,128)(2,1)S(1)}, u32[]{:S(2)}, u32[]{:S(2)}) collective-permute-start(bf16[256,256]{1,0:T(8,128)(2,1)S(1)} %multiply_convert_fusion.refs_2_), channel_id=1, source_target_pairs={{0,1},{1,0},{2,3},{3,2},{4,5},{5,4},{6,7},{7,6},{8,9},{9,8},{10,11... | collective-permute-start | bytes 393224 | tf_op jit(solution)/shard_map/ppermute | solution.py:333
  19.2 17.2 %collective-permute-start.14 = (bf16[256,256]{1,0:T(8,128)(2,1)S(1)}, bf16[256,256]{1,0:T(8,128)(2,1)S(1)}, u32[]{:S(2)}, u32[]{:S(2)}) collective-permute-start(bf16[256,256]{1,0:T(8,128)(2,1)S(1)} %multiply_convert_fusion.refs_2_), channel_id=1, source_target_pairs={{0,2},{1,3},{2,0},{3,1},{4,6},{5,7},{6,4},{7,5},{8,10},{9,11},{10,... | collective-permute-start | bytes 393224 | tf_op jit(solution)/shard_map/ppermute | solution.py:333
  32.6 4.3 %collective-permute-start.12 = (bf16[2,256,256]{2,1,0:T(8,128)(2,1)S(1)}, bf16[2,256,256]{2,1,0:T(8,128)(2,1)S(1)}, u32[]{:S(2)}, u32[]{:S(2)}) collective-permute-start(bf16[2,256,256]{2,1,0:T(8,128)(2,1)S(1)} %bitcast.10), channel_id=1, source_target_pairs={{0,1},{1,0},{2,3},{3,2},{4,5},{5,4},{6,7},{7,6},{8,9},{9,8},{10,11... | collective-permute-start | bytes 786440 | tf_op jit(solution)/shard_map/ppermute | solution.py:333
  34.7 3.5 %collective-permute-start.16 = (bf16[3,128,256]{2,1,0:T(8,128)(2,1)S(1)}, bf16[3,128,256]{2,1,0:T(8,128)(2,1)S(1)}, u32[]{:S(2)}, u32[]{:S(2)}) collective-permute-start(bf16[3,128,256]{2,1,0:T(8,128)(2,1)S(1)} %get-tuple-element.56.refs_8_), channel_id=1, source_target_pairs={{0,1},{1,0},{2,3},{3,2},{4,5},{5,4},{6,7},{7,6},{8,9},{9,8},{10,11... | collective-permute-start | bytes 589832 | tf_op jit(solution)/shard_map/ppermute | solution.py:333
  34.8 3.4 %collective-permute-start.17 = (bf16[3,128,256]{2,1,0:T(8,128)(2,1)S(1)}, bf16[3,128,256]{2,1,0:T(8,128)(2,1)S(1)}, u32[]{:S(2)}, u32[]{:S(2)}) collective-permute-start(bf16[3,128,256]{2,1,0:T(8,128)(2,1)S(1)} %get-tuple-element.55.refs_10_), channel_id=1, source_target_pairs={{0,1},{1,0},{2,3},{3,2},{4,5},{5,4},{6,7},{7,6},{8,9},{9,8},{10,11... | collective-permute-start | bytes 589832 | tf_op jit(solution)/shard_map/ppermute | solution.py:333
  35.3 2.9 %collective-permute-start.18 = (bf16[3,128,256]{2,1,0:T(8,128)(2,1)S(1)}, bf16[3,128,256]{2,1,0:T(8,128)(2,1)S(1)}, u32[]{:S(2)}, u32[]{:S(2)}) collective-permute-start(bf16[3,128,256]{2,1,0:T(8,128)(2,1)S(1)} %get-tuple-element.54.refs_12_), channel_id=1, source_target_pairs={{0,1},{1,0},{2,3},{3,2},{4,5},{5,4},{6,7},{7,6},{8,9},{9,8},{10,11... | collective-permute-start | bytes 589832 | tf_op jit(solution)/shard_map/ppermute | solution.py:333
  36.4 1.5 %collective-permute-start.15 = (bf16[256,256]{1,0:T(8,128)(2,1)S(1)}, bf16[256,256]{1,0:T(8,128)(2,1)S(1)}, u32[]{:S(2)}, u32[]{:S(2)}) collective-permute-start(bf16[256,256]{1,0:T(8,128)(2,1)S(1)} %collective-permute-done.14.refs_6_), channel_id=1, source_target_pairs={{0,1},{1,0},{2,3},{3,2},{4,5},{5,4},{6,7},{7,6},{8,9},{9,8},{10,11... | collective-permute-start | bytes 393224 | tf_op jit(solution)/shard_map/ppermute | solution.py:333
  36.9 1.3 %collective-permute-start.13 = (bf16[256,256]{1,0:T(8,128)(2,1)S(1)}, bf16[256,256]{1,0:T(8,128)(2,1)S(1)}, u32[]{:S(2)}, u32[]{:S(2)}) collective-permute-start(bf16[256,256]{1,0:T(8,128)(2,1)S(1)} %collective-permute-done.7.refs_4_), channel_id=1, source_target_pairs={{0,1},{1,0},{2,3},{3,2},{4,5},{5,4},{6,7},{7,6},{8,9},{9,8},{10,11... | collective-permute-start | bytes 393224 | tf_op jit(solution)/shard_map/ppermute | solution.py:333
